TPU v7x, 128 devices: a whole 4x4x4 slice. The times are simulated.
128 devices in a mesh: hst: 4 (over z), dev: 32 (over y, x, core).
Axes of the slice: x: 4, y: 4, z: 4, core: 2. Of those that a mesh axis runs over, the one named last changes fastest.
Arguments:
- features: bfloat16 [262144, 768], P(('hst', 'dev')), may hold values from -6 to 6
- cache_blocks: bfloat16 [4, 8192, 768], P('hst', 'dev'), may hold values from -6 to 6
- plan: int32 [4, 64], P('hst', 'dev'), may hold values from 0 to 63, as said below
- miss_ids: int32 [128, 4, 32, 16], P(('hst', 'dev')), may hold values from 0 to 2303, as said below
- miss_counts: int32 [128, 4, 32], P(('hst', 'dev')), may hold values from 4 to 16, as said below
- self_ids: int32 [106496], P(('hst', 'dev')), may hold values from 0 to 2047, as said below
- nbr_ids: int32 [106496, 15], P(('hst', 'dev')), may hold values from 0 to 2047, as said below
- hop_counts: int32 [106496], P(('hst', 'dev')), may hold values from 1 to 15, as said below
- seed_counts: int32 [4096], P(('hst', 'dev')), may hold values from 1 to 25, as said below
- w_self1: bfloat16 [768, 1024], replicated, may hold values from -0.21875 to 0.21875
- w_nbr1: bfloat16 [768, 1024], replicated, may hold values from -0.21875 to 0.21875
- w_self2: bfloat16 [1024, 1024], replicated, may hold values from -0.1875 to 0.1875
- w_nbr2: bfloat16 [1024, 1024], replicated, may hold values from -0.1875 to 0.1875
- cotangent: bfloat16 [4096, 1024], P(('hst', 'dev')), may hold values from -1.25 to 1.25
Outputs:
- embedding: bfloat16 [4096, 1024], P(('hst', 'dev'))
- new_cache: bfloat16 [4, 8192, 768], P('hst', 'dev')
- grad_self1: float32 [768, 1024], P(None, ('hst', 'dev'))
- grad_nbr1: float32 [768, 1024], P(None, ('hst', 'dev'))
- grad_self2: float32 [1024, 1024], P(None, ('hst', 'dev'))
- grad_nbr2: float32 [1024, 1024], P(None, ('hst', 'dev'))
Inputs may be any that keep to these rules, and one draw needn't show every extreme that they name: Within each cache domain h, plan[h] is a permutation of the 64 block numbers. `miss_ids`: row numbers into the peer's served table; slots at or past the count are unused. `miss_counts`: in every draw some peer is asked for 16 rows by every device. `self_ids`: each names a used fetched slot p * 16 + c of the same device, c below that device's count for peer p. `nbr_ids`: each names a used fetched slot p * 16 + c of the same device, c below that device's count for peer p. `hop_counts`: the first node of every device has 15. `seed_counts`: the first seed of every device has 25.
All inputs are finite; a program needn't handle non-finite values.
Results may differ from a plain program's by a relative error of at most 0.0052.
Values may be sent and summed in bfloat16 or wider, within the bound.
No kernel may reach another device: no remote copies, remote signals or barrier semaphores. Data moves between devices by JAX's collectives and lax.ppermute only.
A program may use at most 128 MiB of HBM per device.

v0:
```python
import jax
import jax.numpy as jnp
from jax import lax
from jax.sharding import PartitionSpec as P

FAN1 = 25
FAN2 = 15
CSLOT = 2
BLOCK = 128


def local_step(
    frontier, self_rows, nbr_rows, count_one, count_two, w_self1, w_nbr1, w_self2, w_nbr2, cot_rows
):
    seed_count = count_two.shape[0]
    width = w_self2.shape[0]
    width_in = frontier.shape[1]
    own_rows = frontier[self_rows]
    mask_one = jnp.arange(FAN2, dtype=jnp.int32)[None, :] < count_one[:, None]
    summed_one = jnp.zeros((own_rows.shape[0], width_in), jnp.float32)
    for k in range(FAN2):
        picked = frontier[nbr_rows[:, k]].astype(jnp.float32)
        summed_one = summed_one + jnp.where(mask_one[:, k][:, None], picked, jnp.zeros_like(picked))
    mean_one = (summed_one / count_one[:, None].astype(jnp.float32)).astype(jnp.bfloat16)
    hidden_pre = jnp.dot(own_rows, w_self1, preferred_element_type=jnp.float32) + jnp.dot(
        mean_one, w_nbr1, preferred_element_type=jnp.float32
    )
    hidden_one = jax.nn.silu(hidden_pre).astype(jnp.bfloat16)
    seed_rows = hidden_one[:seed_count]
    hop_rows = hidden_one[seed_count:].reshape(seed_count, FAN1, width)
    mask_two = jnp.arange(FAN1, dtype=jnp.int32)[None, :] < count_two[:, None]
    summed_two = jnp.einsum(
        "skh,sk->sh", hop_rows, mask_two.astype(jnp.bfloat16), preferred_element_type=jnp.float32
    )
    mean_two = (summed_two / count_two[:, None].astype(jnp.float32)).astype(jnp.bfloat16)
    embedding = (
        jnp.dot(seed_rows, w_self2, preferred_element_type=jnp.float32)
        + jnp.dot(mean_two, w_nbr2, preferred_element_type=jnp.float32)
    ).astype(jnp.bfloat16)
    grad_self2 = jnp.dot(cot_rows.T, seed_rows, preferred_element_type=jnp.float32)
    grad_nbr2 = jnp.dot(cot_rows.T, mean_two, preferred_element_type=jnp.float32)
    back_self = jnp.dot(cot_rows, w_self2.T, preferred_element_type=jnp.float32)
    back_mean = jnp.dot(cot_rows, w_nbr2.T, preferred_element_type=jnp.float32) / count_two[
        :, None
    ].astype(jnp.float32)
    back_hop = back_mean[:, None, :] * mask_two.astype(jnp.float32)[:, :, None]
    back_hidden = jnp.concatenate([back_self, back_hop.reshape(seed_count * FAN1, width)], 0)
    gate_value = jax.nn.sigmoid(hidden_pre)
    back_pre = (back_hidden * gate_value * (1.0 + hidden_pre * (1.0 - gate_value))).astype(
        jnp.bfloat16
    )
    grad_self1 = jnp.dot(back_pre.T, own_rows, preferred_element_type=jnp.float32)
    grad_nbr1 = jnp.dot(back_pre.T, mean_one, preferred_element_type=jnp.float32)
    return (embedding, (grad_self1, grad_nbr1, grad_self2, grad_nbr2))


def local(
    features,
    cache_blocks,
    plan,
    miss_ids,
    miss_counts,
    self_ids,
    nbr_ids,
    hop_counts,
    seed_counts,
    w_self1,
    w_nbr1,
    w_self2,
    w_nbr2,
    cotangent,
):
    width_in = features.shape[1]
    slot_count = miss_ids.shape[3]
    device_count = lax.axis_size(("hst", "dev"))
    start_cache = jnp.zeros((CSLOT, BLOCK, width_in), jnp.bfloat16)
    current = start_cache
    shard_rows = lax.all_gather(cache_blocks, "dev", axis=1, tiled=True)
    block_count = shard_rows.shape[1] // BLOCK
    arrived = shard_rows[0].reshape(block_count, BLOCK, width_in)
    for target in range(CSLOT):
        offset = plan[0, target]
        inside = (offset >= 0) & (offset < block_count)
        chosen = lax.dynamic_index_in_dim(
            arrived, jnp.clip(offset, 0, block_count - 1), 0, keepdims=False
        )
        current = current.at[target].set(jnp.where(inside, chosen, current[target]))
    new_cache = current.reshape(1, CSLOT * BLOCK, width_in)
    lookup_table = jnp.concatenate([features, new_cache[0]], 0)
    requests = miss_ids.reshape(device_count, slot_count)
    row_data = lookup_table[
        lax.all_to_all(requests, ("hst", "dev"), split_axis=0, concat_axis=0, tiled=True)
    ]
    fetched = lax.all_to_all(row_data, ("hst", "dev"), split_axis=0, concat_axis=0, tiled=True)
    counted = miss_counts.reshape(device_count)
    is_valid = jnp.arange(slot_count, dtype=jnp.int32)[None, :] < counted[:, None]
    fetched = jnp.where(is_valid[:, :, None], fetched, jnp.zeros_like(fetched))
    frontier = fetched.reshape(device_count * slot_count, width_in)
    embedding, grads = local_step(
        frontier,
        self_ids,
        nbr_ids,
        hop_counts,
        seed_counts,
        w_self1,
        w_nbr1,
        w_self2,
        w_nbr2,
        cotangent,
    )
    share_self1, share_nbr1, share_self2, share_nbr2 = (
        lax.psum_scatter(grads[0], ("hst", "dev"), scatter_dimension=0, tiled=True),
        lax.psum_scatter(grads[1], ("hst", "dev"), scatter_dimension=0, tiled=True),
        lax.psum_scatter(grads[2], ("hst", "dev"), scatter_dimension=0, tiled=True),
        lax.psum_scatter(grads[3], ("hst", "dev"), scatter_dimension=0, tiled=True),
    )
    return (embedding, new_cache, share_self1.T, share_nbr1.T, share_self2.T, share_nbr2.T)


def solution(mesh):
    return jax.shard_map(
        local,
        mesh=mesh,
        in_specs=(
            P(("hst", "dev"), None),
            P("hst", "dev", None),
            P("hst", "dev"),
            P(("hst", "dev"), None, None, None),
            P(("hst", "dev"), None, None),
            P(("hst", "dev")),
            P(("hst", "dev"), None),
            P(("hst", "dev")),
            P(("hst", "dev")),
            P(),
            P(),
            P(),
            P(),
            P(("hst", "dev"), None),
        ),
        out_specs=(
            P(("hst", "dev"), None),
            P("hst", "dev", None),
            P(None, ("hst", "dev")),
            P(None, ("hst", "dev")),
            P(None, ("hst", "dev")),
            P(None, ("hst", "dev")),
        ),
        check_vma=False,
    )
```

profile of v0, /device:TPU:0, one launch (start us, length us, event | category | flops | bytes accessed | tf_op | source)
XLA Modules:
  0.0 2006.4 jit_solution(17963824004215073880)
XLA Ops:
  7.2 0.7 all-gather.2.cloned.1.call-update
  7.9 1.5 copy.32
  9.4 11.2 all-to-all-start
  20.6 1.3 fusion.28
  25.8 0.8 lt.138
  26.5 0.7 convert_element_type.95
  27.2 0.7 convert_element_type.98
  27.9 1.9 all-to-all-done
  29.9 45.5 %all-gather.2.cloned.1.call-done = bf16[1,8192,768]{2,1,0:T(8,128)(2,1)} async-done(((bf16[1,256,768]{2,1,0:T(8,128)(2,1)}), bf16[1,8192,768]{2,1,0:T(8,128)(2,1)}) %all-gather.2.cloned.1.call-update) | async-done | bytes 12582928 | tf_op jit(solution)/shard_map/all_gather | solution.py:78
  75.5 1.1 dynamic-slice_select_fusion.1
  76.6 0.7 copy-done.10
  77.3 3.9 pad_maximum_fusion
  81.3 12.6 gather_fusion
  93.8 8.7 all-to-all-start.1
  102.6 2.3 convolution_divide_fusion
  104.9 2.6 mul.30
  107.5 3.8 mul.31
  111.4 0.1 reshape.188
  111.5 0.2 fusion.11
  111.9 0.7 slice_reduce_fusion.14
  112.7 1.4 fusion.30
  114.1 3.9 broadcast_multiply_fusion
  118.0 25.8 %all-to-all-done.1 = bf16[128,16,768]{2,1,0:T(8,128)(2,1)} async-done(((bf16[128,16,768]{2,1,0:T(8,128)(2,1)}), bf16[128,16,768]{2,1,0:T(8,128)(2,1)}, u32[]{:S(2)}, u32[]{:S(2)}) %all-to-all-start.1) | async-done | bytes 3145760 | tf_op jit(solution)/shard_map/all_to_all | solution.py:94
  143.8 3.3 broadcast_select_fusion
  147.1 6.7 gather_fusion.10
  153.8 7.1 gather_fusion.11
  160.9 7.1 gather_fusion.12
  168.0 7.1 gather_fusion.13
  175.1 7.1 gather_fusion.14
  182.2 7.1 gather_fusion.15
  189.2 7.1 gather_fusion.16
  196.3 7.3 gather_fusion.3
  203.6 7.1 gather_fusion.4
  210.7 7.1 gather_fusion.5
  217.8 7.1 gather_fusion.6
  224.8 7.1 gather_fusion.7
  231.9 7.1 gather_fusion.8
  239.0 7.1 gather_fusion.9
  246.1 7.1 gather_fusion.2
  253.2 7.3 gather_fusion.1
  260.6 3.4 fusion.29
  264.1 0.1 copy-done.6
  264.2 0.4 copy-done.7
  264.6 0.4 copy-done.8
  265.0 8.8 divide_convert_fusion
  273.8 3.9 fusion.1
  277.7 1.2 copy-done.25
  278.9 3.5 fusion.32
  282.5 1.2 copy-done.11
  283.7 5.1 fusion.31
  288.9 2.7 slice.226
  291.6 2.7 reshape.186
  294.3 2.0 fusion.4
  296.3 2.8 convolution_bitcast_fusion
  299.1 5.4 copy.35
  304.6 3.6 convolution_bitcast_fusion.1
  308.2 5.4 copy.33
  313.6 1.5 fusion.7
  315.0 0.2 copy-done.1
  315.2 1.1 fusion.2
  316.4 172.1 %reduce-scatter.11.cloned.1.call-done = f32[8,768]{1,0:T(8,128)} async-done(((f32[1024,768]{1,0:T(8,128)}), f32[8,768]{1,0:T(8,128)}) %reduce-scatter.11.cloned.1.call-update) | async-done | bytes 24592 | tf_op jit(solution)/shard_map/reduce_scatter | solution.py:113
  488.5 213.3 %reduce-scatter.9.cloned.1.call-done = f32[8,768]{1,0:T(8,128)} async-done(((f32[1024,768]{1,0:T(8,128)}), f32[8,768]{1,0:T(8,128)}) %reduce-scatter.9.cloned.1.call-update) | async-done | bytes 24592 | tf_op jit(solution)/shard_map/reduce_scatter | solution.py:112
  701.8 650.9 %reduce-scatter.15.cloned.1.call-done = f32[8,1024]{1,0:T(8,128)} async-done(((f32[1024,1024]{1,0:T(8,128)}), f32[8,1024]{1,0:T(8,128)}) %reduce-scatter.15.cloned.1.call-update) | async-done | bytes 32784
  1352.7 646.8 %reduce-scatter.13.cloned.1.call-done = f32[8,1024]{1,0:T(8,128)} async-done(((f32[1024,1024]{1,0:T(8,128)}), f32[8,1024]{1,0:T(8,128)}) %reduce-scatter.13.cloned.1.call-update) | async-done | bytes 32784
  (71 shorter events, 0.7 us)
Async XLA Ops:
  7.2 105.5 %copy-start = (bf16[1024,1024]{1,0:T(8,128)(2,1)S(1)}, bf16[1024,1024]{1,0:T(8,128)(2,1)}, u32[]{:S(2)}) copy-start(bf16[1024,1024]{1,0:T(8,128)(2,1)} %param.29) | copy-start | bytes 6291460
  7.2 68.3 %all-gather.2.cloned.1.call-start = ((), (), s32[]{:S(2)}) async-start(), calls=%async_computation.6 | async-start | bytes 12976128 | tf_op jit(solution)/shard_map/all_gather | solution.py:78
  9.4 20.4 %all-to-all-start = ((s32[128,1,16]{2,1,0:T(1,128)}), s32[128,1,16]{2,1,0:T(1,128)S(1)}, u32[]{:S(2)}, u32[]{:S(2)}) async-start(s32[128,1,16]{2,1,0:T(1,128)} %bitcast.6), calls=%async_computation | async-start | bytes 131072 | tf_op jit(solution)/shard_map/all_to_all | solution.py:92
  76.6 0.7 copy-start.10
  93.8 8.8 copy-start.12
  93.8 50.0 %all-to-all-start.1 = ((bf16[128,16,768]{2,1,0:T(8,128)(2,1)}), bf16[128,16,768]{2,1,0:T(8,128)(2,1)}, u32[]{:S(2)}, u32[]{:S(2)}) async-start(bf16[128,16,768]{2,1,0:T(8,128)(2,1)} %bitcast.66), calls=%async_computation.1 | async-start | bytes 6291456 | tf_op jit(solution)/shard_map/all_to_all | solution.py:94
  102.6 385.9 %reduce-scatter.11.cloned.1.call-start = ((), (), s32[]{:S(2)}) async-start(), calls=%async_computation.8 | async-start | bytes 3170304 | tf_op jit(solution)/shard_map/reduce_scatter | solution.py:113
  107.5 3.8 copy-start.23
  107.5 4.0 copy-start.14
  107.5 4.2 copy-start.22
  107.5 4.3 copy-start.15
  260.5 3.5 copy-start.2
  260.5 3.6 copy-start.3
  260.5 3.6 copy-start.4
  260.5 3.6 copy-start.5
  260.5 3.7 copy-start.6
  260.5 4.1 copy-start.7
  260.5 4.4 copy-start.8
  260.5 4.4 copy-start.16
  260.6 4.4 copy-start.17
  260.6 4.4 copy-start.18
  260.6 4.4 copy-start.19
  260.6 4.4 copy-start.20
  260.6 4.4 copy-start.21
  265.0 8.8 copy-start.9
  265.0 8.8 copy-start.13
  265.0 8.8 copy-start.24
  277.7 1.2 copy-start.25
  282.4 1.3 copy-start.11
  282.4 419.3 %reduce-scatter.9.cloned.1.call-start = ((), (), s32[]{:S(2)}) async-start(), calls=%async_computation.7 | async-start | bytes 3170304 | tf_op jit(solution)/shard_map/reduce_scatter | solution.py:112
  288.8 1063.8 %reduce-scatter.15.cloned.1.call-start = ((), (), s32[]{:S(2)}) async-start(), calls=%async_computation.10 | async-start | bytes 4227072
  304.5 1694.9 %reduce-scatter.13.cloned.1.call-start = ((), (), s32[]{:S(2)}) async-start(), calls=%async_computation.9 | async-start | bytes 4227072
  313.6 1.6 copy-start.1
Sparse Core Ops, SparseCore 0:
  10.2 65.1 all-gather.1
  282.6 205.8 reduce-scatter.10
  493.8 207.9 reduce-scatter.8
  704.6 648.0 reduce-scatter.14
  1355.4 643.9 reduce-scatter.12
where the time goes:
time: 2010 us
  waiting for transfers between devices  1760 us (88%)
  local copies, waits for them, and re-layouts  157 us (8%)
  matrix products  30.6 us (2%)
  other arithmetic  22.8 us (1%)
  starting transfers between devices  20.1 us (1%)
    unnamed x7, waiting for transfers between devices  1300 us
    reduce_scatter x1, waiting for transfers between devices, local(): lax.psum_scatter(grads[0], ('hst', 'dev'), scatter_dimension=0, tiled=True)  213 us
    reduce_scatter x1, waiting for transfers between devices, local(): lax.psum_scatter(grads[1], ('hst', 'dev'), scatter_dimension=0, tiled=True)  172 us
    gather x15, local copies, waits for them, and re-layouts, local_step(): picked = frontier[nbr_rows[:, k]].astype(jnp.float32)  106 us
    all_gather x1, waiting for transfers between devices, local(): shard_rows = lax.all_gather(cache_blocks, 'dev', axis=1, tiled=True)  45.5 us
  transfers between devices with their start and end apart: 7, of which 7 were waited for; matrix products, arithmetic and copies ran while one was open for 3% of the time, Pallas kernels for 0%

commit v1 on v0

v1 whole, which is shorter than its diff:
```python
import jax
import jax.numpy as jnp
from jax import lax
from jax.sharding import PartitionSpec as P

FAN1 = 25
FAN2 = 15
CSLOT = 2
BLOCK = 128
ALL = ("hst", "dev")
BF = jnp.bfloat16
F32 = jnp.float32


def parity_groups(hosts, devs):
    return [
        [h * devs + 2 * i + c for h in range(hosts) for i in range(devs // 2)] for c in range(2)
    ]


def plane_groups(hosts, devs):
    return [
        [h * devs + 2 * i + c for i in range(devs // 2)] for h in range(hosts) for c in range(2)
    ]


def exchange(x, axes, groups=None):
    return lax.all_to_all(
        x, axes, split_axis=0, concat_axis=0, tiled=True, axis_index_groups=groups
    )


def swap_pair(x, devs):
    return lax.ppermute(x, "dev", [(i, i ^ 1) for i in range(devs)])


def gather_octet(x, hosts, devs):
    pair = jnp.concatenate([x, swap_pair(x, devs)], 0)
    parts = [pair]
    for k in range(1, hosts):
        parts.append(lax.ppermute(pair, "hst", [(i, (i + k) % hosts) for i in range(hosts)]))
    return jnp.concatenate(parts, 0)


def local(
    features, cache_blocks, plan, miss_ids, miss_counts, self_ids, nbr_ids, hop_counts,
    seed_counts, w_self1, w_nbr1, w_self2, w_nbr2, cotangent,
):
    hosts = lax.axis_size("hst")
    devs = lax.axis_size("dev")
    count = hosts * devs
    rows_dev, width = features.shape
    hidden = w_self2.shape[0]
    cap = miss_ids.shape[3]
    nodes = self_ids.shape[0]
    seeds = seed_counts.shape[0]
    h = lax.axis_index("hst")
    core = lax.axis_index("dev") % 2
    half = width // 2
    groups = devs // 2
    sub = BLOCK // groups

    note = jnp.concatenate(
        [miss_ids.reshape(count, cap), jnp.broadcast_to(plan, (count, CSLOT))], 1
    )
    note = exchange(note[:, None, :], ALL)[:, 0, :]
    asked = note[:, :cap].reshape(count * cap)
    order = lax.dynamic_slice_in_dim(note[:, cap:], h * devs, devs, 0).reshape(devs * CSLOT)

    pieces = cache_blocks.reshape(CSLOT, groups, sub, 2, half).transpose(3, 1, 0, 2, 4)
    pieces = exchange(pieces.reshape(devs, CSLOT * sub, half), "dev")
    pieces = pieces.reshape(devs * CSLOT, sub, half)[order]
    pieces = exchange(pieces.reshape(devs, CSLOT * sub, half), "dev")
    moved = (
        pieces.reshape(2, groups, CSLOT, sub, half)
        .transpose(2, 1, 3, 0, 4)
        .reshape(CSLOT * BLOCK, width)
    )

    stored = features[jnp.minimum(asked, rows_dev - 1)]
    pick = ((asked - rows_dev)[:, None] == jnp.arange(CSLOT * BLOCK, dtype=jnp.int32)).astype(BF)
    cached = jnp.dot(pick, moved, preferred_element_type=F32).astype(BF)
    served = jnp.where((asked < rows_dev)[:, None], stored, cached)
    fetched = exchange(served.reshape(count, cap, width), ALL).reshape(count * cap, width)

    slot = jnp.arange(count * cap, dtype=jnp.int32)
    used = (jnp.arange(cap, dtype=jnp.int32) < miss_counts.reshape(count, 1)).reshape(-1)
    used = used.astype(BF)
    pick_self = (self_ids[:, None] == slot).astype(BF) * used
    named = jnp.where(jnp.arange(FAN2, dtype=jnp.int32) < hop_counts[:, None], nbr_ids, -1)
    pick_nbr = jnp.zeros((nodes, count * cap), BF)
    for k in range(FAN2):
        pick_nbr = pick_nbr + (named[:, k][:, None] == slot).astype(BF)
    pick_nbr = pick_nbr * used

    own = jnp.dot(pick_self, fetched, preferred_element_type=F32).astype(BF)
    total = jnp.dot(pick_nbr, fetched, preferred_element_type=F32)
    mean_one = (total / hop_counts[:, None].astype(F32)).astype(BF)
    pre = jnp.dot(own, w_self1, preferred_element_type=F32) + jnp.dot(
        mean_one, w_nbr1, preferred_element_type=F32
    )
    gate = jax.nn.sigmoid(pre)
    hidden_one = (pre * gate).astype(BF)
    seed_rows = hidden_one[:seeds]

    position = jnp.arange(nodes, dtype=jnp.int32) - seeds
    owner = jnp.where(position >= 0, position // FAN1, -1)
    live = (owner == jnp.arange(seeds, dtype=jnp.int32)[:, None]) & (
        position % FAN1 < seed_counts[:, None]
    )
    live = live.astype(BF)
    seed_float = seed_counts[:, None].astype(F32)
    total_two = jnp.dot(live, hidden_one, preferred_element_type=F32)
    mean_two = (total_two / seed_float).astype(BF)
    embedding = (
        jnp.dot(seed_rows, w_self2, preferred_element_type=F32)
        + jnp.dot(mean_two, w_nbr2, preferred_element_type=F32)
    ).astype(BF)

    cot_rows = gather_octet(cotangent, hosts, devs)
    cot_rows = lax.dynamic_slice_in_dim(cot_rows, h * (hidden // hosts), hidden // hosts, 1)
    both = gather_octet(jnp.concatenate([seed_rows, mean_two], 1), hosts, devs)
    part_two = lax.dot_general(
        cot_rows, both, (((0,), (0,)), ((), ())), preferred_element_type=F32
    )
    cols = hidden // count
    part_two = part_two.reshape(groups, 2, cols, 2 * hidden)
    part_two = lax.dynamic_index_in_dim(part_two, core, 1, keepdims=False).astype(BF)
    part_two = exchange(part_two, ALL, plane_groups(hosts, devs))
    sum_two = jnp.sum(part_two.astype(F32), 0)

    back_self = lax.dot_general(
        cotangent, w_self2, (((1,), (1,)), ((), ())), preferred_element_type=F32
    )
    back_mean = (
        lax.dot_general(cotangent, w_nbr2, (((1,), (1,)), ((), ())), preferred_element_type=F32)
        / seed_float
    )
    seat = jnp.arange(FAN1, dtype=jnp.int32)[None, :] < seed_counts[:, None]
    back_hop = back_mean[:, None, :] * seat.astype(F32)[:, :, None]
    back = jnp.concatenate([back_self, back_hop.reshape(seeds * FAN1, hidden)], 0)
    back_pre = (back * gate * (1.0 + pre * (1.0 - gate))).astype(BF)

    rows_one = jnp.concatenate([own, mean_one], 1)
    part_one = lax.dot_general(
        back_pre, rows_one, (((0,), (0,)), ((), ())), preferred_element_type=F32
    )
    part_one = part_one.reshape(count // 2, 2, cols, 2 * width)
    give = lax.dynamic_index_in_dim(part_one, 1 - core, 1, keepdims=False).astype(BF)
    keep = lax.dynamic_index_in_dim(part_one, core, 1, keepdims=False)
    part_one = (keep + swap_pair(give, devs).astype(F32)).astype(BF)
    part_one = exchange(part_one, ALL, parity_groups(hosts, devs))
    sum_one = jnp.sum(part_one.astype(F32), 0)
    return (
        embedding,
        moved[None],
        sum_one[:, :width].T,
        sum_one[:, width:].T,
        sum_two[:, :hidden].T,
        sum_two[:, hidden:].T,
    )


def solution(mesh):
    return jax.shard_map(
        local,
        mesh=mesh,
        in_specs=(
            P(ALL, None), P("hst", "dev", None), P("hst", "dev"), P(ALL, None, None, None),
            P(ALL, None, None), P(ALL), P(ALL, None), P(ALL), P(ALL), P(), P(), P(), P(),
            P(ALL, None),
        ),
        out_specs=(
            P(ALL, None), P("hst", "dev", None), P(None, ALL), P(None, ALL), P(None, ALL),
            P(None, ALL),
        ),
        check_vma=False,
    )
```

time: 2010 us -> 217 us (0.11)
  waiting for transfers between devices: 1760 us -> 58.4 us
  local copies, waits for them, and re-layouts: 157 us -> 41.9 us
  starting transfers between devices: 20.1 us -> 50.6 us
    unnamed x7 -> x0, waiting for transfers between devices: 1300 us -> none
    reduce_scatter x2 -> x0, waiting for transfers between devices: 385 us -> none  [the longest x1 213 us: local(): lax.psum_scatter(grads[0], ('hst', 'dev'), scatter_dimension=0, tiled=True)]
    gather x17 -> x2, local copies, waits for them, and re-layouts: 126 us -> 10.8 us  [the longest x1 9.42 us: local(): stored = features[jnp.minimum(asked, rows_dev - 1)]]
    all_gather x1 -> x0, waiting for transfers between devices: 45.5 us -> none  [local(): shard_rows = lax.all_gather(cache_blocks, 'dev', axis=1, tiled=True)]
    ppermute x0 -> x9, waiting for transfers between devices: none -> 23.7 us  [the longest x6 23.7 us: gather_octet(): lax.ppermute(pair, 'hst', [(i, (i + k) % hosts) for i in range(hosts)])]
    all_to_all x2 -> x6, starting transfers between devices: 19.9 us -> 41.4 us  [exchange(): lax.all_to_all(x, axes, split_axis=0, concat_axis=0, tiled=True, axis_ind...]
    dot_general x11 -> x12, matrix products: 30.6 us -> 44.9 us  [the longest x1 17.5 us: local(): total = jnp.dot(pick_nbr, fetched, preferred_element_type=F32)]
  transfers between devices with their start and end apart: 7 -> 15, of which waited for: 7 -> 8; matrix products, arithmetic and copies ran while one was open for 3% -> 43% of each run, Pallas kernels for 0% -> 0%
where the time goes in v1:
time: 217 us; the launch traced here: 216 us
  waiting for transfers between devices  58.4 us (27%)
  starting transfers between devices  50.6 us (23%)
  matrix products  44.9 us (21%)
  local copies, waits for them, and re-layouts  41.9 us (19%)
  other arithmetic  18.6 us (9%)
    all_to_all x6, starting transfers between devices, exchange(): lax.all_to_all(x, axes, split_axis=0, concat_axis=0, tiled=True, axis_ind...  41.4 us
    all_to_all x6, waiting for transfers between devices, exchange(): lax.all_to_all(x, axes, split_axis=0, concat_axis=0, tiled=True, axis_ind...  34.8 us
    ppermute x6, waiting for transfers between devices, gather_octet(): lax.ppermute(pair, 'hst', [(i, (i + k) % hosts) for i in range(hosts)])  23.7 us
    dot_general x1, matrix products, local(): total = jnp.dot(pick_nbr, fetched, preferred_element_type=F32)  17.5 us
    gather x1, local copies, waits for them, and re-layouts, local(): stored = features[jnp.minimum(asked, rows_dev - 1)]  9.42 us
    ppermute x6, starting transfers between devices, gather_octet(): lax.ppermute(pair, 'hst', [(i, (i + k) % hosts) for i in range(hosts)])  8.78 us
    unnamed x78, local copies, waits for them, and re-layouts  6.17 us
    mul x2, local copies, waits for them, and re-layouts, local(): back_hop = back_mean[:, None, :] * seat.astype(F32)[:, :, None]  6.16 us
  transfers between devices with their start and end apart: 15, of which 8 were waited for; matrix products, arithmetic and copies ran while one was open for 43% of the time, Pallas kernels for 0%

profile of v1, /device:TPU:0, one launch (start us, length us, event | category | flops | bytes accessed | tf_op | source)
XLA Modules:
  0.0 215.8 jit_solution(5652070504357789817)
XLA Ops:
  0.6 0.9 copy.33
  1.7 0.7 pad.12.clone
  2.5 0.7 copy.34
  3.2 11.7 %all-to-all-start = ((s32[128,1,18]{2,1,0:T(1,128)}), s32[128,1,18]{2,1,0:T(1,128)}, u32[]{:S(2)}, u32[]{:S(2)}) async-start(s32[128,1,18]{2,1,0:T(1,128)} %copy.34), calls=%async_computation | async-start | bytes 131072 | tf_op jit(solution)/shard_map/all_to_all | solution.py:28
  14.9 1.1 reshape.185
  16.0 0.8 copy.35
  16.8 7.2 %all-to-all-done = s32[128,1,18]{2,1,0:T(1,128)} async-done(((s32[128,1,18]{2,1,0:T(1,128)}), s32[128,1,18]{2,1,0:T(1,128)}, u32[]{:S(2)}, u32[]{:S(2)}) %all-to-all-start) | async-done | bytes 9248 | tf_op jit(solution)/shard_map/all_to_all | solution.py:28
  24.0 3.9 %all-to-all-start.1 = ((bf16[32,16,384]{2,1,0:T(8,128)(2,1)}), bf16[32,16,384]{2,1,0:T(8,128)(2,1)S(1)}, u32[]{:S(2)}, u32[]{:S(2)}) async-start(bf16[32,16,384]{2,1,0:T(8,128)(2,1)} %bitcast.5), calls=%async_computation.1 | async-start | bytes 786432 | tf_op jit(solution)/shard_map/all_to_all | solution.py:28
  27.9 0.9 slice.93
  28.8 1.5 slice_add_fusion
  31.0 0.7 fusion.105
  31.6 0.9 min.18
  33.2 4.9 %all-to-all-done.1 = bf16[32,16,384]{2,1,0:T(8,128)(2,1)S(1)} async-done(((bf16[32,16,384]{2,1,0:T(8,128)(2,1)}), bf16[32,16,384]{2,1,0:T(8,128)(2,1)S(1)}, u32[]{:S(2)}, u32[]{:S(2)}) %all-to-all-start.1) | async-done | bytes 393248 | tf_op jit(solution)/shard_map/all_to_all | solution.py:28
  38.1 1.4 gather_fusion.1
  39.5 3.9 %all-to-all-start.2 = ((bf16[32,16,384]{2,1,0:T(8,128)(2,1)}), bf16[32,16,384]{2,1,0:T(8,128)(2,1)S(1)}, u32[]{:S(2)}, u32[]{:S(2)}) async-start(bf16[32,16,384]{2,1,0:T(8,128)(2,1)} %bitcast.63), calls=%async_computation.2 | async-start | bytes 786432 | tf_op jit(solution)/shard_map/all_to_all | solution.py:28
  43.4 0.9 slice_compare_fusion
  44.2 0.7 lt.133
  44.9 0.9 sub.24
  45.8 0.7 broadcast_clamp_fusion
  46.5 9.4 %gather_fusion = bf16[2048,768]{1,0:T(8,128)(2,1)} fusion(bf16[2048,768]{1,0:T(8,128)(2,1)S(1)} %copy-done, s32[2048]{0:T(1024)S(1)} %broadcast_clamp_fusion), kind=kCustom, calls=%fused_computation | custom fusion | bytes 6299648 | tf_op jit(solution)/shard_map/gather | solution.py:80
  56.0 0.7 copy-done.4
  56.7 1.4 copy.36
  58.2 3.9 %broadcast_select_fusion = bf16[2048,768]{1,0:T(8,128)(2,1)} fusion(bf16[2048,768]{1,0:T(8,128)(2,1)} %gather_fusion, pred[2048]{0:T(1024)(128)(4,1)} %lt.133, bf16[256,768]{1,0:T(8,128)(2,1)S(1)} %bitcast.64, s32[2048]{0:T(1024)S(1)} %sub.24), kind=kOutput, calls=%fused_computation.77 | convolution fusion | flops 808976384 | bytes 6694912 | tf_op jit(solution)/shard_map/dot_general | solution.py:82
  62.1 8.9 %all-to-all-start.3 = ((bf16[128,16,768]{2,1,0:T(8,128)(2,1)}), bf16[128,16,768]{2,1,0:T(8,128)(2,1)}, u32[]{:S(2)}, u32[]{:S(2)}) async-start(bf16[128,16,768]{2,1,0:T(8,128)(2,1)} %bitcast.58), calls=%async_computation.3 | async-start | bytes 6291456 | tf_op jit(solution)/shard_map/all_to_all | solution.py:28
  72.3 0.7 fusion.96
  73.0 0.7 reshape.197
  73.7 2.3 %convolution_divide_fusion = f32[32,1024]{1,0:T(8,128)S(1)} fusion(bf16[32,1024]{1,0:T(8,128)(2,1)} %param.27, bf16[1024,1024]{1,0:T(8,128)(2,1)} %param.26, f32[32]{0:T(128)} %convert_element_type.143), kind=kOutput, calls=%fused_computation.91 | convolution fusion | flops 67141632 | bytes 2293888 | tf_op jit(solution)/shard_map/dot_general | solution.py:136
  76.0 2.5 %mul.53 = f32[32,25,1024]{2,1,0:T(8,128)} broadcast(f32[32,1024]{1,0:T(8,128)S(1)} %convolution_divide_fusion), dimensions={0,2} | broadcast | bytes 3407872 | tf_op jit(solution)/shard_map/mul | solution.py:140
  78.5 3.7 %mul.54 = f32[800,1024]{1,0:T(8,128)} reshape(f32[32,25,1024]{2,1,0:T(8,128)} %mul.53) | data formatting | bytes 6553600 | tf_op jit(solution)/shard_map/mul | solution.py:140
  82.2 0.7 fusion.91
  82.9 0.8 fusion.95
  83.7 3.0 %fusion.113 = f32[32,1024]{1,0:T(8,128)} fusion(bf16[32,1024]{1,0:T(8,128)(2,1)} %param.27, bf16[1024,1024]{1,0:T(8,128)(2,1)} %param.25), kind=kOutput, calls=%fused_computation.176 | convolution fusion | flops 67108864 | bytes 2293760 | tf_op jit(solution)/shard_map/dot_general | solution.py:132
  86.7 4.0 %broadcast_multiply_fusion = f32[800,1024]{1,0:T(8,128)} fusion(f32[800,1024]{1,0:T(8,128)} %mul.54, f32[800]{0:T(1024)S(1)} %copy-done.10), kind=kLoop, calls=%fused_computation.88 | loop fusion | flops 819200 | bytes 6556800 | tf_op jit(solution)/shard_map/mul | solution.py:140
  90.7 0.7 constant_dynamic-update-slice_fusion.1
  91.4 1.5 constant_dynamic-update-slice_fusion
  92.9 1.1 collective-permute-start.2
  94.0 0.7 slice_reduce_fusion.14
  94.7 3.2 %collective-permute-start.3 = (bf16[64,1024]{1,0:T(8,128)(2,1)}, bf16[64,1024]{1,0:T(8,128)(2,1)}, u32[]{:S(2)}, u32[]{:S(2)}) collective-permute-start(bf16[64,1024]{1,0:T(8,128)(2,1)} %get-tuple-element.25), channel_id=1, source_target_pairs={{0,64},{32,96},{64,0},{96,32},{1,65},{33,97},{65,1},{97,33},{2,66}... | collective-permute-start | bytes 393224 | tf_op jit(solution)/shard_map/ppermute | solution.py:41
  98.6 0.9 reshape.196
  99.4 1.3 collective-permute-start.4
  100.7 9.8 %collective-permute-done.2 = bf16[64,1024]{1,0:T(8,128)(2,1)} collective-permute-done((bf16[64,1024]{1,0:T(8,128)(2,1)}, bf16[64,1024]{1,0:T(8,128)(2,1)}, u32[]{:S(2)}, u32[]{:S(2)}) %collective-permute-start.2) | collective-permute-done | bytes 131104 | tf_op jit(solution)/shard_map/ppermute | solution.py:41
  110.5 1.6 constant_dynamic-update-slice_fusion.4
  112.1 2.4 %collective-permute-done.3 = bf16[64,1024]{1,0:T(8,128)(2,1)} collective-permute-done((bf16[64,1024]{1,0:T(8,128)(2,1)}, bf16[64,1024]{1,0:T(8,128)(2,1)}, u32[]{:S(2)}, u32[]{:S(2)}) %collective-permute-start.3) | collective-permute-done | bytes 131104 | tf_op jit(solution)/shard_map/ppermute | solution.py:41
  114.4 1.6 constant_dynamic-update-slice_fusion.3
  116.0 4.9 %fusion.78 = bf16[832,768]{1,0:T(8,128)(2,1)S(1)} fusion(bf16[2048,768]{1,0:T(8,128)(2,1)} %bitcast.12, s32[832]{0:T(1024)} %param.19, bf16[2048]{0:T(1024)(128)(2,1)S(1)} %reshape.196), kind=kOutput, calls=%fused_computation.89 | convolution fusion | flops 2621292544 | bytes 4431104 | tf_op jit(solution)/shard_map/dot_general | solution.py:96
  121.1 1.5 fusion.112
  122.8 17.5 %divide_convert_fusion = bf16[832,768]{1,0:T(8,128)(2,1)S(1)} fusion(bf16[2048,768]{1,0:T(8,128)(2,1)} %bitcast.12, s32[832]{0:T(1024)S(1)} %copy-done.11, s32[832]{0:T(1024)S(1)} %copy-done.12, s32[832]{0:T(1024)S(1)} %copy-done.13, s32[832]{0:T(1024)S(1)} %copy-done.14, s32[832]{0:T(1024)S(1)} %copy-done.15, s32[832]{0:T(1024)S(1)} %copy-done.16, ...), kind=kOutput, calls=%fused_computation.82 | convolution fusion | flops 2724167680 | bytes 4481024 | tf_op jit(solution)/shard_map/dot_general | solution.py:97
  140.3 1.9 multiply_convert_fusion
  143.5 4.1 %fusion.68 = f32[1024,1536]{1,0:T(8,128)S(1)} fusion(bf16[832,768]{1,0:T(8,128)(2,1)S(1)} %divide_convert_fusion, bf16[832,768]{1,0:T(8,128)(2,1)S(1)} %fusion.78, f32[800,1024]{1,0:T(8,128)S(1)} %copy-done.2, f32[32,1024]{1,0:T(8,128)S(1)} %copy-done.7, f32[832,1024]{1,0:T(8,128)S(1)} %get-tuple-element.34), kind=kOutput, calls=%fused_computation.78 | convolution fusion | flops 2630877184 | bytes 15663104 | tf_op jit(solution)/shard_map/dot_general | solution.py:145
  147.7 1.4 fusion.81
  149.2 1.1 constant_dynamic-update-slice_fusion.2
  150.3 3.1 %collective-permute-start.8 = (bf16[64,2048]{1,0:T(8,128)(2,1)S(1)}, bf16[64,2048]{1,0:T(8,128)(2,1)S(1)}, u32[]{:S(2)}, u32[]{:S(2)}) collective-permute-start(bf16[64,2048]{1,0:T(8,128)(2,1)S(1)} %pad_maximum_fusion), channel_id=1, source_target_pairs={{0,96},{32,0},{64,32},{96,64},{1,97},{33,1},{65,33},{97,65},{2,98}... | collective-permute-start | bytes 786440 | tf_op jit(solution)/shard_map/ppermute | solution.py:41
  153.4 11.3 %collective-permute-done.6 = bf16[64,2048]{1,0:T(8,128)(2,1)S(1)} collective-permute-done((bf16[64,2048]{1,0:T(8,128)(2,1)S(1)}, bf16[64,2048]{1,0:T(8,128)(2,1)S(1)}, u32[]{:S(2)}, u32[]{:S(2)}) %collective-permute-start.6) | collective-permute-done | bytes 262176 | tf_op jit(solution)/shard_map/ppermute | solution.py:41
  165.5 0.9 fusion.85
  166.3 5.7 %all-to-all-start.5 = ((bf16[16,8,2048]{2,1,0:T(8,128)(2,1)}), bf16[16,8,2048]{2,1,0:T(8,128)(2,1)}, u32[]{:S(2)}, u32[]{:S(2)}) async-start(bf16[16,8,2048]{2,1,0:T(8,128)(2,1)} %fusion.85), calls=%async_computation.5 | async-start | bytes 1048576 | tf_op jit(solution)/shard_map/all_to_all | solution.py:28
  172.0 4.0 %fusion.67 = bf16[64,8,1536]{2,1,0:T(8,128)(2,1)} fusion(bf16[64,8,1536]{2,1,0:T(8,128)(2,1)} %collective-permute-done, f32[64,2,8,1536]{3,2,1,0:T(8,128)} %bitcast.56, s32[]{:T(128)S(6)} %select_n.86), kind=kLoop, calls=%fused_computation.74 | loop fusion | flops 2359296 | bytes 6291460 | tf_op jit(solution)/shard_map/convert_element_type | solution.py:151
  176.0 7.2 %all-to-all-done.5 = bf16[16,8,2048]{2,1,0:T(8,128)(2,1)} async-done(((bf16[16,8,2048]{2,1,0:T(8,128)(2,1)}), bf16[16,8,2048]{2,1,0:T(8,128)(2,1)}, u32[]{:S(2)}, u32[]{:S(2)}) %all-to-all-start.5) | async-done | bytes 524320 | tf_op jit(solution)/shard_map/all_to_all | solution.py:28
  183.2 7.3 %all-to-all-start.4 = ((bf16[64,8,1536]{2,1,0:T(8,128)(2,1)}), bf16[64,8,1536]{2,1,0:T(8,128)(2,1)}, u32[]{:S(2)}, u32[]{:S(2)}) async-start(bf16[64,8,1536]{2,1,0:T(8,128)(2,1)} %fusion.67), calls=%async_computation.4 | async-start | bytes 3145728 | tf_op jit(solution)/shard_map/all_to_all | solution.py:28
  190.5 1.0 broadcast_in_dim_reshape.3
  191.5 2.1 fusion.110
  193.6 2.7 %fusion.83 = bf16[32,1024]{1,0:T(8,128)(2,1)} fusion(f32[32,1024]{1,0:T(8,128)S(1)} %fusion.110, bf16[32,1024]{1,0:T(8,128)(2,1)} %copy-done.5, bf16[1024,1024]{1,0:T(8,128)(2,1)} %param.26), kind=kOutput, calls=%fused_computation.95 | convolution fusion | flops 67174400 | bytes 2359296 | tf_op jit(solution)/shard_map/dot_general | solution.py:117
  196.3 1.1 convert_reduce_fusion.1
  198.1 15.4 %all-to-all-done.4 = bf16[64,8,1536]{2,1,0:T(8,128)(2,1)} async-done(((bf16[64,8,1536]{2,1,0:T(8,128)(2,1)}), bf16[64,8,1536]{2,1,0:T(8,128)(2,1)}, u32[]{:S(2)}, u32[]{:S(2)}) %all-to-all-start.4) | async-done | bytes 1572896 | tf_op jit(solution)/shard_map/all_to_all | solution.py:28
  213.5 1.7 convert_reduce_fusion
  (104 shorter events, 6.8 us)
Async XLA Ops:
  0.6 45.9 %copy-start = (bf16[2048,768]{1,0:T(8,128)(2,1)S(1)}, bf16[2048,768]{1,0:T(8,128)(2,1)}, u32[]{:S(2)}) copy-start(bf16[2048,768]{1,0:T(8,128)(2,1)} %param.14) | copy-start | bytes 9437188
  3.2 20.8 %all-to-all-start = ((s32[128,1,18]{2,1,0:T(1,128)}), s32[128,1,18]{2,1,0:T(1,128)}, u32[]{:S(2)}, u32[]{:S(2)}) async-start(s32[128,1,18]{2,1,0:T(1,128)} %copy.34), calls=%async_computation | async-start | bytes 131072 | tf_op jit(solution)/shard_map/all_to_all | solution.py:28
  24.0 14.1 %all-to-all-start.1 = ((bf16[32,16,384]{2,1,0:T(8,128)(2,1)}), bf16[32,16,384]{2,1,0:T(8,128)(2,1)S(1)}, u32[]{:S(2)}, u32[]{:S(2)}) async-start(bf16[32,16,384]{2,1,0:T(8,128)(2,1)} %bitcast.5), calls=%async_computation.1 | async-start | bytes 786432 | tf_op jit(solution)/shard_map/all_to_all | solution.py:28
  39.5 16.5 %all-to-all-start.2 = ((bf16[32,16,384]{2,1,0:T(8,128)(2,1)}), bf16[32,16,384]{2,1,0:T(8,128)(2,1)S(1)}, u32[]{:S(2)}, u32[]{:S(2)}) async-start(bf16[32,16,384]{2,1,0:T(8,128)(2,1)} %bitcast.63), calls=%async_computation.2 | async-start | bytes 786432 | tf_op jit(solution)/shard_map/all_to_all | solution.py:28
  56.0 0.7 copy-start.4
  62.1 9.0 %copy-start.29 = (s32[32]{0:T(128)S(1)}, s32[32]{0:T(128)}, u32[]{:S(2)}) copy-start(s32[32]{0:T(128)} %param.22) | copy-start | bytes 388
  62.1 9.6 %copy-start.32 = (s32[1,4,32]{2,1,0:T(4,128)S(1)}, s32[1,4,32]{2,1,0:T(4,128)}, u32[]{:S(2)}) copy-start(s32[1,4,32]{2,1,0:T(4,128)} %param.18) | copy-start | bytes 1540
  62.1 53.9 %all-to-all-start.3 = ((bf16[128,16,768]{2,1,0:T(8,128)(2,1)}), bf16[128,16,768]{2,1,0:T(8,128)(2,1)}, u32[]{:S(2)}, u32[]{:S(2)}) async-start(bf16[128,16,768]{2,1,0:T(8,128)(2,1)} %bitcast.58), calls=%async_computation.3 | async-start | bytes 6291456 | tf_op jit(solution)/shard_map/all_to_all | solution.py:28
  71.0 20.4 %collective-permute-start.1 = (bf16[32,1024]{1,0:T(8,128)(2,1)}, bf16[32,1024]{1,0:T(8,128)(2,1)}, u32[]{:S(2)}, u32[]{:S(2)}) collective-permute-start(bf16[32,1024]{1,0:T(8,128)(2,1)} %param.27), channel_id=1, source_target_pairs={{0,1},{1,0},{2,3},{3,2},{4,5},{5,4},{6,7},{7,6},{8,9},{9,8},{10,11... | collective-permute-start | bytes 196616 | tf_op jit(solution)/shard_map/ppermute | solution.py:34
  78.5 3.7 %copy-start.31 = (s32[128]{0:T(128)S(1)}, s32[128]{0:T(128)}, u32[]{:S(2)}) copy-start(s32[128]{0:T(128)} %lt.129) | copy-start | bytes 1540
  78.5 4.4 %copy-start.9 = (s32[832]{0:T(1024)S(1)}, s32[832]{0:T(1024)}, u32[]{:S(2)}) copy-start(s32[832]{0:T(1024)} %param.21) | copy-start | bytes 9988
  78.5 8.2 %copy-start.10 = (f32[800]{0:T(1024)S(1)}, f32[800]{0:T(1024)}, u32[]{:S(2)}) copy-start(f32[800]{0:T(1024)} %reshape.197) | copy-start | bytes 9604
  86.7 4.0 %copy-start.6 = (bf16[32,1024]{1,0:T(8,128)(2,1)S(1)}, bf16[32,1024]{1,0:T(8,128)(2,1)}, u32[]{:S(2)}) copy-start(bf16[32,1024]{1,0:T(8,128)(2,1)} %param.27) | copy-start | bytes 196612
  92.9 17.6 %collective-permute-start.2 = (bf16[64,1024]{1,0:T(8,128)(2,1)}, bf16[64,1024]{1,0:T(8,128)(2,1)}, u32[]{:S(2)}, u32[]{:S(2)}) collective-permute-start(bf16[64,1024]{1,0:T(8,128)(2,1)} %get-tuple-element.25), channel_id=1, source_target_pairs={{0,32},{32,64},{64,96},{96,0},{1,33},{33,65},{65,97},{97,1},{2,34}... | collective-permute-start | bytes 393224 | tf_op jit(solution)/shard_map/ppermute | solution.py:41
  94.7 19.7 %collective-permute-start.3 = (bf16[64,1024]{1,0:T(8,128)(2,1)}, bf16[64,1024]{1,0:T(8,128)(2,1)}, u32[]{:S(2)}, u32[]{:S(2)}) collective-permute-start(bf16[64,1024]{1,0:T(8,128)(2,1)} %get-tuple-element.25), channel_id=1, source_target_pairs={{0,64},{32,96},{64,0},{96,32},{1,65},{33,97},{65,1},{97,33},{2,66}... | collective-permute-start | bytes 393224 | tf_op jit(solution)/shard_map/ppermute | solution.py:41
  99.4 16.6 %copy-start.25 = (bf16[2048]{0:T(1024)(128)(2,1)}, bf16[2048]{0:T(1024)(128)(2,1)S(1)}, u32[]{:S(2)}) copy-start(bf16[2048]{0:T(1024)(128)(2,1)S(1)} %reshape.196) | copy-start | bytes 12292
  99.4 49.7 %collective-permute-start.4 = (bf16[64,1024]{1,0:T(8,128)(2,1)}, bf16[64,1024]{1,0:T(8,128)(2,1)}, u32[]{:S(2)}, u32[]{:S(2)}) collective-permute-start(bf16[64,1024]{1,0:T(8,128)(2,1)} %get-tuple-element.25), channel_id=1, source_target_pairs={{0,96},{32,0},{64,32},{96,64},{1,97},{33,1},{65,33},{97,65},{2,98}... | collective-permute-start | bytes 393224 | tf_op jit(solution)/shard_map/ppermute | solution.py:41
  116.0 4.9 %copy-start.33 = (bf16[768,1024]{1,0:T(8,128)(2,1)S(1)}, bf16[768,1024]{1,0:T(8,128)(2,1)}, u32[]{:S(2)}) copy-start(bf16[768,1024]{1,0:T(8,128)(2,1)} %param.23) | copy-start | bytes 4718596
  120.9 1.7 copy-start.11
  120.9 1.7 copy-start.12
  120.9 1.7 copy-start.13
  120.9 1.7 copy-start.14
  121.0 1.7 copy-start.15
  121.0 1.7 copy-start.16
  121.0 1.7 copy-start.17
  121.0 1.7 copy-start.18
  121.0 1.7 copy-start.19
  121.0 1.7 copy-start.20
  121.0 1.7 copy-start.21
  121.0 1.7 copy-start.22
  121.0 1.7 copy-start.23
  121.1 1.7 copy-start.24
  121.1 1.7 copy-start.26
  121.1 1.7 copy-start.27
  122.7 17.5 %copy-start.34 = (bf16[768,1024]{1,0:T(8,128)(2,1)S(1)}, bf16[768,1024]{1,0:T(8,128)(2,1)}, u32[]{:S(2)}) copy-start(bf16[768,1024]{1,0:T(8,128)(2,1)} %param.24) | copy-start | bytes 4718596
  140.3 2.0 copy-start.28
  140.3 2.0 copy-start.30
  140.3 3.2 %copy-start.2 = (f32[800,1024]{1,0:T(8,128)S(1)}, f32[800,1024]{1,0:T(8,128)}, u32[]{:S(2)}) copy-start(f32[800,1024]{1,0:T(8,128)} %broadcast_multiply_fusion) | copy-start | bytes 9830404
  140.3 3.2 %copy-start.7 = (f32[32,1024]{1,0:T(8,128)S(1)}, f32[32,1024]{1,0:T(8,128)}, u32[]{:S(2)}) copy-start(f32[32,1024]{1,0:T(8,128)} %fusion.113) | copy-start | bytes 393220
  142.3 1.3 copy-start.3
  142.7 6.3 %copy-start.5 = (bf16[32,1024]{1,0:T(8,128)(2,1)}, bf16[32,1024]{1,0:T(8,128)(2,1)S(1)}, u32[]{:S(2)}) copy-start(bf16[32,1024]{1,0:T(8,128)(2,1)S(1)} %fusion.82) | copy-start | bytes 196612
  142.8 6.3 %collective-permute-start.5 = (bf16[32,2048]{1,0:T(8,128)(2,1)S(1)}, bf16[32,2048]{1,0:T(8,128)(2,1)S(1)}, u32[]{:S(2)}, u32[]{:S(2)}) collective-permute-start(bf16[32,2048]{1,0:T(8,128)(2,1)S(1)} %get-tuple-element.21), channel_id=1, source_target_pairs={{0,1},{1,0},{2,3},{3,2},{4,5},{5,4},{6,7},{7,6},{8,9},{9,8},{10,11... | collective-permute-start | bytes 393224 | tf_op jit(solution)/shard_map/ppermute | solution.py:34
  147.6 17.8 %copy-start.1 = (f32[1024,1536]{1,0:T(8,128)}, f32[1024,1536]{1,0:T(8,128)S(1)}, u32[]{:S(2)}) copy-start(f32[1024,1536]{1,0:T(8,128)S(1)} %fusion.68) | copy-start | bytes 18874372
  147.7 1.5 copy-start.8
  149.0 23.0 %collective-permute-start = (bf16[64,8,1536]{2,1,0:T(8,128)(2,1)}, bf16[64,8,1536]{2,1,0:T(8,128)(2,1)}, u32[]{:S(2)}, u32[]{:S(2)}) collective-permute-start(bf16[64,8,1536]{2,1,0:T(8,128)(2,1)} %fusion.81), channel_id=1, source_target_pairs={{0,1},{1,0},{2,3},{3,2},{4,5},{5,4},{6,7},{7,6},{8,9},{9,8},{10,11... | collective-permute-start | bytes 4718600 | tf_op jit(solution)/shard_map/ppermute | solution.py:34
  149.1 15.6 %collective-permute-start.6 = (bf16[64,2048]{1,0:T(8,128)(2,1)S(1)}, bf16[64,2048]{1,0:T(8,128)(2,1)S(1)}, u32[]{:S(2)}, u32[]{:S(2)}) collective-permute-start(bf16[64,2048]{1,0:T(8,128)(2,1)S(1)} %pad_maximum_fusion), channel_id=1, source_target_pairs={{0,32},{32,64},{64,96},{96,0},{1,33},{33,65},{65,97},{97,1},{2,34}... | collective-permute-start | bytes 786440 | tf_op jit(solution)/shard_map/ppermute | solution.py:41
  150.3 14.7 %collective-permute-start.8 = (bf16[64,2048]{1,0:T(8,128)(2,1)S(1)}, bf16[64,2048]{1,0:T(8,128)(2,1)S(1)}, u32[]{:S(2)}, u32[]{:S(2)}) collective-permute-start(bf16[64,2048]{1,0:T(8,128)(2,1)S(1)} %pad_maximum_fusion), channel_id=1, source_target_pairs={{0,96},{32,0},{64,32},{96,64},{1,97},{33,1},{65,33},{97,65},{2,98}... | collective-permute-start | bytes 786440 | tf_op jit(solution)/shard_map/ppermute | solution.py:41
  153.4 11.3 %collective-permute-start.7 = (bf16[64,2048]{1,0:T(8,128)(2,1)S(1)}, bf16[64,2048]{1,0:T(8,128)(2,1)S(1)}, u32[]{:S(2)}, u32[]{:S(2)}) collective-permute-start(bf16[64,2048]{1,0:T(8,128)(2,1)S(1)} %pad_maximum_fusion), channel_id=1, source_target_pairs={{0,64},{32,96},{64,0},{96,32},{1,65},{33,97},{65,1},{97,33},{2,66}... | collective-permute-start | bytes 786440 | tf_op jit(solution)/shard_map/ppermute | solution.py:41
  166.3 16.9 %all-to-all-start.5 = ((bf16[16,8,2048]{2,1,0:T(8,128)(2,1)}), bf16[16,8,2048]{2,1,0:T(8,128)(2,1)}, u32[]{:S(2)}, u32[]{:S(2)}) async-start(bf16[16,8,2048]{2,1,0:T(8,128)(2,1)} %fusion.85), calls=%async_computation.5 | async-start | bytes 1048576 | tf_op jit(solution)/shard_map/all_to_all | solution.py:28
  183.2 30.3 %all-to-all-start.4 = ((bf16[64,8,1536]{2,1,0:T(8,128)(2,1)}), bf16[64,8,1536]{2,1,0:T(8,128)(2,1)}, u32[]{:S(2)}, u32[]{:S(2)}) async-start(bf16[64,8,1536]{2,1,0:T(8,128)(2,1)} %fusion.67), calls=%async_computation.4 | async-start | bytes 3145728 | tf_op jit(solution)/shard_map/all_to_all | solution.py:28

commit v2 on v1

v2 whole, which is shorter than its diff:
```python
import functools

import jax
import jax.numpy as jnp
from jax import lax
from jax.experimental import pallas as pl
from jax.experimental.pallas import tpu as pltpu
from jax.sharding import PartitionSpec as P


FAN1 = 25
FAN2 = 15
CSLOT = 2
BLOCK = 128
ALL = ("hst", "dev")
BF = jnp.bfloat16
F32 = jnp.float32


def parity_groups(hosts, devs):
    return [
        [h * devs + 2 * i + c for h in range(hosts) for i in range(devs // 2)] for c in range(2)
    ]


def exchange(x, axes, groups=None):
    return lax.all_to_all(
        x, axes, split_axis=0, concat_axis=0, tiled=True, axis_index_groups=groups
    )


def swap_pair(x, devs):
    return lax.ppermute(x, "dev", [(i, i ^ 1) for i in range(devs)])


def along_z(x, k, hosts):
    return lax.ppermute(x, "hst", [(i, (i + k) % hosts) for i in range(hosts)])


def call(body, outs, cost, *args, near=(), far=(), scratch=(), limit=8):
    space = pl.BlockSpec(memory_space=pltpu.VMEM)
    scalar = pl.BlockSpec(memory_space=pltpu.SMEM)
    away = pl.BlockSpec(memory_space=pl.ANY)
    flops, traffic = cost
    kinds = [scalar if x.ndim == 1 else away if i in far else space for i, x in enumerate(args)]
    args = [
        pltpu.with_memory_space_constraint(x, pltpu.VMEM) if i in near else x
        for i, x in enumerate(args)
    ]
    return pl.pallas_call(
        body,
        out_shape=outs,
        in_specs=kinds,
        out_specs=jax.tree.map(lambda _: space, outs),
        scratch_shapes=scratch,
        cost_estimate=pl.CostEstimate(flops=flops, transcendentals=0, bytes_accessed=traffic),
        compiler_params=pltpu.CompilerParams(vmem_limit_bytes=limit << 20),
    )(*args)


def product(a, b):
    return jnp.dot(a, b, preferred_element_type=F32)


def across(a, b):
    return lax.dot_general(a, b, (((0,), (0,)), ((), ())), preferred_element_type=F32)


def along(a, b):
    return lax.dot_general(a, b, (((1,), (1,)), ((), ())), preferred_element_type=F32)


def serve(asked_ref, stored_ref, got_ref, out_hbm, out_ref, sems, *, rows_dev, sub, tile):
    span = got_ref.shape[0] // 2
    half = got_ref.shape[1]
    block = span // CSLOT
    ones = jnp.ones((span, 128), BF)
    copies = []
    for t in range(stored_ref.shape[0] // tile):
        rows = slice(t * tile, (t + 1) * tile)
        row = asked_ref[:, rows] - rows_dev
        inner = row % block
        place = (inner // sub) * (CSLOT * sub) + (row // block) * sub + inner % sub
        place = jnp.where(row >= 0, place, -1)
        pick = (place == lax.broadcasted_iota(jnp.int32, (span, tile), 0)).astype(F32)
        pick = pick.astype(BF)
        hit = across(pick, ones) > 0.5
        for j in range(2):
            cached = across(pick, got_ref[j * span : (j + 1) * span, :])
            for i in range(half // 128):
                cols = slice(j * half + i * 128, j * half + (i + 1) * 128)
                stored = stored_ref[rows, cols].astype(F32)
                cell = jnp.where(hit, cached[:, i * 128 : (i + 1) * 128], stored)
                out_ref[rows, cols] = cell.astype(BF)
        copies.append(
            pltpu.make_async_copy(
                out_ref.at[pl.ds(t * tile, tile), :], out_hbm.at[pl.ds(t * tile, tile), :], sems.at[t]
            )
        )
        copies[-1].start()
    for copy in copies:
        copy.wait()


def serve_all(asked, stored, got, rows_dev, sub, tile):
    slots, width = stored.shape
    space = pl.BlockSpec(memory_space=pltpu.VMEM)
    return pl.pallas_call(
        functools.partial(serve, rows_dev=rows_dev, sub=sub, tile=tile),
        out_shape=pltpu.HBM((slots, width), BF),
        in_specs=[space] * 3,
        out_specs=pl.BlockSpec(memory_space=pltpu.HBM),
        scratch_shapes=[pltpu.VMEM((slots, width), BF), pltpu.SemaphoreType.DMA((slots // tile,))],
        cost_estimate=pl.CostEstimate(
            flops=slots * got.shape[0] * width, transcendentals=0, bytes_accessed=4 * slots * width
        ),
        compiler_params=pltpu.CompilerParams(vmem_limit_bytes=16 << 20),
    )(asked, pltpu.with_memory_space_constraint(stored, pltpu.VMEM), got)


def sort(host_ref, got_ref, *out_refs, sub):
    devs, _, half = got_ref.shape
    hosts = len(out_refs) - 1
    rows = devs * CSLOT * sub
    note = got_ref[:, CSLOT * sub :, :128].astype(F32)
    block = jnp.concatenate(
        [
            jnp.broadcast_to(note[:, :, 64 + j : 65 + j], (devs, sub, 128)).reshape(devs, 1, sub, 128)
            for j in range(CSLOT)
        ],
        1,
    ).reshape(rows, 128)
    inner = lax.broadcasted_iota(jnp.int32, (rows, 128), 0) % sub
    source = block.astype(jnp.int32) * sub + inner
    lane = lax.broadcasted_iota(jnp.int32, (rows, 128), 1)
    pick = jnp.concatenate(
        [(source == lane + i * 128).astype(F32) for i in range(rows // 128)], 1
    ).astype(BF)
    pieces = got_ref[:, : CSLOT * sub, :].reshape(rows, half)
    out_refs[0][...] = product(pick, pieces).astype(BF)
    for k in range(hosts):
        host = (host_ref[0] + k) % hosts
        line = lax.broadcasted_iota(jnp.int32, note.shape, 1)
        out_refs[1 + k][...] = jnp.sum(jnp.where(line == host, note, 0.0), 1).astype(BF)


def decode(host_ref, *refs, cap, top):
    parts, (asked_ref, stored_ref) = refs[:-2], refs[-2:]
    hosts = len(parts)
    devs = parts[0].shape[0]
    span = devs * cap
    lane = lax.broadcasted_iota(jnp.int32, (devs, span), 1)
    spread = (lane // cap == lax.broadcasted_iota(jnp.int32, (devs, span), 0)).astype(F32)
    spread = spread.astype(BF)
    line = lax.broadcasted_iota(jnp.int32, (128, span), 0)
    place = lax.broadcasted_iota(jnp.int32, (128, span), 1) % cap
    scale = jnp.where(line == place, 256.0, jnp.where(line == place + cap, 1.0, 0.0))
    rows = [
        jnp.sum(across(p[...], spread) * scale, 0, keepdims=True).astype(jnp.int32) for p in parts
    ]
    for j in range(hosts):
        turn = (host_ref[0] - j + hosts) % hosts
        row = jnp.zeros((1, span), jnp.int32)
        for k in range(hosts):
            row = jnp.where(turn == k, rows[k], row)
        asked_ref[:, j * span : (j + 1) * span] = row
        stored_ref[:, j * span : (j + 1) * span] = jnp.minimum(row, top)


def mark(near_ref, self_ref, hop_ref, count_ref, one_ref, many_ref, share_ref, used_ref,
         table_ref, *, tile, cap):
    nodes, slots = one_ref.shape
    peers = count_ref.shape[1]
    lane = lax.broadcasted_iota(jnp.int32, (peers, slots), 1)
    spread = lane // cap == lax.broadcasted_iota(jnp.int32, (peers, slots), 0)
    counts = jnp.broadcast_to(count_ref[...].astype(F32), (16, peers)).astype(BF)
    counts = product(counts, spread.astype(F32).astype(BF))
    rank = lax.broadcasted_iota(jnp.int32, counts.shape, 1) % cap
    used_ref[...] = (rank.astype(F32) < counts).astype(F32).astype(BF)

    hop = hop_ref[...]
    near = near_ref[...]
    near = jnp.where(lax.broadcasted_iota(jnp.int32, near.shape, 0) < hop, near, slots)
    rows = jnp.concatenate([near, self_ref[...]], 0)
    high = (rows // 256).astype(F32).astype(BF)
    low = (rows % 256).astype(F32).astype(BF)
    lines = rows.shape[0]
    turn = lax.broadcasted_iota(jnp.int32, (lines, 128), 0)
    turn = (turn == lax.broadcasted_iota(jnp.int32, (lines, 128), 1)).astype(F32).astype(BF)
    table_ref[...] = (256.0 * across(high, turn) + across(low, turn)).astype(jnp.int32)
    all_hop = jnp.broadcast_to(hop.astype(F32), (16, nodes)).astype(BF)
    first = lax.broadcasted_iota(jnp.int32, (16, 128), 0) == 0
    share_ref[...] = 1.0 / across(all_hop, first.astype(F32).astype(BF))
    kind = jnp.int16

    def step(i, carry):
        rows = pl.ds(i * tile, tile)
        table = table_ref[rows, :]
        named = [
            jnp.broadcast_to(table[:, k : k + 1], (tile, 128)).astype(kind)
            for k in range(FAN2 + 1)
        ]
        lane = lax.broadcasted_iota(jnp.int32, (tile, 128), 1)
        yes, no = jnp.ones((tile, 128), BF), jnp.zeros((tile, 128), BF)
        for j in range(slots // 128):
            cols = slice(j * 128, (j + 1) * 128)
            slot = (lane + j * 128).astype(kind)
            live = used_ref[:, cols]
            one_ref[rows, cols] = jnp.where(named[FAN2] == slot, yes, no) * live
            total = jnp.where(named[0] == slot, yes, no)
            for k in range(1, FAN2):
                total = total + jnp.where(named[k] == slot, yes, no)
            many_ref[rows, cols] = total * live
        return carry

    lax.fori_loop(0, nodes // tile, step, 0)


def ready(core_ref, self1_ref, nbr1_ref, order_ref, weight_ref, *, cols):
    width = self1_ref.shape[0]
    hidden = order_ref.shape[0]
    pos = lax.broadcasted_iota(jnp.int32, (1, hidden), 1)
    inner = pos % (hidden // 2)
    side = jnp.where(pos < hidden // 2, 1 - core_ref[0], core_ref[0])
    source = (inner // cols) * (2 * cols) + side * cols + inner % cols
    hot = source == lax.broadcasted_iota(jnp.int32, (hidden, hidden), 0)
    order_ref[...] = hot.astype(F32).astype(BF)
    weight_ref[:width, :] = product(self1_ref[...], order_ref[...]).astype(BF)
    weight_ref[width:, :] = product(nbr1_ref[...], order_ref[...]).astype(BF)


def spread_back(order_ref, self2_ref, nbr2_ref, col_ref, row_ref, cot_ref, *refs):
    others, (back_ref, turned_ref) = refs[:-2], refs[-2:]
    rows = jnp.concatenate([cot_ref[...]] + [r[...] for r in others], 0)
    turned_ref[...] = product(rows, order_ref[...]).astype(BF)
    seeds = cot_ref.shape[0]
    nodes = back_ref.shape[0]
    back_self = along(cot_ref[...], self2_ref[...])
    back_mean = along(cot_ref[...], nbr2_ref[...]) / col_ref[...].astype(F32)
    rest = jnp.concatenate([back_self, back_mean], 0)
    pieces = []
    for _ in range(3):
        piece = rest.astype(BF)
        rest = rest - piece.astype(F32)
        pieces.append(piece)
    lane = lax.broadcasted_iota(jnp.int32, (1, 6 * seeds), 1) % (2 * seeds)
    seed = lane % seeds
    first = jnp.where(lane < seeds, seed, seeds + seed * FAN1)
    last = jnp.where(lane < seeds, seed + 1, first + row_ref[...])
    node = lax.broadcasted_iota(jnp.int32, (nodes, 6 * seeds), 0)
    spread = ((node >= first) & (node < last)).astype(F32).astype(BF)
    pieces = product(jnp.concatenate(pieces, 0), order_ref[...]).astype(BF)
    back_ref[...] = product(spread, pieces)


def layer(host_ref, fetched_hbm, one_hbm, many_hbm, weight_hbm, back_hbm, order_hbm, share_ref, col_ref,
          rows_ref, grad_ref, pair_ref, part0_ref, part1_ref, part2_ref, part3_ref,
          fetched_ref, one_ref, many_ref, weight_ref, back_ref, order_ref, hid_ref, sems, *, tile):
    away = (fetched_hbm, one_hbm, many_hbm, weight_hbm, back_hbm, order_hbm)
    held = (fetched_ref, one_ref, many_ref, weight_ref, back_ref, order_ref)
    loads = [pltpu.make_async_copy(a, b, sems.at[i]) for i, (a, b) in enumerate(zip(away, held))]
    for load in loads:
        load.start()
    nodes = one_ref.shape[0]
    width = fetched_ref.shape[1]
    seeds = col_ref.shape[0]
    hidden = weight_ref.shape[1]
    loads[0].wait()
    loads[1].wait()
    for i in range(nodes // tile):
        rows = slice(i * tile, (i + 1) * tile)
        rows_ref[rows, :width] = product(one_ref[rows, :], fetched_ref[...]).astype(BF)
        if i == 0:
            loads[2].wait()
        total = product(many_ref[rows, :], fetched_ref[...])
        rows_ref[rows, width:] = (total * share_ref[rows, :1]).astype(BF)
        if i == 0:
            loads[3].wait()
            loads[4].wait()
        pre = product(rows_ref[rows, :], weight_ref[...])
        gate = 1.0 / (1.0 + jnp.exp(-pre))
        hid_ref[rows, :] = (pre * gate).astype(BF)
        grad_ref[rows, :] = (back_ref[rows, :] * gate * (1.0 + pre * (1.0 - gate))).astype(BF)
    loads[5].wait()
    node = lax.broadcasted_iota(jnp.int32, (seeds, nodes), 1)
    first = seeds + lax.broadcasted_iota(jnp.int32, (seeds, nodes), 0) * FAN1
    live = ((node >= first) & (node < first + col_ref[...])).astype(F32).astype(BF)
    mean = (product(live, hid_ref[...]) / col_ref[...].astype(F32)).astype(BF)
    pair_ref[:, :hidden] = along(hid_ref[:seeds, :], order_ref[...]).astype(BF)
    pair_ref[:, hidden:] = along(mean, order_ref[...]).astype(BF)
    parts = (part0_ref, part1_ref, part2_ref, part3_ref)
    slab = hidden // len(parts)
    for k in range(len(parts)):
        start = pl.multiple_of((host_ref[0] + k) % len(parts) * slab, slab)
        parts[k][:, :slab] = pair_ref[:, pl.ds(start, slab)]
        parts[k][:, slab:] = pair_ref[:, pl.ds(hidden + start, slab)]


def give_one(grad_ref, rows_ref, give_ref):
    hidden = grad_ref.shape[1]
    give_ref[...] = across(grad_ref[:, : hidden // 2], rows_ref[...]).astype(BF)


def give_two(cot_ref, *refs):
    parts, give_ref = refs[:-1], refs[-1]
    rows = jnp.concatenate([p[...] for p in parts], 0)
    give_ref[...] = across(cot_ref[:, : cot_ref.shape[1] // 2], rows).astype(BF)


def stay(grad_ref, rows_ref, taken_ref, cot_ref, taken2_ref, *refs):
    parts, out_ref = refs[:-1], refs[-1]
    half = grad_ref.shape[1] // 2
    wide = rows_ref.shape[1]
    kept = across(grad_ref[:, half:], rows_ref[...])
    out_ref[:, :wide] = (kept + taken_ref[...].astype(F32)).astype(BF)
    rows = jnp.concatenate([p[...] for p in parts], 0)
    kept = across(cot_ref[:, half:], rows)
    out_ref[:, wide:] = (kept + taken2_ref[...].astype(F32)).astype(BF)


def step(
    features, cache_blocks, plan, miss_ids, miss_counts, self_ids, nbr_ids, hop_counts,
    seed_counts, w_self1, w_nbr1, w_self2, w_nbr2, cotangent,
):
    hosts = lax.axis_size("hst")
    devs = lax.axis_size("dev")
    count = hosts * devs
    rows_dev, width = features.shape
    hidden = w_self2.shape[0]
    cap = miss_ids.shape[3]
    nodes = self_ids.shape[0]
    seeds = seed_counts.shape[0]
    h = lax.axis_index("hst")
    d = lax.axis_index("dev")
    core = d % 2
    half = width // 2
    groups = devs // 2
    sub = BLOCK // groups
    slots = count * cap
    cols = hidden // count
    shape = jax.ShapeDtypeStruct

    pieces = cache_blocks.reshape(CSLOT, groups, sub, 2, half).transpose(3, 1, 0, 2, 4)
    pieces = pieces.reshape(devs, CSLOT * sub, half)
    ids = miss_ids[0].transpose(1, 0, 2)
    ids = jnp.concatenate([ids // 256, ids % 256], 2)
    ids = jnp.pad(ids, ((0, 0), (0, 0), (0, half - 2 * cap)))
    own_plan = jnp.pad(plan[:, None, :], ((0, 0), (0, 0), (64, half - 64 - CSLOT)))
    ids = jnp.pad(ids, ((0, 0), (0, sub - hosts), (0, 0)))
    note = (ids + own_plan).astype(BF)
    got = exchange(jnp.concatenate([pieces, note], 1), "dev")

    cots = [cotangent] + [along_z(cotangent, k, hosts) for k in range(1, hosts)]
    got, cots = lax.optimization_barrier((got, cots))

    line = shape((devs, 128), BF)
    pieces, *parts = call(
        functools.partial(sort, sub=sub),
        (shape((devs * CSLOT * sub, half), BF),) + (line,) * hosts,
        (2 * devs * devs * CSLOT * CSLOT * sub * sub * half, 8 * devs * half),
        h[None], got,
    )
    for k in range(1, hosts):
        parts[k] = along_z(parts[k], k, hosts)
    pieces = exchange(pieces.reshape(devs, CSLOT * sub, half), "dev")
    moved = (
        pieces.reshape(2, groups, CSLOT, sub, half)
        .transpose(2, 1, 3, 0, 4)
        .reshape(CSLOT * BLOCK, width)
    )

    asked, kept = call(
        functools.partial(decode, cap=cap, top=rows_dev - 1),
        (shape((1, slots), jnp.int32), shape((1, slots), jnp.int32)),
        (slots * devs * 256, 64 * slots), h[None], *parts,
    )
    stored = features.at[kept.reshape(slots)].get(mode="promise_in_bounds")
    served = serve_all(
        asked, stored, pieces.reshape(2 * CSLOT * BLOCK, half), rows_dev, sub, 512
    )
    fetched = exchange(served.reshape(count, cap, width), ALL).reshape(slots, width)

    reordered, weight = call(
        functools.partial(ready, cols=cols),
        (pltpu.HBM((hidden, hidden), BF), pltpu.HBM((2 * width, hidden), BF)),
        (4 * width * hidden * hidden, 12 * hidden * hidden),
        core[None], w_self1, w_nbr1, limit=24,
    )
    one, many, share = call(
        functools.partial(mark, tile=16, cap=cap),
        (pltpu.HBM((nodes, slots), BF), pltpu.HBM((nodes, slots), BF), pltpu.HBM((nodes, 128), F32)),
        (nodes * slots * 48, 4 * nodes * slots),
        nbr_ids.T, self_ids[None], hop_counts[None], miss_counts.reshape(1, count), limit=24,
        scratch=[pltpu.VMEM((16, slots), BF), pltpu.VMEM((nodes, 128), jnp.int32)],
    )
    back, turned = call(
        spread_back,
        (pltpu.HBM((nodes, hidden), F32), pltpu.HBM((hosts * seeds, hidden), BF)),
        (8 * seeds * hidden * hidden, 12 * hidden * hidden),
        reordered, w_self2, w_nbr2, seed_counts[:, None], jnp.tile(seed_counts, 6)[None], *cots,
        limit=24,
    )

    held = (fetched, one, many, weight, back, reordered)
    part = shape((seeds, 2 * hidden // hosts), BF)
    rows_one, grad, both, *parts = call(
        functools.partial(layer, tile=nodes // 2),
        (
            pltpu.VMEM((nodes, 2 * width), BF), pltpu.VMEM((nodes, hidden), BF),
            shape((seeds, 2 * hidden), BF), part, part, part, part,
        ),
        (4 * nodes * slots * width, 8 * nodes * slots),
        h[None], *held, share, seed_counts[:, None],
        far=tuple(range(1, 1 + len(held))), limit=40,
        scratch=[pltpu.VMEM(x.shape, x.dtype) for x in held]
        + [pltpu.VMEM((nodes, hidden), BF), pltpu.SemaphoreType.DMA((len(held),))],
    )

    parts = parts[:1] + [along_z(parts[k], k, hosts) for k in range(1, hosts)]
    give = call(
        give_one, shape((hidden // 2, 2 * width), BF),
        (2 * nodes * hidden * width, 4 * hidden * width), grad, rows_one,
        near=(0, 1), limit=16,
    )
    taken = swap_pair(give, devs)
    give = call(
        give_two, shape((hidden // 2, 2 * hidden // hosts), BF),
        (4 * hidden * hidden * seeds, hidden * hidden), turned, *parts,
    )
    taken_two = swap_pair(give, devs)
    tall = 2 * width + 2 * hidden // hosts
    part = call(
        stay, shape((hidden // 2, tall), BF),
        (2 * nodes * hidden * width, 4 * hidden * width), grad, rows_one, taken, turned, taken_two,
        *parts, near=(0, 1), limit=24,
    )
    part = exchange(part.reshape(count // 2, cols, tall), ALL, parity_groups(hosts, devs))

    embedding = (product(both[:, :hidden], w_self2) + product(both[:, hidden:], w_nbr2)).astype(BF)
    sum_one = jnp.sum(part[:, :, : 2 * width].astype(F32), 0)
    sum_two = part[:, :, 2 * width :].reshape(hosts, groups, cols, 2, hidden // hosts)
    sum_two = jnp.sum(sum_two.astype(F32), 1).transpose(2, 1, 0, 3).reshape(2, cols, hidden)
    return (
        embedding,
        moved[None],
        sum_one[:, :width].T,
        sum_one[:, width:].T,
        sum_two[0].T,
        sum_two[1].T,
    )


def solution(mesh):
    return jax.shard_map(
        step,
        mesh=mesh,
        in_specs=(
            P(ALL, None), P("hst", "dev", None), P("hst", "dev"), P(ALL, None, None, None),
            P(ALL, None, None), P(ALL), P(ALL, None), P(ALL), P(ALL), P(), P(), P(), P(),
            P(ALL, None),
        ),
        out_specs=(
            P(ALL, None), P("hst", "dev", None), P(None, ALL), P(None, ALL), P(None, ALL),
            P(None, ALL),
        ),
        check_vma=False,
    )
```

time: 217 us -> 179 us (0.82)
  Pallas kernels: 0 us -> 47.4 us
  matrix products: 44.9 us -> 3.23 us
  waiting for transfers between devices: 58.4 us -> 42.2 us
  other arithmetic: 18.6 us -> 2.91 us
  starting transfers between devices: 50.6 us -> 44 us
  local copies, waits for them, and re-layouts: 41.9 us -> 37.5 us
    pallas_call x0 -> x10, Pallas kernels: none -> 47.4 us  [the longest x9 44.9 us: call(): pl.pallas_call(body, out_shape=outs, in_specs=kinds, out_specs=jax.tree.m...]
    dot_general x12 -> x2, matrix products: 44.9 us -> 3.23 us  [product(): return jnp.dot(a, b, preferred_element_type=F32)]
    ppermute x6 -> x9, waiting for transfers between devices: 23.7 us -> 4.72 us  [along_z(): return lax.ppermute(x, 'hst', [(i, (i + k) % hosts) for i in range(hosts)])]
    all_to_all x6 -> x4, starting transfers between devices: 41.4 us -> 26.8 us  [exchange(): lax.all_to_all(x, axes, split_axis=0, concat_axis=0, tiled=True, axis_ind...]
    unnamed x78 -> x71, local copies, waits for them, and re-layouts: 6.17 us -> 19.9 us
    ppermute x6 -> x9, starting transfers between devices: 8.78 us -> 17 us  [along_z(): return lax.ppermute(x, 'hst', [(i, (i + k) % hosts) for i in range(hosts)])]
    convert_element_type x5 -> x1, other arithmetic: 6.55 us -> 0.04 us  [step(): note = (ids + own_plan).astype(BF)]
    mul x2 -> x0, local copies, waits for them, and re-layouts: 6.16 us -> none  [local(): back_hop = back_mean[:, None, :] * seat.astype(F32)[:, :, None]]
  transfers between devices with their start and end apart: 15 -> 15, of which waited for: 8 -> 7; matrix products, arithmetic and copies ran while one was open for 43% -> 9% of each run, Pallas kernels for 0% -> 14%
where the time goes in v2:
time: 179 us; the launch traced here: 178 us
  Pallas kernels  47.4 us (26%)
  starting transfers between devices  44 us (25%)
  waiting for transfers between devices  42.2 us (24%)
  local copies, waits for them, and re-layouts  37.5 us (21%)
  matrix products  3.23 us (2%)
  other arithmetic  2.91 us (2%)
    pallas_call x9, Pallas kernels, call(): pl.pallas_call(body, out_shape=outs, in_specs=kinds, out_specs=jax.tree.m...  44.9 us
    all_to_all x4, waiting for transfers between devices, exchange(): lax.all_to_all(x, axes, split_axis=0, concat_axis=0, tiled=True, axis_ind...  35.6 us
    all_to_all x4, starting transfers between devices, exchange(): lax.all_to_all(x, axes, split_axis=0, concat_axis=0, tiled=True, axis_ind...  26.8 us
    unnamed x71, local copies, waits for them, and re-layouts  19.9 us
    ppermute x9, starting transfers between devices, along_z(): return lax.ppermute(x, 'hst', [(i, (i + k) % hosts) for i in range(hosts)])  17 us
    gather x1, local copies, waits for them, and re-layouts, step(): stored = features.at[kept.reshape(slots)].get(mode='promise_in_bounds')  9.43 us
    ppermute x9, waiting for transfers between devices, along_z(): return lax.ppermute(x, 'hst', [(i, (i + k) % hosts) for i in range(hosts)])  4.72 us
  transfers between devices with their start and end apart: 15, of which 7 were waited for; matrix products, arithmetic and copies ran while one was open for 9% of the time, Pallas kernels for 14%

profile of v2, /device:TPU:0, one launch (start us, length us, event | category | flops | bytes accessed | tf_op | source)
XLA Modules:
  0.0 178.3 jit_solution(1665599799964627205)
XLA Ops:
  0.7 0.9 pad_reduce_fusion
  1.6 0.9 copy.31
  2.6 1.0 copy.30
  3.8 0.9 pad_maximum_fusion
  4.7 7.5 %all-to-all-start = ((bf16[32,24,384]{2,1,0:T(8,128)(2,1)}), bf16[32,24,384]{2,1,0:T(8,128)(2,1)}, u32[]{:S(2)}, u32[]{:S(2)}) async-start(bf16[32,24,384]{2,1,0:T(8,128)(2,1)} %pad_maximum_fusion), calls=%async_computation | async-start | bytes 1179648 | tf_op jit(solution)/shard_map/all_to_all | solution.py:27
  12.3 4.0 %collective-permute-start.1 = (bf16[32,1024]{1,0:T(8,128)(2,1)S(1)}, bf16[32,1024]{1,0:T(8,128)(2,1)S(1)}, u32[]{:S(2)}, u32[]{:S(2)}) collective-permute-start(bf16[32,1024]{1,0:T(8,128)(2,1)S(1)} %copy-done.12), channel_id=1, source_target_pairs={{0,64},{32,96},{64,0},{96,32},{1,65},{33,97},{65,1},{97,33},{2,66}... | collective-permute-start | bytes 196616 | tf_op jit(solution)/shard_map/ppermute | solution.py:37
  16.2 1.0 collective-permute-start
  17.2 2.2 %collective-permute-start.2 = (bf16[32,1024]{1,0:T(8,128)(2,1)S(1)}, bf16[32,1024]{1,0:T(8,128)(2,1)S(1)}, u32[]{:S(2)}, u32[]{:S(2)}) collective-permute-start(bf16[32,1024]{1,0:T(8,128)(2,1)S(1)} %copy-done.12), channel_id=1, source_target_pairs={{0,96},{32,0},{64,32},{96,64},{1,97},{33,1},{65,33},{97,65},{2,98}... | collective-permute-start | bytes 196616 | tf_op jit(solution)/shard_map/ppermute | solution.py:37
  19.5 0.6 copy-done.14
  20.1 1.6 collective-permute-done.refs_0_
  21.7 0.6 copy-done.16
  22.3 0.6 copy-done.18
  23.0 1.6 all-to-all-done.got_ref
  24.6 2.2 %shard_map.181 = (bf16[512,384]{1,0:T(8,128)(2,1)S(1)}, bf16[32,128]{1,0:T(8,128)(2,1)S(1)}, bf16[32,128]{1,0:T(8,128)(2,1)}, bf16[32,128]{1,0:T(8,128)(2,1)}, bf16[32,128]{1,0:T(8,128)(2,1)S(1)}) custom-call(s32[1]{0:T(128)} %bitcast.host_ref, bf16[32,24,384]{2,1,0:T(8,128)(2,1)} %all-to-all-done.got_ref), custom_call_target="tpu_custom_call" | custom-call | flops 201326592 | bytes 98304 | tf_op jit(solution)/shard_map/pallas_call | solution.py:50
  26.8 0.7 copy-done.9
  27.5 0.6 copy-done.28
  28.1 1.9 %collective-permute-start.3 = (bf16[32,128]{1,0:T(8,128)(2,1)}, bf16[32,128]{1,0:T(8,128)(2,1)S(1)}, u32[]{:S(2)}, u32[]{:S(2)}) collective-permute-start(bf16[32,128]{1,0:T(8,128)(2,1)} %get-tuple-element.34), channel_id=1, source_target_pairs={{0,32},{32,64},{64,96},{96,0},{1,33},{33,65},{65,97},{97,1},{2,34}... | collective-permute-start | bytes 24584 | tf_op jit(solution)/shard_map/ppermute | solution.py:37
  30.1 3.6 %collective-permute-start.4 = (bf16[32,128]{1,0:T(8,128)(2,1)}, bf16[32,128]{1,0:T(8,128)(2,1)}, u32[]{:S(2)}, u32[]{:S(2)}) collective-permute-start(bf16[32,128]{1,0:T(8,128)(2,1)} %get-tuple-element.35), channel_id=1, source_target_pairs={{0,64},{32,96},{64,0},{96,32},{1,65},{33,97},{65,1},{97,33},{2,66}... | collective-permute-start | bytes 24584 | tf_op jit(solution)/shard_map/ppermute | solution.py:37
  33.6 1.0 collective-permute-start.5
  34.6 3.9 %all-to-all-start.1 = ((bf16[32,16,384]{2,1,0:T(8,128)(2,1)}), bf16[32,16,384]{2,1,0:T(8,128)(2,1)S(1)}, u32[]{:S(2)}, u32[]{:S(2)}) async-start(bf16[32,16,384]{2,1,0:T(8,128)(2,1)} %bitcast.63), calls=%async_computation.1 | async-start | bytes 786432 | tf_op jit(solution)/shard_map/all_to_all | solution.py:27
  38.6 0.7 copy-done.29
  39.3 1.1 shard_map.182
  40.4 9.4 %gather_fusion = bf16[2048,768]{1,0:T(8,128)(2,1)} fusion(bf16[2048,768]{1,0:T(8,128)(2,1)S(1)} %copy-done, s32[2048]{0:T(1024)S(1)} %broadcast_clamp_fusion), kind=kCustom, calls=%fused_computation | custom fusion | bytes 6299648 | tf_op jit(solution)/shard_map/gather | solution.py:377
  49.8 1.9 %copy-done.1 = bf16[2048,768]{1,0:T(8,128)(2,1)S(1)} copy-done((bf16[2048,768]{1,0:T(8,128)(2,1)S(1)}, bf16[2048,768]{1,0:T(8,128)(2,1)}, u32[]{:S(2)}) %copy-start.1) | copy-done | bytes 3145752
  51.7 2.5 %shard_map.183 = bf16[2048,768]{1,0:T(8,128)(2,1)} custom-call(s32[1,2048]{1,0:T(1,128)S(1)} %get-tuple-element.37.asked_ref, bf16[2048,768]{1,0:T(8,128)(2,1)S(1)} %copy-done.1, bf16[512,384]{1,0:T(8,128)(2,1)S(1)} %bitcast.61), custom_call_target="tpu_custom_call" | custom-call | flops 805306368 | bytes 6291456 | tf_op jit(solution)/shard_map/pallas_call | solution.py:108
  54.3 9.2 %all-to-all-start.2 = ((bf16[128,16,768]{2,1,0:T(8,128)(2,1)}), bf16[128,16,768]{2,1,0:T(8,128)(2,1)}, u32[]{:S(2)}, u32[]{:S(2)}) async-start(bf16[128,16,768]{2,1,0:T(8,128)(2,1)} %bitcast.65), calls=%async_computation.2 | async-start | bytes 6291456 | tf_op jit(solution)/shard_map/all_to_all | solution.py:27
  63.5 0.6 reshape.86.count_ref
  64.1 0.6 broadcast_in_dim.24.self_ref
  64.7 0.6 broadcast_in_dim.25.hop_ref
  65.3 0.6 broadcast_in_dim_tile.3.row_ref
  65.9 0.7 copy.32.col_ref
  66.7 0.7 copy-done.21
  67.3 0.7 copy-done.22
  68.0 0.7 copy-done.23
  68.7 0.8 copy-done.26
  69.5 13.2 %shard_map.184 = (bf16[832,2048]{1,0:T(8,128)(2,1)}, bf16[832,2048]{1,0:T(8,128)(2,1)}, f32[832,128]{1,0:T(8,128)}) custom-call(s32[15,832]{1,0:T(8,128)S(1)} %bitcast.64, s32[1,832]{1,0:T(1,128)S(1)} %copy-done.21, s32[1,832]{1,0:T(1,128)S(1)} %copy-done.22, s32[1,128]{1,0:T(1,128)S(1)} %copy-done.23), custom_call_target="tpu_custom_call" | custom-call | flops 81788928 | bytes 6815744 | tf_op jit(solution)/shard_map/pallas_call | solution.py:50
  82.7 1.4 copy-done.24
  84.1 1.4 copy-done.25
  85.6 5.1 %shard_map.185 = (bf16[1024,1024]{1,0:T(8,128)(2,1)}, bf16[1536,1024]{1,0:T(8,128)(2,1)}) custom-call(s32[1]{0:T(128)} %bitcast.15.core_ref, bf16[768,1024]{1,0:T(8,128)(2,1)S(1)} %copy-done.24, bf16[768,1024]{1,0:T(8,128)(2,1)S(1)} %copy-done.25), custom_call_target="tpu_custom_call" | custom-call | flops 3221225472 | bytes 12582912 | tf_op jit(solution)/shard_map/pallas_call | solution.py:50
  90.7 1.6 copy-done.6
  92.3 4.4 %shard_map.186 = (f32[832,1024]{1,0:T(8,128)}, bf16[128,1024]{1,0:T(8,128)(2,1)}) custom-call(bf16[1024,1024]{1,0:T(8,128)(2,1)S(1)} %copy-done.6, bf16[1024,1024]{1,0:T(8,128)(2,1)S(1)} %copy-done.2, bf16[1024,1024]{1,0:T(8,128)(2,1)S(1)} %copy-done.3, s32[32,1]{1,0:T(8,128)S(1)} %copy.32.col_ref, s32[1,192]{1,0:T(1,128)S(1)} %copy-done.20, ...), custom_call_target="tpu_custom_call" | custom-call | flops 268435456 | bytes 12582912 | tf_op jit(solution)/shard_map/pallas_call | solution.py:50
  96.7 7.8 %all-to-all-done.2 = bf16[128,16,768]{2,1,0:T(8,128)(2,1)} async-done(((bf16[128,16,768]{2,1,0:T(8,128)(2,1)}), bf16[128,16,768]{2,1,0:T(8,128)(2,1)}, u32[]{:S(2)}, u32[]{:S(2)}) %all-to-all-start.2) | async-done | bytes 3145760 | tf_op jit(solution)/shard_map/all_to_all | solution.py:27
  104.6 1.6 copy-done.7
  106.1 1.9 %copy-done.27 = bf16[1536,1024]{1,0:T(8,128)(2,1)S(1)} copy-done((bf16[1536,1024]{1,0:T(8,128)(2,1)S(1)}, bf16[1536,1024]{1,0:T(8,128)(2,1)}, u32[]{:S(2)}) %copy-start.27) | copy-done | bytes 3145752
  108.0 1.0 copy-done.30
  109.0 14.8 %shard_map.187 = (bf16[832,1536]{1,0:T(8,128)(2,1)S(1)}, bf16[832,1024]{1,0:T(8,128)(2,1)S(1)}, bf16[32,2048]{1,0:T(8,128)(2,1)S(1)}, bf16[32,512]{1,0:T(8,128)(...) custom-call(s32[1]{0:T(128)} %bitcast.host_ref, ...), custom_call_target="tpu_custom_call" | custom-call | flops 5234491392 | bytes 13631488 | tf_op jit(solution)/shard_map/pallas_call | solution.py:50
  123.9 1.8 %shard_map.188 = bf16[512,1536]{1,0:T(8,128)(2,1)S(1)} custom-call(bf16[832,1024]{1,0:T(8,128)(2,1)S(1)} %get-tuple-element.51.grad_ref, bf16[832,1536]{1,0:T(8,128)(2,1)S(1)} %get-tuple-element.52.rows_ref), custom_call_target="tpu_custom_call" | custom-call | flops 1308622848 | bytes 3145728 | tf_op jit(solution)/shard_map/pallas_call | solution.py:50
  126.0 1.9 %collective-permute-start.8 = (bf16[32,512]{1,0:T(8,128)(2,1)S(1)}, bf16[32,512]{1,0:T(8,128)(2,1)S(1)}, u32[]{:S(2)}, u32[]{:S(2)}) collective-permute-start(bf16[32,512]{1,0:T(8,128)(2,1)S(1)} %get-tuple-element.56), channel_id=1, source_target_pairs={{0,64},{32,96},{64,0},{96,32},{1,65},{33,97},{65,1},{97,33},{2,66}... | collective-permute-start | bytes 98312 | tf_op jit(solution)/shard_map/ppermute | solution.py:37
  127.9 1.2 collective-permute-start.9
  129.1 2.4 %collective-permute-done.7.refs_1_ = bf16[32,512]{1,0:T(8,128)(2,1)S(1)} collective-permute-done((bf16[32,512]{1,0:T(8,128)(2,1)S(1)}, bf16[32,512]{1,0:T(8,128)(2,1)S(1)}, u32[]{:S(2)}, u32[]{:S(2)}) %collective-permute-start.7) | collective-permute-done | bytes 32800 | tf_op jit(solution)/shard_map/ppermute | solution.py:37
  131.5 0.7 collective-permute-done.9.refs_3_
  132.2 0.3 shard_map.189
  132.6 1.9 %collective-permute-done.10.taken2_ref = bf16[512,512]{1,0:T(8,128)(2,1)S(1)} collective-permute-done((bf16[512,512]{1,0:T(8,128)(2,1)S(1)}, bf16[512,512]{1,0:T(8,128)(2,1)S(1)}, u32[]{:S(2)}, u32[]{:S(2)}) %collective-permute-start.10) | collective-permute-done | bytes 524320 | tf_op jit(solution)/shard_map/ppermute | solution.py:33
  134.5 2.0 %shard_map.190 = bf16[512,2048]{1,0:T(8,128)(2,1)S(1)} custom-call(bf16[832,1024]{1,0:T(8,128)(2,1)S(1)} %get-tuple-element.51.grad_ref, bf16[832,1536]{1,0:T(8,128)(2,1)S(1)} %get-tuple-element.52.rows_ref, bf16[512,1536]{1,0:T(8,128)(2,1)S(1)} %collective-permute-done.6.taken_ref, bf16[128,1024]{1,0:T(8,128)(2,1)S(1)} %copy-done.8, ...), custom_call_target="tpu_custom_call" | custom-call | flops 1308622848 | bytes 3145728 | tf_op jit(solution)/shard_map/pallas_call | solution.py:50
  136.5 1.4 copy-done.5
  137.9 6.2 %all-to-all-start.3 = ((bf16[64,8,2048]{2,1,0:T(8,128)(2,1)}), bf16[64,8,2048]{2,1,0:T(8,128)(2,1)}, u32[]{:S(2)}, u32[]{:S(2)}) async-start(bf16[64,8,2048]{2,1,0:T(8,128)(2,1)} %bitcast.60), calls=%async_computation.3 | async-start | bytes 4194304 | tf_op jit(solution)/shard_map/all_to_all | solution.py:27
  144.1 0.8 copy.34
  144.8 2.1 %fusion.4 = f32[32,1024]{1,0:T(8,128)S(1)} fusion(bf16[1024,1024]{1,0:T(8,128)(2,1)} %self2_ref.1, bf16[32,2048]{1,0:T(8,128)(2,1)} %copy-done.10), kind=kOutput, calls=%fused_computation.18 | convolution fusion | flops 67108864 | bytes 2293760 | tf_op jit(solution)/shard_map/dot_general | solution.py:62
  147.0 1.1 fusion
  148.1 26.2 %all-to-all-done.3 = bf16[64,8,2048]{2,1,0:T(8,128)(2,1)} async-done(((bf16[64,8,2048]{2,1,0:T(8,128)(2,1)}), bf16[64,8,2048]{2,1,0:T(8,128)(2,1)}, u32[]{:S(2)}, u32[]{:S(2)}) %all-to-all-start.3) | async-done | bytes 2097184 | tf_op jit(solution)/shard_map/all_to_all | solution.py:27
  174.3 1.1 slice.39
  175.4 0.6 fusion.7
  176.0 1.7 convert_reduce_fusion
  177.7 0.6 slice_bitcast_fusion
  (70 shorter events, 0.9 us)
Async XLA Ops:
  0.6 39.7 %copy-start = (bf16[2048,768]{1,0:T(8,128)(2,1)S(1)}, bf16[2048,768]{1,0:T(8,128)(2,1)}, u32[]{:S(2)}) copy-start(bf16[2048,768]{1,0:T(8,128)(2,1)} %param.14) | copy-start | bytes 9437188
  0.6 11.6 %copy-start.12 = (bf16[32,1024]{1,0:T(8,128)(2,1)S(1)}, bf16[32,1024]{1,0:T(8,128)(2,1)}, u32[]{:S(2)}) copy-start(bf16[32,1024]{1,0:T(8,128)(2,1)} %cot_ref) | copy-start | bytes 196612
  4.7 19.9 %all-to-all-start = ((bf16[32,24,384]{2,1,0:T(8,128)(2,1)}), bf16[32,24,384]{2,1,0:T(8,128)(2,1)}, u32[]{:S(2)}, u32[]{:S(2)}) async-start(bf16[32,24,384]{2,1,0:T(8,128)(2,1)} %pad_maximum_fusion), calls=%async_computation | async-start | bytes 1179648 | tf_op jit(solution)/shard_map/all_to_all | solution.py:27
  12.3 7.2 %collective-permute-start.1 = (bf16[32,1024]{1,0:T(8,128)(2,1)S(1)}, bf16[32,1024]{1,0:T(8,128)(2,1)S(1)}, u32[]{:S(2)}, u32[]{:S(2)}) collective-permute-start(bf16[32,1024]{1,0:T(8,128)(2,1)S(1)} %copy-done.12), channel_id=1, source_target_pairs={{0,64},{32,96},{64,0},{96,32},{1,65},{33,97},{65,1},{97,33},{2,66}... | collective-permute-start | bytes 196616 | tf_op jit(solution)/shard_map/ppermute | solution.py:37
  16.2 5.5 %collective-permute-start = (bf16[32,1024]{1,0:T(8,128)(2,1)S(1)}, bf16[32,1024]{1,0:T(8,128)(2,1)S(1)}, u32[]{:S(2)}, u32[]{:S(2)}) collective-permute-start(bf16[32,1024]{1,0:T(8,128)(2,1)S(1)} %copy-done.12), channel_id=1, source_target_pairs={{0,32},{32,64},{64,96},{96,0},{1,33},{33,65},{65,97},{97,1},{2,34}... | collective-permute-start | bytes 196616 | tf_op jit(solution)/shard_map/ppermute | solution.py:37
  17.2 5.1 %collective-permute-start.2 = (bf16[32,1024]{1,0:T(8,128)(2,1)S(1)}, bf16[32,1024]{1,0:T(8,128)(2,1)S(1)}, u32[]{:S(2)}, u32[]{:S(2)}) collective-permute-start(bf16[32,1024]{1,0:T(8,128)(2,1)S(1)} %copy-done.12), channel_id=1, source_target_pairs={{0,96},{32,0},{64,32},{96,64},{1,97},{33,1},{65,33},{97,65},{2,98}... | collective-permute-start | bytes 196616 | tf_op jit(solution)/shard_map/ppermute | solution.py:37
  19.5 0.6 copy-start.14
  21.7 0.6 copy-start.16
  22.3 0.6 copy-start.18
  26.8 0.7 copy-start.9
  27.5 0.6 copy-start.28
  28.1 10.4 %collective-permute-start.3 = (bf16[32,128]{1,0:T(8,128)(2,1)}, bf16[32,128]{1,0:T(8,128)(2,1)S(1)}, u32[]{:S(2)}, u32[]{:S(2)}) collective-permute-start(bf16[32,128]{1,0:T(8,128)(2,1)} %get-tuple-element.34), channel_id=1, source_target_pairs={{0,32},{32,64},{64,96},{96,0},{1,33},{33,65},{65,97},{97,1},{2,34}... | collective-permute-start | bytes 24584 | tf_op jit(solution)/shard_map/ppermute | solution.py:37
  30.1 8.5 %collective-permute-start.4 = (bf16[32,128]{1,0:T(8,128)(2,1)}, bf16[32,128]{1,0:T(8,128)(2,1)}, u32[]{:S(2)}, u32[]{:S(2)}) collective-permute-start(bf16[32,128]{1,0:T(8,128)(2,1)} %get-tuple-element.35), channel_id=1, source_target_pairs={{0,64},{32,96},{64,0},{96,32},{1,65},{33,97},{65,1},{97,33},{2,66}... | collective-permute-start | bytes 24584 | tf_op jit(solution)/shard_map/ppermute | solution.py:37
  33.6 4.9 %collective-permute-start.5 = (bf16[32,128]{1,0:T(8,128)(2,1)S(1)}, bf16[32,128]{1,0:T(8,128)(2,1)}, u32[]{:S(2)}, u32[]{:S(2)}) collective-permute-start(bf16[32,128]{1,0:T(8,128)(2,1)S(1)} %get-tuple-element.36), channel_id=1, source_target_pairs={{0,96},{32,0},{64,32},{96,64},{1,97},{33,1},{65,33},{97,65},{2,98}... | collective-permute-start | bytes 24584 | tf_op jit(solution)/shard_map/ppermute | solution.py:37
  34.6 15.2 %all-to-all-start.1 = ((bf16[32,16,384]{2,1,0:T(8,128)(2,1)}), bf16[32,16,384]{2,1,0:T(8,128)(2,1)S(1)}, u32[]{:S(2)}, u32[]{:S(2)}) async-start(bf16[32,16,384]{2,1,0:T(8,128)(2,1)} %bitcast.63), calls=%async_computation.1 | async-start | bytes 786432 | tf_op jit(solution)/shard_map/all_to_all | solution.py:27
  38.6 0.7 copy-start.29
  49.8 1.9 %copy-start.1 = (bf16[2048,768]{1,0:T(8,128)(2,1)S(1)}, bf16[2048,768]{1,0:T(8,128)(2,1)}, u32[]{:S(2)}) copy-start(bf16[2048,768]{1,0:T(8,128)(2,1)} %gather_fusion) | copy-start | bytes 9437188
  54.2 9.3 %copy-start.34 = (s32[1,4,32]{2,1,0:T(4,128)S(1)}, s32[1,4,32]{2,1,0:T(4,128)}, u32[]{:S(2)}) copy-start(s32[1,4,32]{2,1,0:T(4,128)} %param.18) | copy-start | bytes 1540
  54.2 9.9 %copy-start.31 = (s32[832]{0:T(1024)S(1)}, s32[832]{0:T(1024)}, u32[]{:S(2)}) copy-start(s32[832]{0:T(1024)} %param.19) | copy-start | bytes 9988
  54.3 10.4 %copy-start.32 = (s32[832]{0:T(1024)S(1)}, s32[832]{0:T(1024)}, u32[]{:S(2)}) copy-start(s32[832]{0:T(1024)} %param.21) | copy-start | bytes 9988
  54.3 11.0 %copy-start.33 = (s32[32]{0:T(128)S(1)}, s32[32]{0:T(128)}, u32[]{:S(2)}) copy-start(s32[32]{0:T(128)} %param.22) | copy-start | bytes 388
  54.3 50.3 %all-to-all-start.2 = ((bf16[128,16,768]{2,1,0:T(8,128)(2,1)}), bf16[128,16,768]{2,1,0:T(8,128)(2,1)}, u32[]{:S(2)}, u32[]{:S(2)}) async-start(bf16[128,16,768]{2,1,0:T(8,128)(2,1)} %bitcast.65), calls=%async_computation.2 | async-start | bytes 6291456 | tf_op jit(solution)/shard_map/all_to_all | solution.py:27
  66.7 0.7 copy-start.21
  67.3 0.7 copy-start.22
  68.0 0.7 copy-start.23
  68.7 0.8 copy-start.26
  82.7 1.4 copy-start.24
  84.1 1.4 copy-start.25
  85.5 5.1 %copy-start.2 = (bf16[1024,1024]{1,0:T(8,128)(2,1)S(1)}, bf16[1024,1024]{1,0:T(8,128)(2,1)}, u32[]{:S(2)}) copy-start(bf16[1024,1024]{1,0:T(8,128)(2,1)} %self2_ref.1) | copy-start | bytes 6291460
  85.5 5.1 %copy-start.3 = (bf16[1024,1024]{1,0:T(8,128)(2,1)S(1)}, bf16[1024,1024]{1,0:T(8,128)(2,1)}, u32[]{:S(2)}) copy-start(bf16[1024,1024]{1,0:T(8,128)(2,1)} %nbr2_ref.1) | copy-start | bytes 6291460
  85.5 5.1 %copy-start.13 = (bf16[32,1024]{1,0:T(8,128)(2,1)S(1)}, bf16[32,1024]{1,0:T(8,128)(2,1)}, u32[]{:S(2)}) copy-start(bf16[32,1024]{1,0:T(8,128)(2,1)} %cot_ref) | copy-start | bytes 196612
  85.5 5.1 %copy-start.15 = (bf16[32,1024]{1,0:T(8,128)(2,1)S(1)}, bf16[32,1024]{1,0:T(8,128)(2,1)}, u32[]{:S(2)}) copy-start(bf16[32,1024]{1,0:T(8,128)(2,1)} %copy-done.14) | copy-start | bytes 196612
  85.5 5.1 %copy-start.17 = (bf16[32,1024]{1,0:T(8,128)(2,1)S(1)}, bf16[32,1024]{1,0:T(8,128)(2,1)}, u32[]{:S(2)}) copy-start(bf16[32,1024]{1,0:T(8,128)(2,1)} %copy-done.16) | copy-start | bytes 196612
  85.5 5.1 %copy-start.19 = (bf16[32,1024]{1,0:T(8,128)(2,1)S(1)}, bf16[32,1024]{1,0:T(8,128)(2,1)}, u32[]{:S(2)}) copy-start(bf16[32,1024]{1,0:T(8,128)(2,1)} %copy-done.18) | copy-start | bytes 196612
  85.6 5.1 %copy-start.20 = (s32[1,192]{1,0:T(1,128)S(1)}, s32[1,192]{1,0:T(1,128)}, u32[]{:S(2)}) copy-start(s32[1,192]{1,0:T(1,128)} %broadcast_in_dim_tile.3.row_ref) | copy-start | bytes 2308
  90.7 1.6 copy-start.6
  104.5 1.6 copy-start.7
  106.1 1.9 %copy-start.27 = (bf16[1536,1024]{1,0:T(8,128)(2,1)S(1)}, bf16[1536,1024]{1,0:T(8,128)(2,1)}, u32[]{:S(2)}) copy-start(bf16[1536,1024]{1,0:T(8,128)(2,1)} %get-tuple-element.42.weight_hbm) | copy-start | bytes 9437188
  108.0 1.0 copy-start.30
  123.8 1.9 %copy-start.10 = (bf16[32,2048]{1,0:T(8,128)(2,1)}, bf16[32,2048]{1,0:T(8,128)(2,1)S(1)}, u32[]{:S(2)}) copy-start(bf16[32,2048]{1,0:T(8,128)(2,1)S(1)} %get-tuple-element.50) | copy-start | bytes 393220
  123.8 8.4 %copy-start.8 = (bf16[128,1024]{1,0:T(8,128)(2,1)S(1)}, bf16[128,1024]{1,0:T(8,128)(2,1)}, u32[]{:S(2)}) copy-start(bf16[128,1024]{1,0:T(8,128)(2,1)} %get-tuple-element.53.cot_ref) | copy-start | bytes 786436
  125.7 8.8 %collective-permute-start.6 = (bf16[512,1536]{1,0:T(8,128)(2,1)S(1)}, bf16[512,1536]{1,0:T(8,128)(2,1)S(1)}, u32[]{:S(2)}, u32[]{:S(2)}) collective-permute-start(bf16[512,1536]{1,0:T(8,128)(2,1)S(1)} %shard_map.188), channel_id=1, source_target_pairs={{0,1},{1,0},{2,3},{3,2},{4,5},{5,4},{6,7},{7,6},{8,9},{9,8},{10,11... | collective-permute-start | bytes 4718600 | tf_op jit(solution)/shard_map/ppermute | solution.py:33
  125.8 5.7 %collective-permute-start.7 = (bf16[32,512]{1,0:T(8,128)(2,1)S(1)}, bf16[32,512]{1,0:T(8,128)(2,1)S(1)}, u32[]{:S(2)}, u32[]{:S(2)}) collective-permute-start(bf16[32,512]{1,0:T(8,128)(2,1)S(1)} %get-tuple-element.55), channel_id=1, source_target_pairs={{0,32},{32,64},{64,96},{96,0},{1,33},{33,65},{65,97},{97,1},{2,34}... | collective-permute-start | bytes 98312 | tf_op jit(solution)/shard_map/ppermute | solution.py:37
  126.0 5.5 %collective-permute-start.8 = (bf16[32,512]{1,0:T(8,128)(2,1)S(1)}, bf16[32,512]{1,0:T(8,128)(2,1)S(1)}, u32[]{:S(2)}, u32[]{:S(2)}) collective-permute-start(bf16[32,512]{1,0:T(8,128)(2,1)S(1)} %get-tuple-element.56), channel_id=1, source_target_pairs={{0,64},{32,96},{64,0},{96,32},{1,65},{33,97},{65,1},{97,33},{2,66}... | collective-permute-start | bytes 98312 | tf_op jit(solution)/shard_map/ppermute | solution.py:37
  127.9 4.3 %collective-permute-start.9 = (bf16[32,512]{1,0:T(8,128)(2,1)S(1)}, bf16[32,512]{1,0:T(8,128)(2,1)S(1)}, u32[]{:S(2)}, u32[]{:S(2)}) collective-permute-start(bf16[32,512]{1,0:T(8,128)(2,1)S(1)} %get-tuple-element.57), channel_id=1, source_target_pairs={{0,96},{32,0},{64,32},{96,64},{1,97},{33,1},{65,33},{97,65},{2,98}... | collective-permute-start | bytes 98312 | tf_op jit(solution)/shard_map/ppermute | solution.py:37
  132.5 2.0 %collective-permute-start.10 = (bf16[512,512]{1,0:T(8,128)(2,1)S(1)}, bf16[512,512]{1,0:T(8,128)(2,1)S(1)}, u32[]{:S(2)}, u32[]{:S(2)}) collective-permute-start(bf16[512,512]{1,0:T(8,128)(2,1)S(1)} %shard_map.189), channel_id=1, source_target_pairs={{0,1},{1,0},{2,3},{3,2},{4,5},{5,4},{6,7},{7,6},{8,9},{9,8},{10,11... | collective-permute-start | bytes 1572872 | tf_op jit(solution)/shard_map/ppermute | solution.py:33
  136.5 1.4 copy-start.5
  137.9 36.4 %all-to-all-start.3 = ((bf16[64,8,2048]{2,1,0:T(8,128)(2,1)}), bf16[64,8,2048]{2,1,0:T(8,128)(2,1)}, u32[]{:S(2)}, u32[]{:S(2)}) async-start(bf16[64,8,2048]{2,1,0:T(8,128)(2,1)} %bitcast.60), calls=%async_computation.3 | async-start | bytes 4194304 | tf_op jit(solution)/shard_map/all_to_all | solution.py:27
  144.0 2.9 %copy-start.4 = (bf16[1024,1024]{1,0:T(8,128)(2,1)S(1)}, bf16[1024,1024]{1,0:T(8,128)(2,1)}, u32[]{:S(2)}) copy-start(bf16[1024,1024]{1,0:T(8,128)(2,1)} %nbr2_ref.1) | copy-start | bytes 6291460
  144.0 2.9 %copy-start.11 = (bf16[32,2048]{1,0:T(8,128)(2,1)S(1)}, bf16[32,2048]{1,0:T(8,128)(2,1)}, u32[]{:S(2)}) copy-start(bf16[32,2048]{1,0:T(8,128)(2,1)} %copy-done.10) | copy-start | bytes 393220

commit v3 on v2

--- a/solution.py
+++ b/solution.py
@@ -37,21 +37,34 @@
     return lax.ppermute(x, "hst", [(i, (i + k) % hosts) for i in range(hosts)])
 
 
+class Left:
+    def __init__(self, shape, kind):
+        self.ref = pltpu.HBM(shape, kind)
+
+
+def is_left(x):
+    return isinstance(x, Left)
+
+
 def call(body, outs, cost, *args, near=(), far=(), scratch=(), limit=8):
     space = pl.BlockSpec(memory_space=pltpu.VMEM)
     scalar = pl.BlockSpec(memory_space=pltpu.SMEM)
-    away = pl.BlockSpec(memory_space=pl.ANY)
+    away = pl.BlockSpec(memory_space=pltpu.HBM)
     flops, traffic = cost
     kinds = [scalar if x.ndim == 1 else away if i in far else space for i, x in enumerate(args)]
+    place = {**{i: pltpu.VMEM for i in near}, **{i: pltpu.HBM for i in far}}
     args = [
-        pltpu.with_memory_space_constraint(x, pltpu.VMEM) if i in near else x
+        pltpu.with_memory_space_constraint(x, place[i]) if i in place else x
         for i, x in enumerate(args)
     ]
+    left = [isinstance(x, Left) for x in jax.tree.leaves(outs, is_leaf=is_left)]
+    outs = jax.tree.map(lambda x: x.ref if is_left(x) else x, outs, is_leaf=is_left)
+    tree = jax.tree.structure(outs)
     return pl.pallas_call(
         body,
         out_shape=outs,
         in_specs=kinds,
-        out_specs=jax.tree.map(lambda _: space, outs),
+        out_specs=jax.tree.unflatten(tree, [away if x else space for x in left]),
         scratch_shapes=scratch,
         cost_estimate=pl.CostEstimate(flops=flops, transcendentals=0, bytes_accessed=traffic),
         compiler_params=pltpu.CompilerParams(vmem_limit_bytes=limit << 20),
@@ -70,13 +83,59 @@
     return lax.dot_general(a, b, (((1,), (1,)), ((), ())), preferred_element_type=F32)
 
 
-def serve(asked_ref, stored_ref, got_ref, out_hbm, out_ref, sems, *, rows_dev, sub, tile):
+def pack(plan_ref, ids_hbm, block_hbm, out_ref, ids_ref, block_ref, sems, *, sub):
+    devs, _, _ = out_ref.shape
+    groups = devs // 2
+    half = block_ref.shape[1] // 2
+    load_ids = pltpu.make_async_copy(ids_hbm, ids_ref, sems.at[0])
+    load_block = pltpu.make_async_copy(block_hbm, block_ref, sems.at[1])
+    load_ids.start()
+    load_block.start()
+    load_ids.wait()
+    hosts, cap, _ = ids_ref.shape
+    line = lax.broadcasted_iota(jnp.int32, (cap, 128), 0)
+    lane = lax.broadcasted_iota(jnp.int32, (cap, 128), 1)
+    to_high = (lane == line).astype(F32).astype(BF)
+    to_low = (lane == line + cap).astype(F32).astype(BF)
+    row = lax.broadcasted_iota(jnp.int32, (devs, sub, 128), 1)
+    lane = lax.broadcasted_iota(jnp.int32, (devs, sub, 128), 2)
+    note = jnp.zeros((devs, sub, 128), F32)
+    for k in range(hosts):
+        ids = ids_ref[k]
+        high = (ids // 256).astype(F32).astype(BF)
+        low = (ids % 256).astype(F32).astype(BF)
+        part = across(high, to_high) + across(low, to_low)
+        note = jnp.where(row == k, part[:, None, :], note)
+    for j in range(CSLOT):
+        note = jnp.where(lane == 64 + j, plan_ref[j].astype(F32), note)
+    out_ref[:, :, CSLOT * half :] = note.astype(BF)
+    load_block.wait()
+    block = block_ref[...].astype(F32).reshape(CSLOT, groups, sub, 2 * half)
+    for j in range(2):
+        for i in range(CSLOT):
+            piece = block[i, :, :, j * half : (j + 1) * half].astype(BF)
+            out_ref[j * groups : (j + 1) * groups, :, i * half : (i + 1) * half] = piece
+
+
+def serve(asked_ref, got_ref, stored_hbm, out_hbm, stored_ref, out_ref, in_sems, out_sems, *,
+          rows_dev, sub, tile):
+    steps = stored_ref.shape[0] // tile
     span = got_ref.shape[0] // 2
     half = got_ref.shape[1]
     block = span // CSLOT
     ones = jnp.ones((span, 128), BF)
-    copies = []
-    for t in range(stored_ref.shape[0] // tile):
+    chunks = [pl.ds(t * tile, tile) for t in range(steps)]
+    loads = [
+        pltpu.make_async_copy(stored_hbm.at[c, :], stored_ref.at[c, :], in_sems.at[t])
+        for t, c in enumerate(chunks)
+    ]
+    stores = [
+        pltpu.make_async_copy(out_ref.at[c, :], out_hbm.at[c, :], out_sems.at[t])
+        for t, c in enumerate(chunks)
+    ]
+    for load in loads:
+        load.start()
+    for t in range(steps):
         rows = slice(t * tile, (t + 1) * tile)
         row = asked_ref[:, rows] - rows_dev
         inner = row % block
@@ -85,44 +144,25 @@
         pick = (place == lax.broadcasted_iota(jnp.int32, (span, tile), 0)).astype(F32)
         pick = pick.astype(BF)
         hit = across(pick, ones) > 0.5
+        cached = [across(pick, got_ref[j * span : (j + 1) * span, :]) for j in range(2)]
+        loads[t].wait()
         for j in range(2):
-            cached = across(pick, got_ref[j * span : (j + 1) * span, :])
             for i in range(half // 128):
                 cols = slice(j * half + i * 128, j * half + (i + 1) * 128)
                 stored = stored_ref[rows, cols].astype(F32)
-                cell = jnp.where(hit, cached[:, i * 128 : (i + 1) * 128], stored)
+                cell = jnp.where(hit, cached[j][:, i * 128 : (i + 1) * 128], stored)
                 out_ref[rows, cols] = cell.astype(BF)
-        copies.append(
-            pltpu.make_async_copy(
-                out_ref.at[pl.ds(t * tile, tile), :], out_hbm.at[pl.ds(t * tile, tile), :], sems.at[t]
-            )
-        )
-        copies[-1].start()
-    for copy in copies:
-        copy.wait()
-
-
-def serve_all(asked, stored, got, rows_dev, sub, tile):
-    slots, width = stored.shape
-    space = pl.BlockSpec(memory_space=pltpu.VMEM)
-    return pl.pallas_call(
-        functools.partial(serve, rows_dev=rows_dev, sub=sub, tile=tile),
-        out_shape=pltpu.HBM((slots, width), BF),
-        in_specs=[space] * 3,
-        out_specs=pl.BlockSpec(memory_space=pltpu.HBM),
-        scratch_shapes=[pltpu.VMEM((slots, width), BF), pltpu.SemaphoreType.DMA((slots // tile,))],
-        cost_estimate=pl.CostEstimate(
-            flops=slots * got.shape[0] * width, transcendentals=0, bytes_accessed=4 * slots * width
-        ),
-        compiler_params=pltpu.CompilerParams(vmem_limit_bytes=16 << 20),
-    )(asked, pltpu.with_memory_space_constraint(stored, pltpu.VMEM), got)
-
-
-def sort(host_ref, got_ref, *out_refs, sub):
-    devs, _, half = got_ref.shape
-    hosts = len(out_refs) - 1
+        stores[t].start()
+    for store in stores:
+        store.wait()
+
+
+def sort(host_ref, got_ref, pieces_ref, *part_refs, sub):
+    devs, _, tall = got_ref.shape
+    hosts = len(part_refs)
+    half = (tall - 128) // CSLOT
     rows = devs * CSLOT * sub
-    note = got_ref[:, CSLOT * sub :, :128].astype(F32)
+    note = got_ref[:, :, CSLOT * half :].astype(F32)
     block = jnp.concatenate(
         [
             jnp.broadcast_to(note[:, :, 64 + j : 65 + j], (devs, sub, 128)).reshape(devs, 1, sub, 128)
@@ -130,18 +170,22 @@
         ],
         1,
     ).reshape(rows, 128)
+    block = block.astype(jnp.int32)
     inner = lax.broadcasted_iota(jnp.int32, (rows, 128), 0) % sub
-    source = block.astype(jnp.int32) * sub + inner
     lane = lax.broadcasted_iota(jnp.int32, (rows, 128), 1)
-    pick = jnp.concatenate(
-        [(source == lane + i * 128).astype(F32) for i in range(rows // 128)], 1
-    ).astype(BF)
-    pieces = got_ref[:, : CSLOT * sub, :].reshape(rows, half)
-    out_refs[0][...] = product(pick, pieces).astype(BF)
+    total = jnp.zeros((rows, half), F32)
+    for j in range(CSLOT):
+        source = jnp.where(block % CSLOT == j, block // CSLOT * sub + inner, -1)
+        pick = jnp.concatenate(
+            [(source == lane + i * 128).astype(F32) for i in range(devs * sub // 128)], 1
+        ).astype(BF)
+        piece = got_ref[:, :, j * half : (j + 1) * half].astype(F32).reshape(devs * sub, half)
+        total = total + product(pick, piece.astype(BF))
+    pieces_ref[...] = total.astype(BF)
+    line = lax.broadcasted_iota(jnp.int32, note.shape, 1)
     for k in range(hosts):
         host = (host_ref[0] + k) % hosts
-        line = lax.broadcasted_iota(jnp.int32, note.shape, 1)
-        out_refs[1 + k][...] = jnp.sum(jnp.where(line == host, note, 0.0), 1).astype(BF)
+        part_refs[k][...] = jnp.sum(jnp.where(line == host, note, 0.0), 1).astype(BF)
 
 
 def decode(host_ref, *refs, cap, top):
@@ -155,14 +199,15 @@
     line = lax.broadcasted_iota(jnp.int32, (128, span), 0)
     place = lax.broadcasted_iota(jnp.int32, (128, span), 1) % cap
     scale = jnp.where(line == place, 256.0, jnp.where(line == place + cap, 1.0, 0.0))
-    rows = [
-        jnp.sum(across(p[...], spread) * scale, 0, keepdims=True).astype(jnp.int32) for p in parts
-    ]
+    found = []
+    for part in parts:
+        ids = across(part[...], spread) * scale
+        found.append(jnp.sum(ids, 0, keepdims=True).astype(jnp.int32))
     for j in range(hosts):
         turn = (host_ref[0] - j + hosts) % hosts
-        row = jnp.zeros((1, span), jnp.int32)
-        for k in range(hosts):
-            row = jnp.where(turn == k, rows[k], row)
+        row = found[0]
+        for k in range(1, hosts):
+            row = jnp.where(turn == k, found[k], row)
         asked_ref[:, j * span : (j + 1) * span] = row
         stored_ref[:, j * span : (j + 1) * span] = jnp.minimum(row, top)
 
@@ -216,7 +261,7 @@
     lax.fori_loop(0, nodes // tile, step, 0)
 
 
-def ready(core_ref, self1_ref, nbr1_ref, order_ref, weight_ref, *, cols):
+def ready(core_ref, self1_ref, nbr1_ref, order_ref, natural_ref, weight_ref, *, cols):
     width = self1_ref.shape[0]
     hidden = order_ref.shape[0]
     pos = lax.broadcasted_iota(jnp.int32, (1, hidden), 1)
@@ -225,6 +270,10 @@
     source = (inner // cols) * (2 * cols) + side * cols + inner % cols
     hot = source == lax.broadcasted_iota(jnp.int32, (hidden, hidden), 0)
     order_ref[...] = hot.astype(F32).astype(BF)
+    block = pos // cols
+    place = jnp.where(block % 2 == core_ref[0], hidden // 2, 0) + block // 2 * cols + pos % cols
+    hot = place == lax.broadcasted_iota(jnp.int32, (hidden, hidden), 0)
+    natural_ref[...] = hot.astype(F32).astype(BF)
     weight_ref[:width, :] = product(self1_ref[...], order_ref[...]).astype(BF)
     weight_ref[width:, :] = product(nbr1_ref[...], order_ref[...]).astype(BF)
 
@@ -253,14 +302,14 @@
     back_ref[...] = product(spread, pieces)
 
 
-def layer(host_ref, fetched_hbm, one_hbm, many_hbm, weight_hbm, back_hbm, order_hbm, share_ref, col_ref,
+def layer(host_ref, fetched_hbm, one_hbm, many_hbm, weight_hbm, back_hbm, natural_hbm, share_hbm, col_ref,
           rows_ref, grad_ref, pair_ref, part0_ref, part1_ref, part2_ref, part3_ref,
-          fetched_ref, one_ref, many_ref, weight_ref, back_ref, order_ref, hid_ref, sems, *, tile):
-    away = (fetched_hbm, one_hbm, many_hbm, weight_hbm, back_hbm, order_hbm)
-    held = (fetched_ref, one_ref, many_ref, weight_ref, back_ref, order_ref)
+          fetched_ref, one_ref, many_ref, weight_ref, back_ref, natural_ref, share_ref, hid_ref, sems, *, tile):
+    away = (fetched_hbm, one_hbm, many_hbm, weight_hbm, back_hbm, natural_hbm, share_hbm)
+    held = (fetched_ref, one_ref, many_ref, weight_ref, back_ref, natural_ref, share_ref)
     loads = [pltpu.make_async_copy(a, b, sems.at[i]) for i, (a, b) in enumerate(zip(away, held))]
-    for load in loads:
-        load.start()
+    for i in (0, 1, 2, 6, 3, 4, 5):
+        loads[i].start()
     nodes = one_ref.shape[0]
     width = fetched_ref.shape[1]
     seeds = col_ref.shape[0]
@@ -272,6 +321,7 @@
         rows_ref[rows, :width] = product(one_ref[rows, :], fetched_ref[...]).astype(BF)
         if i == 0:
             loads[2].wait()
+            loads[6].wait()
         total = product(many_ref[rows, :], fetched_ref[...])
         rows_ref[rows, width:] = (total * share_ref[rows, :1]).astype(BF)
         if i == 0:
@@ -286,8 +336,9 @@
     first = seeds + lax.broadcasted_iota(jnp.int32, (seeds, nodes), 0) * FAN1
     live = ((node >= first) & (node < first + col_ref[...])).astype(F32).astype(BF)
     mean = (product(live, hid_ref[...]) / col_ref[...].astype(F32)).astype(BF)
-    pair_ref[:, :hidden] = along(hid_ref[:seeds, :], order_ref[...]).astype(BF)
-    pair_ref[:, hidden:] = along(mean, order_ref[...]).astype(BF)
+    both = product(jnp.concatenate([hid_ref[:seeds, :], mean], 0), natural_ref[...]).astype(BF)
+    pair_ref[:, :hidden] = both[:seeds, :]
+    pair_ref[:, hidden:] = both[seeds:, :]
     parts = (part0_ref, part1_ref, part2_ref, part3_ref)
     slab = hidden // len(parts)
     for k in range(len(parts)):
@@ -307,15 +358,54 @@
     give_ref[...] = across(cot_ref[:, : cot_ref.shape[1] // 2], rows).astype(BF)
 
 
-def stay(grad_ref, rows_ref, taken_ref, cot_ref, taken2_ref, *refs):
-    parts, out_ref = refs[:-1], refs[-1]
+def stay(grad_ref, rows_ref, taken_ref, cot_ref, taken2_ref, *refs, steps):
+    parts, (out_hbm, out_ref, sems) = refs[:-3], refs[-3:]
     half = grad_ref.shape[1] // 2
     wide = rows_ref.shape[1]
-    kept = across(grad_ref[:, half:], rows_ref[...])
-    out_ref[:, :wide] = (kept + taken_ref[...].astype(F32)).astype(BF)
     rows = jnp.concatenate([p[...] for p in parts], 0)
-    kept = across(cot_ref[:, half:], rows)
-    out_ref[:, wide:] = (kept + taken2_ref[...].astype(F32)).astype(BF)
+    tile = half // steps
+    stores = []
+    for t in range(steps):
+        cols = slice(half + t * tile, half + (t + 1) * tile)
+        chunk = slice(t * tile, (t + 1) * tile)
+        kept = across(grad_ref[:, cols], rows_ref[...])
+        out_ref[chunk, :wide] = (kept + taken_ref[chunk, :].astype(F32)).astype(BF)
+        kept = across(cot_ref[:, cols], rows)
+        out_ref[chunk, wide:] = (kept + taken2_ref[chunk, :].astype(F32)).astype(BF)
+        window = pl.ds(t * tile, tile)
+        stores.append(
+            pltpu.make_async_copy(out_ref.at[window, :], out_hbm.at[window, :], sems.at[t])
+        )
+        stores[-1].start()
+    for store in stores:
+        store.wait()
+
+
+def total(part_hbm, self1_ref, nbr1_ref, self2_ref, nbr2_ref, part_ref, sems, *, hosts):
+    sources = part_hbm.shape[0] // hosts
+    width = self1_ref.shape[1]
+    slab = self2_ref.shape[1] // hosts
+    loads = []
+    for i in range(hosts):
+        window = pl.ds(i * sources, sources)
+        loads.append(pltpu.make_async_copy(part_hbm.at[window], part_ref.at[window], sems.at[i]))
+        loads[-1].start()
+    for i in range(hosts):
+        loads[i].wait()
+        group = slice(i * sources, (i + 1) * sources)
+
+        def add(start, size):
+            return jnp.sum(part_ref[group, :, start : start + size].astype(F32), 0)
+
+        if i == 0:
+            self1_ref[...] = add(0, width)
+            nbr1_ref[...] = add(width, width)
+        else:
+            self1_ref[...] += add(0, width)
+            nbr1_ref[...] += add(width, width)
+        cols = slice(i * slab, (i + 1) * slab)
+        self2_ref[:, cols] = add(2 * width, slab)
+        nbr2_ref[:, cols] = add(2 * width + slab, slab)
 
 
 def step(
@@ -340,15 +430,16 @@
     cols = hidden // count
     shape = jax.ShapeDtypeStruct
 
-    pieces = cache_blocks.reshape(CSLOT, groups, sub, 2, half).transpose(3, 1, 0, 2, 4)
-    pieces = pieces.reshape(devs, CSLOT * sub, half)
-    ids = miss_ids[0].transpose(1, 0, 2)
-    ids = jnp.concatenate([ids // 256, ids % 256], 2)
-    ids = jnp.pad(ids, ((0, 0), (0, 0), (0, half - 2 * cap)))
-    own_plan = jnp.pad(plan[:, None, :], ((0, 0), (0, 0), (64, half - 64 - CSLOT)))
-    ids = jnp.pad(ids, ((0, 0), (0, sub - hosts), (0, 0)))
-    note = (ids + own_plan).astype(BF)
-    got = exchange(jnp.concatenate([pieces, note], 1), "dev")
+    tall = CSLOT * half + 128
+    ids, block = miss_ids[0].transpose(0, 2, 1), cache_blocks[0]
+    got = call(
+        functools.partial(pack, sub=sub), pltpu.HBM((devs, sub, tall), BF),
+        (16 * devs * sub * tall, 4 * devs * sub * tall), plan.reshape(CSLOT), ids, block,
+        far=(1, 2),
+        scratch=[pltpu.VMEM(x.shape, x.dtype) for x in (ids, block)]
+        + [pltpu.SemaphoreType.DMA((2,))],
+    )
+    got = exchange(got, "dev")
 
     cots = [cotangent] + [along_z(cotangent, k, hosts) for k in range(1, hosts)]
     got, cots = lax.optimization_barrier((got, cots))
@@ -356,12 +447,11 @@
     line = shape((devs, 128), BF)
     pieces, *parts = call(
         functools.partial(sort, sub=sub),
-        (shape((devs * CSLOT * sub, half), BF),) + (line,) * hosts,
+        (pltpu.HBM((devs * CSLOT * sub, half), BF),) + (line,) * hosts,
         (2 * devs * devs * CSLOT * CSLOT * sub * sub * half, 8 * devs * half),
         h[None], got,
     )
-    for k in range(1, hosts):
-        parts[k] = along_z(parts[k], k, hosts)
+    parts = parts[:1] + [along_z(parts[k], k, hosts) for k in range(1, hosts)]
     pieces = exchange(pieces.reshape(devs, CSLOT * sub, half), "dev")
     moved = (
         pieces.reshape(2, groups, CSLOT, sub, half)
@@ -369,20 +459,25 @@
         .reshape(CSLOT * BLOCK, width)
     )
 
+    line = shape((1, slots), jnp.int32)
     asked, kept = call(
-        functools.partial(decode, cap=cap, top=rows_dev - 1),
-        (shape((1, slots), jnp.int32), shape((1, slots), jnp.int32)),
+        functools.partial(decode, cap=cap, top=rows_dev - 1), (line, line),
         (slots * devs * 256, 64 * slots), h[None], *parts,
     )
     stored = features.at[kept.reshape(slots)].get(mode="promise_in_bounds")
-    served = serve_all(
-        asked, stored, pieces.reshape(2 * CSLOT * BLOCK, half), rows_dev, sub, 512
+    tile = 256
+    served = call(
+        functools.partial(serve, rows_dev=rows_dev, sub=sub, tile=tile),
+        Left((slots, width), BF), (4 * slots * CSLOT * BLOCK * width, 4 * slots * width),
+        asked, pieces.reshape(2 * CSLOT * BLOCK, half), stored, far=(2,), limit=16,
+        scratch=[pltpu.VMEM((slots, width), BF)] * 2
+        + [pltpu.SemaphoreType.DMA((slots // tile,))] * 2,
     )
     fetched = exchange(served.reshape(count, cap, width), ALL).reshape(slots, width)
 
-    reordered, weight = call(
+    reordered, natural, weight = call(
         functools.partial(ready, cols=cols),
-        (pltpu.HBM((hidden, hidden), BF), pltpu.HBM((2 * width, hidden), BF)),
+        (pltpu.HBM((hidden, hidden), BF), pltpu.HBM((hidden, hidden), BF), pltpu.HBM((2 * width, hidden), BF)),
         (4 * width * hidden * hidden, 12 * hidden * hidden),
         core[None], w_self1, w_nbr1, limit=24,
     )
@@ -401,7 +496,7 @@
         limit=24,
     )
 
-    held = (fetched, one, many, weight, back, reordered)
+    held = (fetched, one, many, weight, back, natural, share)
     part = shape((seeds, 2 * hidden // hosts), BF)
     rows_one, grad, both, *parts = call(
         functools.partial(layer, tile=nodes // 2),
@@ -410,7 +505,7 @@
             shape((seeds, 2 * hidden), BF), part, part, part, part,
         ),
         (4 * nodes * slots * width, 8 * nodes * slots),
-        h[None], *held, share, seed_counts[:, None],
+        h[None], *held, seed_counts[:, None],
         far=tuple(range(1, 1 + len(held))), limit=40,
         scratch=[pltpu.VMEM(x.shape, x.dtype) for x in held]
         + [pltpu.VMEM((nodes, hidden), BF), pltpu.SemaphoreType.DMA((len(held),))],
@@ -430,24 +525,21 @@
     taken_two = swap_pair(give, devs)
     tall = 2 * width + 2 * hidden // hosts
     part = call(
-        stay, shape((hidden // 2, tall), BF),
+        functools.partial(stay, steps=2), Left((hidden // 2, tall), BF),
         (2 * nodes * hidden * width, 4 * hidden * width), grad, rows_one, taken, turned, taken_two,
         *parts, near=(0, 1), limit=24,
+        scratch=[pltpu.VMEM((hidden // 2, tall), BF), pltpu.SemaphoreType.DMA((2,))],
     )
     part = exchange(part.reshape(count // 2, cols, tall), ALL, parity_groups(hosts, devs))
 
     embedding = (product(both[:, :hidden], w_self2) + product(both[:, hidden:], w_nbr2)).astype(BF)
-    sum_one = jnp.sum(part[:, :, : 2 * width].astype(F32), 0)
-    sum_two = part[:, :, 2 * width :].reshape(hosts, groups, cols, 2, hidden // hosts)
-    sum_two = jnp.sum(sum_two.astype(F32), 1).transpose(2, 1, 0, 3).reshape(2, cols, hidden)
-    return (
-        embedding,
-        moved[None],
-        sum_one[:, :width].T,
-        sum_one[:, width:].T,
-        sum_two[0].T,
-        sum_two[1].T,
-    )
+    narrow, broad = shape((cols, width), F32), shape((cols, hidden), F32)
+    sums = call(
+        functools.partial(total, hosts=hosts), (narrow, narrow, broad, broad),
+        (count * cols * tall, count * cols * tall), part, far=(0,), limit=16,
+        scratch=[pltpu.VMEM(part.shape, BF), pltpu.SemaphoreType.DMA((hosts,))],
+    )
+    return (embedding, moved[None]) + tuple(x.T for x in sums)
 
 
 def solution(mesh):

time: 179 us -> 171 us (0.955)
  local copies, waits for them, and re-layouts: 37.5 us -> 22.8 us
  Pallas kernels: 47.4 us -> 56.1 us
  other arithmetic: 2.91 us -> 0.02 us
    unnamed x71 -> x58, local copies, waits for them, and re-layouts: 19.9 us -> 9.46 us
    pallas_call x10 -> x12, Pallas kernels: 47.4 us -> 56.1 us  [call(): pl.pallas_call(body, out_shape=outs, in_specs=kinds, out_specs=jax.tree.u...]
  transfers between devices with their start and end apart: 15 -> 15, of which waited for: 7 -> 7; matrix products, arithmetic and copies ran while one was open for 9% -> 10% of each run, Pallas kernels for 14% -> 15%
where the time goes in v3:
time: 171 us; the launch traced here: 170 us
  Pallas kernels  56.1 us (33%)
  starting transfers between devices  44.8 us (26%)
  waiting for transfers between devices  41.5 us (24%)
  local copies, waits for them, and re-layouts  22.8 us (13%)
  matrix products  3.23 us (2%)
    pallas_call x12, Pallas kernels, call(): pl.pallas_call(body, out_shape=outs, in_specs=kinds, out_specs=jax.tree.u...  56.1 us
    all_to_all x4, waiting for transfers between devices, exchange(): lax.all_to_all(x, axes, split_axis=0, concat_axis=0, tiled=True, axis_ind...  34.7 us
    all_to_all x4, starting transfers between devices, exchange(): lax.all_to_all(x, axes, split_axis=0, concat_axis=0, tiled=True, axis_ind...  27.6 us
    ppermute x9, starting transfers between devices, along_z(): return lax.ppermute(x, 'hst', [(i, (i + k) % hosts) for i in range(hosts)])  17 us
    unnamed x58, local copies, waits for them, and re-layouts  9.46 us
    gather x1, local copies, waits for them, and re-layouts, step(): stored = features.at[kept.reshape(slots)].get(mode='promise_in_bounds')  9.43 us
    ppermute x9, waiting for transfers between devices, along_z(): return lax.ppermute(x, 'hst', [(i, (i + k) % hosts) for i in range(hosts)])  4.92 us
  transfers between devices with their start and end apart: 15, of which 7 were waited for; matrix products, arithmetic and copies ran while one was open for 10% of the time, Pallas kernels for 15%

profile of v3, /device:TPU:0, one launch (start us, length us, event | category | flops | bytes accessed | tf_op | source)
XLA Modules:
  0.0 169.6 jit_solution(10915941380414681455)
XLA Ops:
  0.6 0.0 copy-start
  0.7 0.8 copy-done.18
  1.5 2.4 %shard_map.181 = bf16[32,8,896]{2,1,0:T(8,128)(2,1)} custom-call(s32[2]{0:T(128)S(1)} %bitcast.29, s32[4,16,32]{2,1,0:T(8,128)} %bitcast.36, bf16[256,768]{1,0:T(8,128)(2,1)} %bitcast.33), custom_call_target="tpu_custom_call" | custom-call | flops 3670016 | bytes 917504 | tf_op jit(solution)/shard_map/pallas_call | solution.py:63
  3.9 7.6 %all-to-all-start = ((bf16[32,8,896]{2,1,0:T(8,128)(2,1)}), bf16[32,8,896]{2,1,0:T(8,128)(2,1)}, u32[]{:S(2)}, u32[]{:S(2)}) async-start(bf16[32,8,896]{2,1,0:T(8,128)(2,1)} %shard_map.181), calls=%async_computation | async-start | bytes 917504 | tf_op jit(solution)/shard_map/all_to_all | solution.py:27
  11.5 4.0 %collective-permute-start.1 = (bf16[32,1024]{1,0:T(8,128)(2,1)}, bf16[32,1024]{1,0:T(8,128)(2,1)S(1)}, u32[]{:S(2)}, u32[]{:S(2)}) collective-permute-start(bf16[32,1024]{1,0:T(8,128)(2,1)} %cot_ref), channel_id=1, source_target_pairs={{0,64},{32,96},{64,0},{96,32},{1,65},{33,97},{65,1},{97,33},{2,66}... | collective-permute-start | bytes 196616 | tf_op jit(solution)/shard_map/ppermute | solution.py:37
  15.4 1.0 collective-permute-start
  16.4 2.2 %collective-permute-start.2 = (bf16[32,1024]{1,0:T(8,128)(2,1)}, bf16[32,1024]{1,0:T(8,128)(2,1)S(1)}, u32[]{:S(2)}, u32[]{:S(2)}) collective-permute-start(bf16[32,1024]{1,0:T(8,128)(2,1)} %cot_ref), channel_id=1, source_target_pairs={{0,96},{32,0},{64,32},{96,64},{1,97},{33,1},{65,33},{97,65},{2,98}... | collective-permute-start | bytes 196616 | tf_op jit(solution)/shard_map/ppermute | solution.py:37
  18.7 0.6 copy-done.9
  19.3 1.8 %collective-permute-done.refs_0_ = bf16[32,1024]{1,0:T(8,128)(2,1)S(1)} collective-permute-done((bf16[32,1024]{1,0:T(8,128)(2,1)}, bf16[32,1024]{1,0:T(8,128)(2,1)S(1)}, u32[]{:S(2)}, u32[]{:S(2)}) %collective-permute-start) | collective-permute-done | bytes 65568 | tf_op jit(solution)/shard_map/ppermute | solution.py:37
  21.1 1.2 all-to-all-done.got_ref
  22.3 2.5 %shard_map.182 = (bf16[512,384]{1,0:T(8,128)(2,1)}, bf16[32,128]{1,0:T(8,128)(2,1)S(1)}, bf16[32,128]{1,0:T(8,128)(2,1)}, bf16[32,128]{1,0:T(8,128)(2,1)}, bf16[32,128]{1,0:T(8,128)(2,1)S(1)}) custom-call(s32[1]{0:T(128)} %bitcast.host_ref, bf16[32,8,896]{2,1,0:T(8,128)(2,1)} %all-to-all-done.got_ref), custom_call_target="tpu_custom_call" | custom-call | flops 201326592 | bytes 98304 | tf_op jit(solution)/shard_map/pallas_call | solution.py:63
  24.8 1.9 %collective-permute-start.3 = (bf16[32,128]{1,0:T(8,128)(2,1)}, bf16[32,128]{1,0:T(8,128)(2,1)S(1)}, u32[]{:S(2)}, u32[]{:S(2)}) collective-permute-start(bf16[32,128]{1,0:T(8,128)(2,1)} %get-tuple-element.39), channel_id=1, source_target_pairs={{0,32},{32,64},{64,96},{96,0},{1,33},{33,65},{65,97},{97,1},{2,34}... | collective-permute-start | bytes 24584 | tf_op jit(solution)/shard_map/ppermute | solution.py:37
  26.7 3.6 %collective-permute-start.4 = (bf16[32,128]{1,0:T(8,128)(2,1)}, bf16[32,128]{1,0:T(8,128)(2,1)}, u32[]{:S(2)}, u32[]{:S(2)}) collective-permute-start(bf16[32,128]{1,0:T(8,128)(2,1)} %get-tuple-element.40), channel_id=1, source_target_pairs={{0,64},{32,96},{64,0},{96,32},{1,65},{33,97},{65,1},{97,33},{2,66}... | collective-permute-start | bytes 24584 | tf_op jit(solution)/shard_map/ppermute | solution.py:37
  30.3 1.0 collective-permute-start.5
  31.3 4.3 %all-to-all-start.1 = ((bf16[32,16,384]{2,1,0:T(8,128)(2,1)}), bf16[32,16,384]{2,1,0:T(8,128)(2,1)S(1)}, u32[]{:S(2)}, u32[]{:S(2)}) async-start(bf16[32,16,384]{2,1,0:T(8,128)(2,1)} %bitcast.34), calls=%async_computation.1 | async-start | bytes 786432 | tf_op jit(solution)/shard_map/all_to_all | solution.py:27
  35.7 0.0 copy-start.24
  35.7 0.7 copy-done.24
  36.4 1.1 shard_map.183
  37.5 9.4 %gather_fusion = bf16[2048,768]{1,0:T(8,128)(2,1)} fusion(bf16[2048,768]{1,0:T(8,128)(2,1)S(1)} %copy-done, s32[2048]{0:T(1024)S(1)} %broadcast_clamp_fusion), kind=kCustom, calls=%fused_computation | custom fusion | bytes 6299648 | tf_op jit(solution)/shard_map/gather | solution.py:467
  46.9 5.2 %shard_map.184 = bf16[2048,768]{1,0:T(8,128)(2,1)} custom-call(s32[1,2048]{1,0:T(1,128)S(1)} %get-tuple-element.42.asked_ref, bf16[512,384]{1,0:T(8,128)(2,1)S(1)} %bitcast.27, bf16[2048,768]{1,0:T(8,128)(2,1)} %gather_fusion), custom_call_target="tpu_custom_call" | custom-call | flops 1610612736 | bytes 6291456 | tf_op jit(solution)/shard_map/pallas_call | solution.py:63
  52.1 0.0 copy-start.28
  52.2 0.0 copy-start.25
  52.2 0.0 copy-start.26
  52.2 0.0 copy-start.27
  52.2 9.6 %all-to-all-start.2 = ((bf16[128,16,768]{2,1,0:T(8,128)(2,1)}), bf16[128,16,768]{2,1,0:T(8,128)(2,1)}, u32[]{:S(2)}, u32[]{:S(2)}) async-start(bf16[128,16,768]{2,1,0:T(8,128)(2,1)} %bitcast.31), calls=%async_computation.2 | async-start | bytes 6291456 | tf_op jit(solution)/shard_map/all_to_all | solution.py:27
  61.8 0.6 reshape.74.count_ref
  62.4 0.6 broadcast_in_dim.20.self_ref
  63.0 0.6 broadcast_in_dim.21.hop_ref
  63.5 0.6 broadcast_in_dim_tile.3.row_ref
  64.2 0.7 copy.23.col_ref
  64.9 0.7 copy-done.16
  65.6 0.7 copy-done.17
  66.3 0.7 copy-done.19
  67.0 0.8 copy-done.22
  67.8 13.2 %shard_map.185 = (bf16[832,2048]{1,0:T(8,128)(2,1)}, bf16[832,2048]{1,0:T(8,128)(2,1)}, f32[832,128]{1,0:T(8,128)}) custom-call(s32[15,832]{1,0:T(8,128)S(1)} %bitcast.30, s32[1,832]{1,0:T(1,128)S(1)} %copy-done.16, s32[1,832]{1,0:T(1,128)S(1)} %copy-done.17, s32[1,128]{1,0:T(1,128)S(1)} %copy-done.19), custom_call_target="tpu_custom_call" | custom-call | flops 81788928 | bytes 6815744 | tf_op jit(solution)/shard_map/pallas_call | solution.py:63
  81.0 1.4 copy-done.20
  82.4 1.4 copy-done.21
  83.8 0.0 copy-start.12
  83.8 0.0 copy-start.15
  83.8 5.8 %shard_map.186 = (bf16[1024,1024]{1,0:T(8,128)(2,1)}, bf16[1024,1024]{1,0:T(8,128)(2,1)}, bf16[1536,1024]{1,0:T(8,128)(2,1)}) custom-call(s32[1]{0:T(128)} %bitcast.12.core_ref, bf16[768,1024]{1,0:T(8,128)(2,1)S(1)} %copy-done.20, bf16[768,1024]{1,0:T(8,128)(2,1)S(1)} %copy-done.21), custom_call_target="tpu_custom_call" | custom-call | flops 3221225472 | bytes 12582912 | tf_op jit(solution)/shard_map/pallas_call | solution.py:63
  89.7 1.6 copy-done.4
  91.3 4.4 %shard_map.187 = (f32[832,1024]{1,0:T(8,128)}, bf16[128,1024]{1,0:T(8,128)(2,1)}) custom-call(bf16[1024,1024]{1,0:T(8,128)(2,1)S(1)} %copy-done.4, bf16[1024,1024]{1,0:T(8,128)(2,1)S(1)} %copy-done.1, bf16[1024,1024]{1,0:T(8,128)(2,1)S(1)} %copy-done.2, s32[32,1]{1,0:T(8,128)S(1)} %copy.23.col_ref, s32[1,192]{1,0:T(1,128)S(1)} %copy-done.15, ...), custom_call_target="tpu_custom_call" | custom-call | flops 268435456 | bytes 12582912 | tf_op jit(solution)/shard_map/pallas_call | solution.py:63
  95.7 7.3 %all-to-all-done.2 = bf16[128,16,768]{2,1,0:T(8,128)(2,1)} async-done(((bf16[128,16,768]{2,1,0:T(8,128)(2,1)}), bf16[128,16,768]{2,1,0:T(8,128)(2,1)}, u32[]{:S(2)}, u32[]{:S(2)}) %all-to-all-start.2) | async-done | bytes 3145760 | tf_op jit(solution)/shard_map/all_to_all | solution.py:27
  103.0 14.2 %shard_map.188 = (bf16[832,1536]{1,0:T(8,128)(2,1)S(1)}, bf16[832,1024]{1,0:T(8,128)(2,1)S(1)}, bf16[32,2048]{1,0:T(8,128)(2,1)S(1)}, bf16[32,512]{1,0:T(8,128)(...) custom-call(s32[1]{0:T(128)} %bitcast.host_ref, ...), custom_call_target="tpu_custom_call" | custom-call | flops 5234491392 | bytes 13631488 | tf_op jit(solution)/shard_map/pallas_call | solution.py:63
  117.2 0.0 copy-start.5
  117.2 1.8 %shard_map.189 = bf16[512,1536]{1,0:T(8,128)(2,1)S(1)} custom-call(bf16[832,1024]{1,0:T(8,128)(2,1)S(1)} %get-tuple-element.57.grad_ref, bf16[832,1536]{1,0:T(8,128)(2,1)S(1)} %get-tuple-element.58.rows_ref), custom_call_target="tpu_custom_call" | custom-call | flops 1308622848 | bytes 3145728 | tf_op jit(solution)/shard_map/pallas_call | solution.py:63
  119.0 0.1 collective-permute-start.6
  119.1 0.2 collective-permute-start.7
  119.3 1.9 %collective-permute-start.8 = (bf16[32,512]{1,0:T(8,128)(2,1)S(1)}, bf16[32,512]{1,0:T(8,128)(2,1)S(1)}, u32[]{:S(2)}, u32[]{:S(2)}) collective-permute-start(bf16[32,512]{1,0:T(8,128)(2,1)S(1)} %get-tuple-element.62), channel_id=1, source_target_pairs={{0,64},{32,96},{64,0},{96,32},{1,65},{33,97},{65,1},{97,33},{2,66}... | collective-permute-start | bytes 98312 | tf_op jit(solution)/shard_map/ppermute | solution.py:37
  121.2 1.2 collective-permute-start.9
  122.4 2.4 %collective-permute-done.7.refs_1_ = bf16[32,512]{1,0:T(8,128)(2,1)S(1)} collective-permute-done((bf16[32,512]{1,0:T(8,128)(2,1)S(1)}, bf16[32,512]{1,0:T(8,128)(2,1)S(1)}, u32[]{:S(2)}, u32[]{:S(2)}) %collective-permute-start.7) | collective-permute-done | bytes 32800 | tf_op jit(solution)/shard_map/ppermute | solution.py:37
  124.8 0.7 collective-permute-done.9.refs_3_
  125.5 0.3 shard_map.190
  125.8 0.1 collective-permute-start.10
  125.9 1.9 %collective-permute-done.10.taken2_ref = bf16[512,512]{1,0:T(8,128)(2,1)S(1)} collective-permute-done((bf16[512,512]{1,0:T(8,128)(2,1)S(1)}, bf16[512,512]{1,0:T(8,128)(2,1)S(1)}, u32[]{:S(2)}, u32[]{:S(2)}) %collective-permute-start.10) | collective-permute-done | bytes 524320 | tf_op jit(solution)/shard_map/ppermute | solution.py:33
  127.8 3.0 %shard_map.191 = bf16[512,2048]{1,0:T(8,128)(2,1)} custom-call(bf16[832,1024]{1,0:T(8,128)(2,1)S(1)} %get-tuple-element.57.grad_ref, bf16[832,1536]{1,0:T(8,128)(2,1)S(1)} %get-tuple-element.58.rows_ref, bf16[512,1536]{1,0:T(8,128)(2,1)S(1)} %collective-permute-done.6.taken_ref, bf16[128,1024]{1,0:T(8,128)(2,1)S(1)} %copy-done.5, ...), custom_call_target="tpu_custom_call" | custom-call | flops 1308622848 | bytes 3145728 | tf_op jit(solution)/shard_map/pallas_call | solution.py:63
  130.8 6.2 %all-to-all-start.3 = ((bf16[64,8,2048]{2,1,0:T(8,128)(2,1)}), bf16[64,8,2048]{2,1,0:T(8,128)(2,1)}, u32[]{:S(2)}, u32[]{:S(2)}) async-start(bf16[64,8,2048]{2,1,0:T(8,128)(2,1)} %bitcast.32), calls=%async_computation.3 | async-start | bytes 4194304 | tf_op jit(solution)/shard_map/all_to_all | solution.py:27
  137.0 0.0 copy-start.3
  137.0 0.8 copy.25
  137.8 2.1 %fusion.2 = f32[32,1024]{1,0:T(8,128)S(1)} fusion(bf16[1024,1024]{1,0:T(8,128)(2,1)} %self2_ref.1, bf16[32,2048]{1,0:T(8,128)(2,1)} %copy-done.6), kind=kOutput, calls=%fused_computation.4 | convolution fusion | flops 67108864 | bytes 2293760 | tf_op jit(solution)/shard_map/dot_general | solution.py:75
  139.9 0.0 copy-done.3
  139.9 1.1 fusion
  141.1 26.2 %all-to-all-done.3.part_hbm = bf16[64,8,2048]{2,1,0:T(8,128)(2,1)} async-done(((bf16[64,8,2048]{2,1,0:T(8,128)(2,1)}), bf16[64,8,2048]{2,1,0:T(8,128)(2,1)}, u32[]{:S(2)}, u32[]{:S(2)}) %all-to-all-start.3) | async-done | bytes 2097184 | tf_op jit(solution)/shard_map/all_to_all | solution.py:27
  167.2 2.2 %shard_map.192 = (f32[8,768]{1,0:T(8,128)}, f32[8,768]{1,0:T(8,128)}, f32[8,1024]{1,0:T(8,128)}, f32[8,1024]{1,0:T(8,128)}) custom-call(bf16[64,8,2048]{2,1,0:T(8,128)(2,1)} %all-to-all-done.3.part_hbm), custom_call_target="tpu_custom_call" | custom-call | flops 2097152 | bytes 2097152 | tf_op jit(solution)/shard_map/pallas_call | solution.py:63
  (48 shorter events, 0.1 us)
Async XLA Ops:
  0.6 36.9 %copy-start = (bf16[2048,768]{1,0:T(8,128)(2,1)S(1)}, bf16[2048,768]{1,0:T(8,128)(2,1)}, u32[]{:S(2)}) copy-start(bf16[2048,768]{1,0:T(8,128)(2,1)} %param.14) | copy-start | bytes 9437188
  0.6 0.8 copy-start.18
  3.9 18.4 %all-to-all-start = ((bf16[32,8,896]{2,1,0:T(8,128)(2,1)}), bf16[32,8,896]{2,1,0:T(8,128)(2,1)}, u32[]{:S(2)}, u32[]{:S(2)}) async-start(bf16[32,8,896]{2,1,0:T(8,128)(2,1)} %shard_map.181), calls=%async_computation | async-start | bytes 917504 | tf_op jit(solution)/shard_map/all_to_all | solution.py:27
  11.5 7.2 %collective-permute-start.1 = (bf16[32,1024]{1,0:T(8,128)(2,1)}, bf16[32,1024]{1,0:T(8,128)(2,1)S(1)}, u32[]{:S(2)}, u32[]{:S(2)}) collective-permute-start(bf16[32,1024]{1,0:T(8,128)(2,1)} %cot_ref), channel_id=1, source_target_pairs={{0,64},{32,96},{64,0},{96,32},{1,65},{33,97},{65,1},{97,33},{2,66}... | collective-permute-start | bytes 196616 | tf_op jit(solution)/shard_map/ppermute | solution.py:37
  15.4 5.7 %collective-permute-start = (bf16[32,1024]{1,0:T(8,128)(2,1)}, bf16[32,1024]{1,0:T(8,128)(2,1)S(1)}, u32[]{:S(2)}, u32[]{:S(2)}) collective-permute-start(bf16[32,1024]{1,0:T(8,128)(2,1)} %cot_ref), channel_id=1, source_target_pairs={{0,32},{32,64},{64,96},{96,0},{1,33},{33,65},{65,97},{97,1},{2,34}... | collective-permute-start | bytes 196616 | tf_op jit(solution)/shard_map/ppermute | solution.py:37
  16.4 4.7 %collective-permute-start.2 = (bf16[32,1024]{1,0:T(8,128)(2,1)}, bf16[32,1024]{1,0:T(8,128)(2,1)S(1)}, u32[]{:S(2)}, u32[]{:S(2)}) collective-permute-start(bf16[32,1024]{1,0:T(8,128)(2,1)} %cot_ref), channel_id=1, source_target_pairs={{0,96},{32,0},{64,32},{96,64},{1,97},{33,1},{65,33},{97,65},{2,98}... | collective-permute-start | bytes 196616 | tf_op jit(solution)/shard_map/ppermute | solution.py:37
  18.7 0.6 copy-start.9
  21.1 10.2 %copy-start.11 = (bf16[32,1024]{1,0:T(8,128)(2,1)}, bf16[32,1024]{1,0:T(8,128)(2,1)S(1)}, u32[]{:S(2)}) copy-start(bf16[32,1024]{1,0:T(8,128)(2,1)S(1)} %collective-permute-done.refs_0_) | copy-start | bytes 196612
  21.1 10.2 %copy-start.13 = (bf16[32,1024]{1,0:T(8,128)(2,1)}, bf16[32,1024]{1,0:T(8,128)(2,1)S(1)}, u32[]{:S(2)}) copy-start(bf16[32,1024]{1,0:T(8,128)(2,1)S(1)} %collective-permute-done.2.refs_2_) | copy-start | bytes 196612
  24.8 6.5 %copy-start.23 = (bf16[32,128]{1,0:T(8,128)(2,1)}, bf16[32,128]{1,0:T(8,128)(2,1)S(1)}, u32[]{:S(2)}) copy-start(bf16[32,128]{1,0:T(8,128)(2,1)S(1)} %get-tuple-element.38.refs_0_) | copy-start | bytes 24580
  24.8 10.9 %collective-permute-start.3 = (bf16[32,128]{1,0:T(8,128)(2,1)}, bf16[32,128]{1,0:T(8,128)(2,1)S(1)}, u32[]{:S(2)}, u32[]{:S(2)}) collective-permute-start(bf16[32,128]{1,0:T(8,128)(2,1)} %get-tuple-element.39), channel_id=1, source_target_pairs={{0,32},{32,64},{64,96},{96,0},{1,33},{33,65},{65,97},{97,1},{2,34}... | collective-permute-start | bytes 24584 | tf_op jit(solution)/shard_map/ppermute | solution.py:37
  26.7 8.9 %collective-permute-start.4 = (bf16[32,128]{1,0:T(8,128)(2,1)}, bf16[32,128]{1,0:T(8,128)(2,1)}, u32[]{:S(2)}, u32[]{:S(2)}) collective-permute-start(bf16[32,128]{1,0:T(8,128)(2,1)} %get-tuple-element.40), channel_id=1, source_target_pairs={{0,64},{32,96},{64,0},{96,32},{1,65},{33,97},{65,1},{97,33},{2,66}... | collective-permute-start | bytes 24584 | tf_op jit(solution)/shard_map/ppermute | solution.py:37
  30.3 5.4 %collective-permute-start.5 = (bf16[32,128]{1,0:T(8,128)(2,1)S(1)}, bf16[32,128]{1,0:T(8,128)(2,1)}, u32[]{:S(2)}, u32[]{:S(2)}) collective-permute-start(bf16[32,128]{1,0:T(8,128)(2,1)S(1)} %get-tuple-element.41), channel_id=1, source_target_pairs={{0,96},{32,0},{64,32},{96,64},{1,97},{33,1},{65,33},{97,65},{2,98}... | collective-permute-start | bytes 24584 | tf_op jit(solution)/shard_map/ppermute | solution.py:37
  31.3 15.6 %all-to-all-start.1 = ((bf16[32,16,384]{2,1,0:T(8,128)(2,1)}), bf16[32,16,384]{2,1,0:T(8,128)(2,1)S(1)}, u32[]{:S(2)}, u32[]{:S(2)}) async-start(bf16[32,16,384]{2,1,0:T(8,128)(2,1)} %bitcast.34), calls=%async_computation.1 | async-start | bytes 786432 | tf_op jit(solution)/shard_map/all_to_all | solution.py:27
  35.7 0.7 copy-start.24
  52.1 9.6 %copy-start.28 = (s32[1,4,32]{2,1,0:T(4,128)S(1)}, s32[1,4,32]{2,1,0:T(4,128)}, u32[]{:S(2)}) copy-start(s32[1,4,32]{2,1,0:T(4,128)} %param.18) | copy-start | bytes 1540
  52.2 10.2 %copy-start.25 = (s32[832]{0:T(1024)S(1)}, s32[832]{0:T(1024)}, u32[]{:S(2)}) copy-start(s32[832]{0:T(1024)} %param.19) | copy-start | bytes 9988
  52.2 10.8 %copy-start.26 = (s32[832]{0:T(1024)S(1)}, s32[832]{0:T(1024)}, u32[]{:S(2)}) copy-start(s32[832]{0:T(1024)} %param.21) | copy-start | bytes 9988
  52.2 11.4 %copy-start.27 = (s32[32]{0:T(128)S(1)}, s32[32]{0:T(128)}, u32[]{:S(2)}) copy-start(s32[32]{0:T(128)} %param.22) | copy-start | bytes 388
  52.2 50.8 %all-to-all-start.2 = ((bf16[128,16,768]{2,1,0:T(8,128)(2,1)}), bf16[128,16,768]{2,1,0:T(8,128)(2,1)}, u32[]{:S(2)}, u32[]{:S(2)}) async-start(bf16[128,16,768]{2,1,0:T(8,128)(2,1)} %bitcast.31), calls=%async_computation.2 | async-start | bytes 6291456 | tf_op jit(solution)/shard_map/all_to_all | solution.py:27
  64.9 0.7 copy-start.16
  65.6 0.7 copy-start.17
  66.3 0.7 copy-start.19
  66.9 0.8 copy-start.22
  81.0 1.4 copy-start.20
  82.4 1.4 copy-start.21
  83.8 5.8 %copy-start.1 = (bf16[1024,1024]{1,0:T(8,128)(2,1)S(1)}, bf16[1024,1024]{1,0:T(8,128)(2,1)}, u32[]{:S(2)}) copy-start(bf16[1024,1024]{1,0:T(8,128)(2,1)} %self2_ref.1) | copy-start | bytes 6291460
  83.8 5.8 %copy-start.2 = (bf16[1024,1024]{1,0:T(8,128)(2,1)S(1)}, bf16[1024,1024]{1,0:T(8,128)(2,1)}, u32[]{:S(2)}) copy-start(bf16[1024,1024]{1,0:T(8,128)(2,1)} %nbr2_ref.1) | copy-start | bytes 6291460
  83.8 5.8 %copy-start.8 = (bf16[32,1024]{1,0:T(8,128)(2,1)S(1)}, bf16[32,1024]{1,0:T(8,128)(2,1)}, u32[]{:S(2)}) copy-start(bf16[32,1024]{1,0:T(8,128)(2,1)} %cot_ref) | copy-start | bytes 196612
  83.8 5.8 %copy-start.10 = (bf16[32,1024]{1,0:T(8,128)(2,1)S(1)}, bf16[32,1024]{1,0:T(8,128)(2,1)}, u32[]{:S(2)}) copy-start(bf16[32,1024]{1,0:T(8,128)(2,1)} %copy-done.9) | copy-start | bytes 196612
  83.8 5.8 %copy-start.12 = (bf16[32,1024]{1,0:T(8,128)(2,1)S(1)}, bf16[32,1024]{1,0:T(8,128)(2,1)}, u32[]{:S(2)}) copy-start(bf16[32,1024]{1,0:T(8,128)(2,1)} %copy-done.11) | copy-start | bytes 196612
  83.8 5.8 %copy-start.14 = (bf16[32,1024]{1,0:T(8,128)(2,1)S(1)}, bf16[32,1024]{1,0:T(8,128)(2,1)}, u32[]{:S(2)}) copy-start(bf16[32,1024]{1,0:T(8,128)(2,1)} %copy-done.13) | copy-start | bytes 196612
  83.8 5.8 %copy-start.15 = (s32[1,192]{1,0:T(1,128)S(1)}, s32[1,192]{1,0:T(1,128)}, u32[]{:S(2)}) copy-start(s32[1,192]{1,0:T(1,128)} %broadcast_in_dim_tile.3.row_ref) | copy-start | bytes 2308
  89.7 1.6 copy-start.4
  117.2 1.9 %copy-start.6 = (bf16[32,2048]{1,0:T(8,128)(2,1)}, bf16[32,2048]{1,0:T(8,128)(2,1)S(1)}, u32[]{:S(2)}) copy-start(bf16[32,2048]{1,0:T(8,128)(2,1)S(1)} %get-tuple-element.56) | copy-start | bytes 393220
  117.2 8.4 %copy-start.5 = (bf16[128,1024]{1,0:T(8,128)(2,1)S(1)}, bf16[128,1024]{1,0:T(8,128)(2,1)}, u32[]{:S(2)}) copy-start(bf16[128,1024]{1,0:T(8,128)(2,1)} %get-tuple-element.59.cot_ref) | copy-start | bytes 786436
  119.0 8.8 %collective-permute-start.6 = (bf16[512,1536]{1,0:T(8,128)(2,1)S(1)}, bf16[512,1536]{1,0:T(8,128)(2,1)S(1)}, u32[]{:S(2)}, u32[]{:S(2)}) collective-permute-start(bf16[512,1536]{1,0:T(8,128)(2,1)S(1)} %shard_map.189), channel_id=1, source_target_pairs={{0,1},{1,0},{2,3},{3,2},{4,5},{5,4},{6,7},{7,6},{8,9},{9,8},{10,11... | collective-permute-start | bytes 4718600 | tf_op jit(solution)/shard_map/ppermute | solution.py:33
  119.1 5.7 %collective-permute-start.7 = (bf16[32,512]{1,0:T(8,128)(2,1)S(1)}, bf16[32,512]{1,0:T(8,128)(2,1)S(1)}, u32[]{:S(2)}, u32[]{:S(2)}) collective-permute-start(bf16[32,512]{1,0:T(8,128)(2,1)S(1)} %get-tuple-element.61), channel_id=1, source_target_pairs={{0,32},{32,64},{64,96},{96,0},{1,33},{33,65},{65,97},{97,1},{2,34}... | collective-permute-start | bytes 98312 | tf_op jit(solution)/shard_map/ppermute | solution.py:37
  119.3 5.5 %collective-permute-start.8 = (bf16[32,512]{1,0:T(8,128)(2,1)S(1)}, bf16[32,512]{1,0:T(8,128)(2,1)S(1)}, u32[]{:S(2)}, u32[]{:S(2)}) collective-permute-start(bf16[32,512]{1,0:T(8,128)(2,1)S(1)} %get-tuple-element.62), channel_id=1, source_target_pairs={{0,64},{32,96},{64,0},{96,32},{1,65},{33,97},{65,1},{97,33},{2,66}... | collective-permute-start | bytes 98312 | tf_op jit(solution)/shard_map/ppermute | solution.py:37
  121.2 4.3 %collective-permute-start.9 = (bf16[32,512]{1,0:T(8,128)(2,1)S(1)}, bf16[32,512]{1,0:T(8,128)(2,1)S(1)}, u32[]{:S(2)}, u32[]{:S(2)}) collective-permute-start(bf16[32,512]{1,0:T(8,128)(2,1)S(1)} %get-tuple-element.63), channel_id=1, source_target_pairs={{0,96},{32,0},{64,32},{96,64},{1,97},{33,1},{65,33},{97,65},{2,98}... | collective-permute-start | bytes 98312 | tf_op jit(solution)/shard_map/ppermute | solution.py:37
  125.8 2.0 %collective-permute-start.10 = (bf16[512,512]{1,0:T(8,128)(2,1)S(1)}, bf16[512,512]{1,0:T(8,128)(2,1)S(1)}, u32[]{:S(2)}, u32[]{:S(2)}) collective-permute-start(bf16[512,512]{1,0:T(8,128)(2,1)S(1)} %shard_map.190), channel_id=1, source_target_pairs={{0,1},{1,0},{2,3},{3,2},{4,5},{5,4},{6,7},{7,6},{8,9},{9,8},{10,11... | collective-permute-start | bytes 1572872 | tf_op jit(solution)/shard_map/ppermute | solution.py:33
  130.8 36.4 %all-to-all-start.3 = ((bf16[64,8,2048]{2,1,0:T(8,128)(2,1)}), bf16[64,8,2048]{2,1,0:T(8,128)(2,1)}, u32[]{:S(2)}, u32[]{:S(2)}) async-start(bf16[64,8,2048]{2,1,0:T(8,128)(2,1)} %bitcast.32), calls=%async_computation.3 | async-start | bytes 4194304 | tf_op jit(solution)/shard_map/all_to_all | solution.py:27
  137.0 2.9 %copy-start.3 = (bf16[1024,1024]{1,0:T(8,128)(2,1)S(1)}, bf16[1024,1024]{1,0:T(8,128)(2,1)}, u32[]{:S(2)}) copy-start(bf16[1024,1024]{1,0:T(8,128)(2,1)} %nbr2_ref.1) | copy-start | bytes 6291460
  137.0 2.9 %copy-start.7 = (bf16[32,2048]{1,0:T(8,128)(2,1)S(1)}, bf16[32,2048]{1,0:T(8,128)(2,1)}, u32[]{:S(2)}) copy-start(bf16[32,2048]{1,0:T(8,128)(2,1)} %copy-done.6) | copy-start | bytes 393220

commit v4 on v3

--- a/solution.py
+++ b/solution.py
@@ -358,20 +358,23 @@
     give_ref[...] = across(cot_ref[:, : cot_ref.shape[1] // 2], rows).astype(BF)
 
 
-def stay(grad_ref, rows_ref, taken_ref, cot_ref, taken2_ref, *refs, steps):
-    parts, (out_hbm, out_ref, sems) = refs[:-3], refs[-3:]
+def hold(grad_ref, rows_ref, cot_ref, *refs):
+    parts, kept_ref = refs[:-1], refs[-1]
     half = grad_ref.shape[1] // 2
     wide = rows_ref.shape[1]
+    kept_ref[:, :wide] = across(grad_ref[:, half:], rows_ref[...])
     rows = jnp.concatenate([p[...] for p in parts], 0)
-    tile = half // steps
+    kept_ref[:, wide:] = across(cot_ref[:, half:], rows)
+
+
+def stay(kept_ref, taken_ref, taken2_ref, out_hbm, out_ref, sems, *, steps):
+    wide = taken_ref.shape[1]
+    tile = kept_ref.shape[0] // steps
     stores = []
     for t in range(steps):
-        cols = slice(half + t * tile, half + (t + 1) * tile)
         chunk = slice(t * tile, (t + 1) * tile)
-        kept = across(grad_ref[:, cols], rows_ref[...])
-        out_ref[chunk, :wide] = (kept + taken_ref[chunk, :].astype(F32)).astype(BF)
-        kept = across(cot_ref[:, cols], rows)
-        out_ref[chunk, wide:] = (kept + taken2_ref[chunk, :].astype(F32)).astype(BF)
+        out_ref[chunk, :wide] = (kept_ref[chunk, :wide] + taken_ref[chunk, :].astype(F32)).astype(BF)
+        out_ref[chunk, wide:] = (kept_ref[chunk, wide:] + taken2_ref[chunk, :].astype(F32)).astype(BF)
         window = pl.ds(t * tile, tile)
         stores.append(
             pltpu.make_async_copy(out_ref.at[window, :], out_hbm.at[window, :], sems.at[t])
@@ -524,11 +527,16 @@
     )
     taken_two = swap_pair(give, devs)
     tall = 2 * width + 2 * hidden // hosts
+    parts, _ = lax.optimization_barrier((parts, give))
+    kept = call(
+        hold, pltpu.VMEM((hidden // 2, tall), F32),
+        (2 * nodes * hidden * width, 4 * hidden * width), grad, rows_one, turned, *parts,
+        near=(0, 1), limit=24,
+    )
     part = call(
-        functools.partial(stay, steps=2), Left((hidden // 2, tall), BF),
-        (2 * nodes * hidden * width, 4 * hidden * width), grad, rows_one, taken, turned, taken_two,
-        *parts, near=(0, 1), limit=24,
-        scratch=[pltpu.VMEM((hidden // 2, tall), BF), pltpu.SemaphoreType.DMA((2,))],
+        functools.partial(stay, steps=4), Left((hidden // 2, tall), BF),
+        (hidden * tall, 4 * hidden * tall), kept, taken, taken_two, near=(0,), limit=24,
+        scratch=[pltpu.VMEM((hidden // 2, tall), BF), pltpu.SemaphoreType.DMA((4,))],
     )
     part = exchange(part.reshape(count // 2, cols, tall), ALL, parity_groups(hosts, devs))
 

time: 171 us -> 170 us (level)
    ppermute x2, waiting for transfers between devices: 1.9 us -> 0.01 us  [swap_pair(): return lax.ppermute(x, 'dev', [(i, i ^ 1) for i in range(devs)])]
    pallas_call x12 -> x13, Pallas kernels: 56.1 us -> 56.6 us  [call(): pl.pallas_call(body, out_shape=outs, in_specs=kinds, out_specs=jax.tree.u...]
  transfers between devices with their start and end apart: 15 -> 15, of which waited for: 7 -> 6; matrix products, arithmetic and copies ran while one was open for 10% -> 10% of each run, Pallas kernels for 15% -> 16%
where the time goes in v4:
time: 170 us; the launch traced here: 169 us
  Pallas kernels  56.6 us (33%)
  starting transfers between devices  44.8 us (26%)
  waiting for transfers between devices  40 us (24%)
  local copies, waits for them, and re-layouts  22.8 us (13%)
  matrix products  3.23 us (2%)
    pallas_call x13, Pallas kernels, call(): pl.pallas_call(body, out_shape=outs, in_specs=kinds, out_specs=jax.tree.u...  56.6 us
    all_to_all x4, waiting for transfers between devices, exchange(): lax.all_to_all(x, axes, split_axis=0, concat_axis=0, tiled=True, axis_ind...  35.1 us
    all_to_all x4, starting transfers between devices, exchange(): lax.all_to_all(x, axes, split_axis=0, concat_axis=0, tiled=True, axis_ind...  27.6 us
    ppermute x9, starting transfers between devices, along_z(): return lax.ppermute(x, 'hst', [(i, (i + k) % hosts) for i in range(hosts)])  17 us
    unnamed x58, local copies, waits for them, and re-layouts  9.46 us
    gather x1, local copies, waits for them, and re-layouts, step(): stored = features.at[kept.reshape(slots)].get(mode='promise_in_bounds')  9.43 us
    ppermute x9, waiting for transfers between devices, along_z(): return lax.ppermute(x, 'hst', [(i, (i + k) % hosts) for i in range(hosts)])  4.92 us
  transfers between devices with their start and end apart: 15, of which 6 were waited for; matrix products, arithmetic and copies ran while one was open for 10% of the time, Pallas kernels for 16%

profile of v4, /device:TPU:0, one launch (start us, length us, event | category | flops | bytes accessed | tf_op | source)
XLA Modules:
  0.0 168.7 jit_solution(6445616799847815751)
XLA Ops:
  0.6 0.0 copy-start
  0.7 0.8 copy-done.18
  1.5 2.4 %shard_map.181 = bf16[32,8,896]{2,1,0:T(8,128)(2,1)} custom-call(s32[2]{0:T(128)S(1)} %bitcast.29, s32[4,16,32]{2,1,0:T(8,128)} %bitcast.36, bf16[256,768]{1,0:T(8,128)(2,1)} %bitcast.33), custom_call_target="tpu_custom_call" | custom-call | flops 3670016 | bytes 917504 | tf_op jit(solution)/shard_map/pallas_call | solution.py:63
  3.9 7.6 %all-to-all-start = ((bf16[32,8,896]{2,1,0:T(8,128)(2,1)}), bf16[32,8,896]{2,1,0:T(8,128)(2,1)}, u32[]{:S(2)}, u32[]{:S(2)}) async-start(bf16[32,8,896]{2,1,0:T(8,128)(2,1)} %shard_map.181), calls=%async_computation | async-start | bytes 917504 | tf_op jit(solution)/shard_map/all_to_all | solution.py:27
  11.5 4.0 %collective-permute-start.1 = (bf16[32,1024]{1,0:T(8,128)(2,1)}, bf16[32,1024]{1,0:T(8,128)(2,1)S(1)}, u32[]{:S(2)}, u32[]{:S(2)}) collective-permute-start(bf16[32,1024]{1,0:T(8,128)(2,1)} %cot_ref), channel_id=1, source_target_pairs={{0,64},{32,96},{64,0},{96,32},{1,65},{33,97},{65,1},{97,33},{2,66}... | collective-permute-start | bytes 196616 | tf_op jit(solution)/shard_map/ppermute | solution.py:37
  15.4 1.0 collective-permute-start
  16.4 2.2 %collective-permute-start.2 = (bf16[32,1024]{1,0:T(8,128)(2,1)}, bf16[32,1024]{1,0:T(8,128)(2,1)S(1)}, u32[]{:S(2)}, u32[]{:S(2)}) collective-permute-start(bf16[32,1024]{1,0:T(8,128)(2,1)} %cot_ref), channel_id=1, source_target_pairs={{0,96},{32,0},{64,32},{96,64},{1,97},{33,1},{65,33},{97,65},{2,98}... | collective-permute-start | bytes 196616 | tf_op jit(solution)/shard_map/ppermute | solution.py:37
  18.7 0.6 copy-done.9
  19.3 1.8 %collective-permute-done.refs_0_ = bf16[32,1024]{1,0:T(8,128)(2,1)S(1)} collective-permute-done((bf16[32,1024]{1,0:T(8,128)(2,1)}, bf16[32,1024]{1,0:T(8,128)(2,1)S(1)}, u32[]{:S(2)}, u32[]{:S(2)}) %collective-permute-start) | collective-permute-done | bytes 65568 | tf_op jit(solution)/shard_map/ppermute | solution.py:37
  21.1 1.2 all-to-all-done.got_ref
  22.3 2.5 %shard_map.182 = (bf16[512,384]{1,0:T(8,128)(2,1)}, bf16[32,128]{1,0:T(8,128)(2,1)S(1)}, bf16[32,128]{1,0:T(8,128)(2,1)}, bf16[32,128]{1,0:T(8,128)(2,1)}, bf16[32,128]{1,0:T(8,128)(2,1)S(1)}) custom-call(s32[1]{0:T(128)} %bitcast.host_ref, bf16[32,8,896]{2,1,0:T(8,128)(2,1)} %all-to-all-done.got_ref), custom_call_target="tpu_custom_call" | custom-call | flops 201326592 | bytes 98304 | tf_op jit(solution)/shard_map/pallas_call | solution.py:63
  24.8 1.9 %collective-permute-start.3 = (bf16[32,128]{1,0:T(8,128)(2,1)}, bf16[32,128]{1,0:T(8,128)(2,1)S(1)}, u32[]{:S(2)}, u32[]{:S(2)}) collective-permute-start(bf16[32,128]{1,0:T(8,128)(2,1)} %get-tuple-element.43), channel_id=1, source_target_pairs={{0,32},{32,64},{64,96},{96,0},{1,33},{33,65},{65,97},{97,1},{2,34}... | collective-permute-start | bytes 24584 | tf_op jit(solution)/shard_map/ppermute | solution.py:37
  26.7 3.6 %collective-permute-start.4 = (bf16[32,128]{1,0:T(8,128)(2,1)}, bf16[32,128]{1,0:T(8,128)(2,1)}, u32[]{:S(2)}, u32[]{:S(2)}) collective-permute-start(bf16[32,128]{1,0:T(8,128)(2,1)} %get-tuple-element.44), channel_id=1, source_target_pairs={{0,64},{32,96},{64,0},{96,32},{1,65},{33,97},{65,1},{97,33},{2,66}... | collective-permute-start | bytes 24584 | tf_op jit(solution)/shard_map/ppermute | solution.py:37
  30.3 1.0 collective-permute-start.5
  31.3 4.3 %all-to-all-start.1 = ((bf16[32,16,384]{2,1,0:T(8,128)(2,1)}), bf16[32,16,384]{2,1,0:T(8,128)(2,1)S(1)}, u32[]{:S(2)}, u32[]{:S(2)}) async-start(bf16[32,16,384]{2,1,0:T(8,128)(2,1)} %bitcast.34), calls=%async_computation.1 | async-start | bytes 786432 | tf_op jit(solution)/shard_map/all_to_all | solution.py:27
  35.7 0.0 copy-start.24
  35.7 0.7 copy-done.24
  36.4 1.1 shard_map.183
  37.5 9.4 %gather_fusion = bf16[2048,768]{1,0:T(8,128)(2,1)} fusion(bf16[2048,768]{1,0:T(8,128)(2,1)S(1)} %copy-done, s32[2048]{0:T(1024)S(1)} %broadcast_clamp_fusion), kind=kCustom, calls=%fused_computation | custom fusion | bytes 6299648 | tf_op jit(solution)/shard_map/gather | solution.py:470
  46.9 5.2 %shard_map.184 = bf16[2048,768]{1,0:T(8,128)(2,1)} custom-call(s32[1,2048]{1,0:T(1,128)S(1)} %get-tuple-element.46.asked_ref, bf16[512,384]{1,0:T(8,128)(2,1)S(1)} %bitcast.27, bf16[2048,768]{1,0:T(8,128)(2,1)} %gather_fusion), custom_call_target="tpu_custom_call" | custom-call | flops 1610612736 | bytes 6291456 | tf_op jit(solution)/shard_map/pallas_call | solution.py:63
  52.1 0.0 copy-start.28
  52.2 0.0 copy-start.25
  52.2 0.0 copy-start.26
  52.2 0.0 copy-start.27
  52.2 9.6 %all-to-all-start.2 = ((bf16[128,16,768]{2,1,0:T(8,128)(2,1)}), bf16[128,16,768]{2,1,0:T(8,128)(2,1)}, u32[]{:S(2)}, u32[]{:S(2)}) async-start(bf16[128,16,768]{2,1,0:T(8,128)(2,1)} %bitcast.31), calls=%async_computation.2 | async-start | bytes 6291456 | tf_op jit(solution)/shard_map/all_to_all | solution.py:27
  61.8 0.6 reshape.74.count_ref
  62.4 0.6 broadcast_in_dim.20.self_ref
  63.0 0.6 broadcast_in_dim.21.hop_ref
  63.5 0.6 broadcast_in_dim_tile.3.row_ref
  64.2 0.7 copy.23.col_ref
  64.9 0.7 copy-done.16
  65.6 0.7 copy-done.17
  66.3 0.7 copy-done.19
  67.0 0.8 copy-done.22
  67.8 13.2 %shard_map.185 = (bf16[832,2048]{1,0:T(8,128)(2,1)}, bf16[832,2048]{1,0:T(8,128)(2,1)}, f32[832,128]{1,0:T(8,128)}) custom-call(s32[15,832]{1,0:T(8,128)S(1)} %bitcast.30, s32[1,832]{1,0:T(1,128)S(1)} %copy-done.16, s32[1,832]{1,0:T(1,128)S(1)} %copy-done.17, s32[1,128]{1,0:T(1,128)S(1)} %copy-done.19), custom_call_target="tpu_custom_call" | custom-call | flops 81788928 | bytes 6815744 | tf_op jit(solution)/shard_map/pallas_call | solution.py:63
  81.0 1.4 copy-done.20
  82.4 1.4 copy-done.21
  83.8 0.0 copy-start.12
  83.8 0.0 copy-start.15
  83.8 5.8 %shard_map.186 = (bf16[1024,1024]{1,0:T(8,128)(2,1)}, bf16[1024,1024]{1,0:T(8,128)(2,1)}, bf16[1536,1024]{1,0:T(8,128)(2,1)}) custom-call(s32[1]{0:T(128)} %bitcast.12.core_ref, bf16[768,1024]{1,0:T(8,128)(2,1)S(1)} %copy-done.20, bf16[768,1024]{1,0:T(8,128)(2,1)S(1)} %copy-done.21), custom_call_target="tpu_custom_call" | custom-call | flops 3221225472 | bytes 12582912 | tf_op jit(solution)/shard_map/pallas_call | solution.py:63
  89.7 1.6 copy-done.4
  91.3 4.4 %shard_map.187 = (f32[832,1024]{1,0:T(8,128)}, bf16[128,1024]{1,0:T(8,128)(2,1)}) custom-call(bf16[1024,1024]{1,0:T(8,128)(2,1)S(1)} %copy-done.4, bf16[1024,1024]{1,0:T(8,128)(2,1)S(1)} %copy-done.1, bf16[1024,1024]{1,0:T(8,128)(2,1)S(1)} %copy-done.2, s32[32,1]{1,0:T(8,128)S(1)} %copy.23.col_ref, s32[1,192]{1,0:T(1,128)S(1)} %copy-done.15, ...), custom_call_target="tpu_custom_call" | custom-call | flops 268435456 | bytes 12582912 | tf_op jit(solution)/shard_map/pallas_call | solution.py:63
  95.7 7.3 %all-to-all-done.2 = bf16[128,16,768]{2,1,0:T(8,128)(2,1)} async-done(((bf16[128,16,768]{2,1,0:T(8,128)(2,1)}), bf16[128,16,768]{2,1,0:T(8,128)(2,1)}, u32[]{:S(2)}, u32[]{:S(2)}) %all-to-all-start.2) | async-done | bytes 3145760 | tf_op jit(solution)/shard_map/all_to_all | solution.py:27
  103.0 14.2 %shard_map.188 = (bf16[832,1536]{1,0:T(8,128)(2,1)S(1)}, bf16[832,1024]{1,0:T(8,128)(2,1)S(1)}, bf16[32,2048]{1,0:T(8,128)(2,1)S(1)}, bf16[32,512]{1,0:T(8,128)(...) custom-call(s32[1]{0:T(128)} %bitcast.host_ref, ...), custom_call_target="tpu_custom_call" | custom-call | flops 5234491392 | bytes 13631488 | tf_op jit(solution)/shard_map/pallas_call | solution.py:63
  117.2 0.0 copy-start.5
  117.2 1.8 %shard_map.191 = bf16[512,1536]{1,0:T(8,128)(2,1)S(1)} custom-call(bf16[832,1024]{1,0:T(8,128)(2,1)S(1)} %get-tuple-element.61.grad_ref, bf16[832,1536]{1,0:T(8,128)(2,1)S(1)} %get-tuple-element.62.rows_ref), custom_call_target="tpu_custom_call" | custom-call | flops 1308622848 | bytes 3145728 | tf_op jit(solution)/shard_map/pallas_call | solution.py:63
  119.0 0.1 collective-permute-start.9
  119.1 0.2 collective-permute-start.6
  119.3 1.9 %collective-permute-start.7 = (bf16[32,512]{1,0:T(8,128)(2,1)S(1)}, bf16[32,512]{1,0:T(8,128)(2,1)S(1)}, u32[]{:S(2)}, u32[]{:S(2)}) collective-permute-start(bf16[32,512]{1,0:T(8,128)(2,1)S(1)} %get-tuple-element.66), channel_id=1, source_target_pairs={{0,64},{32,96},{64,0},{96,32},{1,65},{33,97},{65,1},{97,33},{2,66}... | collective-permute-start | bytes 98312 | tf_op jit(solution)/shard_map/ppermute | solution.py:37
  121.2 1.2 collective-permute-start.8
  122.4 2.4 %collective-permute-done.6.refs_1_ = bf16[32,512]{1,0:T(8,128)(2,1)S(1)} collective-permute-done((bf16[32,512]{1,0:T(8,128)(2,1)S(1)}, bf16[32,512]{1,0:T(8,128)(2,1)S(1)}, u32[]{:S(2)}, u32[]{:S(2)}) %collective-permute-start.6) | collective-permute-done | bytes 32800 | tf_op jit(solution)/shard_map/ppermute | solution.py:37
  124.8 0.7 collective-permute-done.8.refs_3_
  125.5 0.3 shard_map.189
  125.8 0.1 collective-permute-start.10
  125.9 2.0 %shard_map.190.kept_ref = f32[512,2048]{1,0:T(8,128)S(1)} custom-call(bf16[832,1024]{1,0:T(8,128)(2,1)S(1)} %get-tuple-element.61.grad_ref, bf16[832,1536]{1,0:T(8,128)(2,1)S(1)} %get-tuple-element.62.rows_ref, bf16[128,1024]{1,0:T(8,128)(2,1)S(1)} %copy-done.5, bf16[32,512]{1,0:T(8,128)(2,1)S(1)} %get-tuple-element.68.refs_0_, ...), custom_call_target="tpu_custom_call" | custom-call | flops 1308622848 | bytes 3145728 | tf_op jit(solution)/shard_map/pallas_call | solution.py:63
  127.9 1.5 shard_map.192
  129.4 6.2 %all-to-all-start.3 = ((bf16[64,8,2048]{2,1,0:T(8,128)(2,1)}), bf16[64,8,2048]{2,1,0:T(8,128)(2,1)}, u32[]{:S(2)}, u32[]{:S(2)}) async-start(bf16[64,8,2048]{2,1,0:T(8,128)(2,1)} %bitcast.32), calls=%async_computation.3 | async-start | bytes 4194304 | tf_op jit(solution)/shard_map/all_to_all | solution.py:27
  135.6 0.0 copy-start.3
  135.6 0.8 copy.25
  136.4 2.1 %fusion.2 = f32[32,1024]{1,0:T(8,128)S(1)} fusion(bf16[1024,1024]{1,0:T(8,128)(2,1)} %self2_ref.1, bf16[32,2048]{1,0:T(8,128)(2,1)} %copy-done.6), kind=kOutput, calls=%fused_computation.4 | convolution fusion | flops 67108864 | bytes 2293760 | tf_op jit(solution)/shard_map/dot_general | solution.py:75
  138.5 0.0 copy-done.3
  138.6 1.1 fusion
  139.7 26.6 %all-to-all-done.3.part_hbm = bf16[64,8,2048]{2,1,0:T(8,128)(2,1)} async-done(((bf16[64,8,2048]{2,1,0:T(8,128)(2,1)}), bf16[64,8,2048]{2,1,0:T(8,128)(2,1)}, u32[]{:S(2)}, u32[]{:S(2)}) %all-to-all-start.3) | async-done | bytes 2097184 | tf_op jit(solution)/shard_map/all_to_all | solution.py:27
  166.2 2.2 %shard_map.193 = (f32[8,768]{1,0:T(8,128)}, f32[8,768]{1,0:T(8,128)}, f32[8,1024]{1,0:T(8,128)}, f32[8,1024]{1,0:T(8,128)}) custom-call(bf16[64,8,2048]{2,1,0:T(8,128)(2,1)} %all-to-all-done.3.part_hbm), custom_call_target="tpu_custom_call" | custom-call | flops 2097152 | bytes 2097152 | tf_op jit(solution)/shard_map/pallas_call | solution.py:63
  (49 shorter events, 0.1 us)
Async XLA Ops:
  0.6 36.9 %copy-start = (bf16[2048,768]{1,0:T(8,128)(2,1)S(1)}, bf16[2048,768]{1,0:T(8,128)(2,1)}, u32[]{:S(2)}) copy-start(bf16[2048,768]{1,0:T(8,128)(2,1)} %param.14) | copy-start | bytes 9437188
  0.6 0.8 copy-start.18
  3.9 18.4 %all-to-all-start = ((bf16[32,8,896]{2,1,0:T(8,128)(2,1)}), bf16[32,8,896]{2,1,0:T(8,128)(2,1)}, u32[]{:S(2)}, u32[]{:S(2)}) async-start(bf16[32,8,896]{2,1,0:T(8,128)(2,1)} %shard_map.181), calls=%async_computation | async-start | bytes 917504 | tf_op jit(solution)/shard_map/all_to_all | solution.py:27
  11.5 7.2 %collective-permute-start.1 = (bf16[32,1024]{1,0:T(8,128)(2,1)}, bf16[32,1024]{1,0:T(8,128)(2,1)S(1)}, u32[]{:S(2)}, u32[]{:S(2)}) collective-permute-start(bf16[32,1024]{1,0:T(8,128)(2,1)} %cot_ref), channel_id=1, source_target_pairs={{0,64},{32,96},{64,0},{96,32},{1,65},{33,97},{65,1},{97,33},{2,66}... | collective-permute-start | bytes 196616 | tf_op jit(solution)/shard_map/ppermute | solution.py:37
  15.4 5.7 %collective-permute-start = (bf16[32,1024]{1,0:T(8,128)(2,1)}, bf16[32,1024]{1,0:T(8,128)(2,1)S(1)}, u32[]{:S(2)}, u32[]{:S(2)}) collective-permute-start(bf16[32,1024]{1,0:T(8,128)(2,1)} %cot_ref), channel_id=1, source_target_pairs={{0,32},{32,64},{64,96},{96,0},{1,33},{33,65},{65,97},{97,1},{2,34}... | collective-permute-start | bytes 196616 | tf_op jit(solution)/shard_map/ppermute | solution.py:37
  16.4 4.7 %collective-permute-start.2 = (bf16[32,1024]{1,0:T(8,128)(2,1)}, bf16[32,1024]{1,0:T(8,128)(2,1)S(1)}, u32[]{:S(2)}, u32[]{:S(2)}) collective-permute-start(bf16[32,1024]{1,0:T(8,128)(2,1)} %cot_ref), channel_id=1, source_target_pairs={{0,96},{32,0},{64,32},{96,64},{1,97},{33,1},{65,33},{97,65},{2,98}... | collective-permute-start | bytes 196616 | tf_op jit(solution)/shard_map/ppermute | solution.py:37
  18.7 0.6 copy-start.9
  21.1 10.2 %copy-start.11 = (bf16[32,1024]{1,0:T(8,128)(2,1)}, bf16[32,1024]{1,0:T(8,128)(2,1)S(1)}, u32[]{:S(2)}) copy-start(bf16[32,1024]{1,0:T(8,128)(2,1)S(1)} %collective-permute-done.refs_0_) | copy-start | bytes 196612
  21.1 10.2 %copy-start.13 = (bf16[32,1024]{1,0:T(8,128)(2,1)}, bf16[32,1024]{1,0:T(8,128)(2,1)S(1)}, u32[]{:S(2)}) copy-start(bf16[32,1024]{1,0:T(8,128)(2,1)S(1)} %collective-permute-done.2.refs_2_) | copy-start | bytes 196612
  24.8 6.5 %copy-start.23 = (bf16[32,128]{1,0:T(8,128)(2,1)}, bf16[32,128]{1,0:T(8,128)(2,1)S(1)}, u32[]{:S(2)}) copy-start(bf16[32,128]{1,0:T(8,128)(2,1)S(1)} %get-tuple-element.42.refs_0_) | copy-start | bytes 24580
  24.8 10.9 %collective-permute-start.3 = (bf16[32,128]{1,0:T(8,128)(2,1)}, bf16[32,128]{1,0:T(8,128)(2,1)S(1)}, u32[]{:S(2)}, u32[]{:S(2)}) collective-permute-start(bf16[32,128]{1,0:T(8,128)(2,1)} %get-tuple-element.43), channel_id=1, source_target_pairs={{0,32},{32,64},{64,96},{96,0},{1,33},{33,65},{65,97},{97,1},{2,34}... | collective-permute-start | bytes 24584 | tf_op jit(solution)/shard_map/ppermute | solution.py:37
  26.7 8.9 %collective-permute-start.4 = (bf16[32,128]{1,0:T(8,128)(2,1)}, bf16[32,128]{1,0:T(8,128)(2,1)}, u32[]{:S(2)}, u32[]{:S(2)}) collective-permute-start(bf16[32,128]{1,0:T(8,128)(2,1)} %get-tuple-element.44), channel_id=1, source_target_pairs={{0,64},{32,96},{64,0},{96,32},{1,65},{33,97},{65,1},{97,33},{2,66}... | collective-permute-start | bytes 24584 | tf_op jit(solution)/shard_map/ppermute | solution.py:37
  30.3 5.4 %collective-permute-start.5 = (bf16[32,128]{1,0:T(8,128)(2,1)S(1)}, bf16[32,128]{1,0:T(8,128)(2,1)}, u32[]{:S(2)}, u32[]{:S(2)}) collective-permute-start(bf16[32,128]{1,0:T(8,128)(2,1)S(1)} %get-tuple-element.45), channel_id=1, source_target_pairs={{0,96},{32,0},{64,32},{96,64},{1,97},{33,1},{65,33},{97,65},{2,98}... | collective-permute-start | bytes 24584 | tf_op jit(solution)/shard_map/ppermute | solution.py:37
  31.3 15.6 %all-to-all-start.1 = ((bf16[32,16,384]{2,1,0:T(8,128)(2,1)}), bf16[32,16,384]{2,1,0:T(8,128)(2,1)S(1)}, u32[]{:S(2)}, u32[]{:S(2)}) async-start(bf16[32,16,384]{2,1,0:T(8,128)(2,1)} %bitcast.34), calls=%async_computation.1 | async-start | bytes 786432 | tf_op jit(solution)/shard_map/all_to_all | solution.py:27
  35.7 0.7 copy-start.24
  52.1 9.6 %copy-start.28 = (s32[1,4,32]{2,1,0:T(4,128)S(1)}, s32[1,4,32]{2,1,0:T(4,128)}, u32[]{:S(2)}) copy-start(s32[1,4,32]{2,1,0:T(4,128)} %param.18) | copy-start | bytes 1540
  52.2 10.2 %copy-start.25 = (s32[832]{0:T(1024)S(1)}, s32[832]{0:T(1024)}, u32[]{:S(2)}) copy-start(s32[832]{0:T(1024)} %param.19) | copy-start | bytes 9988
  52.2 10.8 %copy-start.26 = (s32[832]{0:T(1024)S(1)}, s32[832]{0:T(1024)}, u32[]{:S(2)}) copy-start(s32[832]{0:T(1024)} %param.21) | copy-start | bytes 9988
  52.2 11.4 %copy-start.27 = (s32[32]{0:T(128)S(1)}, s32[32]{0:T(128)}, u32[]{:S(2)}) copy-start(s32[32]{0:T(128)} %param.22) | copy-start | bytes 388
  52.2 50.8 %all-to-all-start.2 = ((bf16[128,16,768]{2,1,0:T(8,128)(2,1)}), bf16[128,16,768]{2,1,0:T(8,128)(2,1)}, u32[]{:S(2)}, u32[]{:S(2)}) async-start(bf16[128,16,768]{2,1,0:T(8,128)(2,1)} %bitcast.31), calls=%async_computation.2 | async-start | bytes 6291456 | tf_op jit(solution)/shard_map/all_to_all | solution.py:27
  64.9 0.7 copy-start.16
  65.6 0.7 copy-start.17
  66.3 0.7 copy-start.19
  66.9 0.8 copy-start.22
  81.0 1.4 copy-start.20
  82.4 1.4 copy-start.21
  83.8 5.8 %copy-start.1 = (bf16[1024,1024]{1,0:T(8,128)(2,1)S(1)}, bf16[1024,1024]{1,0:T(8,128)(2,1)}, u32[]{:S(2)}) copy-start(bf16[1024,1024]{1,0:T(8,128)(2,1)} %self2_ref.1) | copy-start | bytes 6291460
  83.8 5.8 %copy-start.2 = (bf16[1024,1024]{1,0:T(8,128)(2,1)S(1)}, bf16[1024,1024]{1,0:T(8,128)(2,1)}, u32[]{:S(2)}) copy-start(bf16[1024,1024]{1,0:T(8,128)(2,1)} %nbr2_ref.1) | copy-start | bytes 6291460
  83.8 5.8 %copy-start.8 = (bf16[32,1024]{1,0:T(8,128)(2,1)S(1)}, bf16[32,1024]{1,0:T(8,128)(2,1)}, u32[]{:S(2)}) copy-start(bf16[32,1024]{1,0:T(8,128)(2,1)} %cot_ref) | copy-start | bytes 196612
  83.8 5.8 %copy-start.10 = (bf16[32,1024]{1,0:T(8,128)(2,1)S(1)}, bf16[32,1024]{1,0:T(8,128)(2,1)}, u32[]{:S(2)}) copy-start(bf16[32,1024]{1,0:T(8,128)(2,1)} %copy-done.9) | copy-start | bytes 196612
  83.8 5.8 %copy-start.12 = (bf16[32,1024]{1,0:T(8,128)(2,1)S(1)}, bf16[32,1024]{1,0:T(8,128)(2,1)}, u32[]{:S(2)}) copy-start(bf16[32,1024]{1,0:T(8,128)(2,1)} %copy-done.11) | copy-start | bytes 196612
  83.8 5.8 %copy-start.14 = (bf16[32,1024]{1,0:T(8,128)(2,1)S(1)}, bf16[32,1024]{1,0:T(8,128)(2,1)}, u32[]{:S(2)}) copy-start(bf16[32,1024]{1,0:T(8,128)(2,1)} %copy-done.13) | copy-start | bytes 196612
  83.8 5.8 %copy-start.15 = (s32[1,192]{1,0:T(1,128)S(1)}, s32[1,192]{1,0:T(1,128)}, u32[]{:S(2)}) copy-start(s32[1,192]{1,0:T(1,128)} %broadcast_in_dim_tile.3.row_ref) | copy-start | bytes 2308
  89.7 1.6 copy-start.4
  117.2 1.9 %copy-start.6 = (bf16[32,2048]{1,0:T(8,128)(2,1)}, bf16[32,2048]{1,0:T(8,128)(2,1)S(1)}, u32[]{:S(2)}) copy-start(bf16[32,2048]{1,0:T(8,128)(2,1)S(1)} %get-tuple-element.60) | copy-start | bytes 393220
  117.2 8.4 %copy-start.5 = (bf16[128,1024]{1,0:T(8,128)(2,1)S(1)}, bf16[128,1024]{1,0:T(8,128)(2,1)}, u32[]{:S(2)}) copy-start(bf16[128,1024]{1,0:T(8,128)(2,1)} %get-tuple-element.63.cot_ref) | copy-start | bytes 786436
  119.0 8.9 %collective-permute-start.9 = (bf16[512,1536]{1,0:T(8,128)(2,1)S(1)}, bf16[512,1536]{1,0:T(8,128)(2,1)S(1)}, u32[]{:S(2)}, u32[]{:S(2)}) collective-permute-start(bf16[512,1536]{1,0:T(8,128)(2,1)S(1)} %shard_map.191), channel_id=1, source_target_pairs={{0,1},{1,0},{2,3},{3,2},{4,5},{5,4},{6,7},{7,6},{8,9},{9,8},{10,11... | collective-permute-start | bytes 4718600 | tf_op jit(solution)/shard_map/ppermute | solution.py:33
  119.1 5.7 %collective-permute-start.6 = (bf16[32,512]{1,0:T(8,128)(2,1)S(1)}, bf16[32,512]{1,0:T(8,128)(2,1)S(1)}, u32[]{:S(2)}, u32[]{:S(2)}) collective-permute-start(bf16[32,512]{1,0:T(8,128)(2,1)S(1)} %get-tuple-element.65), channel_id=1, source_target_pairs={{0,32},{32,64},{64,96},{96,0},{1,33},{33,65},{65,97},{97,1},{2,34}... | collective-permute-start | bytes 98312 | tf_op jit(solution)/shard_map/ppermute | solution.py:37
  119.3 5.5 %collective-permute-start.7 = (bf16[32,512]{1,0:T(8,128)(2,1)S(1)}, bf16[32,512]{1,0:T(8,128)(2,1)S(1)}, u32[]{:S(2)}, u32[]{:S(2)}) collective-permute-start(bf16[32,512]{1,0:T(8,128)(2,1)S(1)} %get-tuple-element.66), channel_id=1, source_target_pairs={{0,64},{32,96},{64,0},{96,32},{1,65},{33,97},{65,1},{97,33},{2,66}... | collective-permute-start | bytes 98312 | tf_op jit(solution)/shard_map/ppermute | solution.py:37
  121.2 4.3 %collective-permute-start.8 = (bf16[32,512]{1,0:T(8,128)(2,1)S(1)}, bf16[32,512]{1,0:T(8,128)(2,1)S(1)}, u32[]{:S(2)}, u32[]{:S(2)}) collective-permute-start(bf16[32,512]{1,0:T(8,128)(2,1)S(1)} %get-tuple-element.67), channel_id=1, source_target_pairs={{0,96},{32,0},{64,32},{96,64},{1,97},{33,1},{65,33},{97,65},{2,98}... | collective-permute-start | bytes 98312 | tf_op jit(solution)/shard_map/ppermute | solution.py:37
  125.8 2.1 %collective-permute-start.10 = (bf16[512,512]{1,0:T(8,128)(2,1)S(1)}, bf16[512,512]{1,0:T(8,128)(2,1)S(1)}, u32[]{:S(2)}, u32[]{:S(2)}) collective-permute-start(bf16[512,512]{1,0:T(8,128)(2,1)S(1)} %shard_map.189), channel_id=1, source_target_pairs={{0,1},{1,0},{2,3},{3,2},{4,5},{5,4},{6,7},{7,6},{8,9},{9,8},{10,11... | collective-permute-start | bytes 1572872 | tf_op jit(solution)/shard_map/ppermute | solution.py:33
  129.4 36.8 %all-to-all-start.3 = ((bf16[64,8,2048]{2,1,0:T(8,128)(2,1)}), bf16[64,8,2048]{2,1,0:T(8,128)(2,1)}, u32[]{:S(2)}, u32[]{:S(2)}) async-start(bf16[64,8,2048]{2,1,0:T(8,128)(2,1)} %bitcast.32), calls=%async_computation.3 | async-start | bytes 4194304 | tf_op jit(solution)/shard_map/all_to_all | solution.py:27
  135.6 2.9 %copy-start.3 = (bf16[1024,1024]{1,0:T(8,128)(2,1)S(1)}, bf16[1024,1024]{1,0:T(8,128)(2,1)}, u32[]{:S(2)}) copy-start(bf16[1024,1024]{1,0:T(8,128)(2,1)} %nbr2_ref.1) | copy-start | bytes 6291460
  135.6 2.9 %copy-start.7 = (bf16[32,2048]{1,0:T(8,128)(2,1)S(1)}, bf16[32,2048]{1,0:T(8,128)(2,1)}, u32[]{:S(2)}) copy-start(bf16[32,2048]{1,0:T(8,128)(2,1)} %copy-done.6) | copy-start | bytes 393220
